TPU v7x, 32 devices: a whole 2x2x4 slice. The times are simulated.
32 devices in a mesh: win: 2 (over x), lat: 4 (over y, core), lon: 4 (over z).
Axes of the slice: x: 2, y: 2, z: 4, core: 2. Of those that a mesh axis runs over, the one named last changes fastest.
Arguments:
- increment: float32 [2, 3, 256, 1024], P('win', None, 'lat', 'lon'), may hold values from -6 to 6
- model_weight: float32 [2, 3, 256, 1024], P('win', None, 'lat', 'lon'), may hold values from 0.25 to 4
- winds: float32 [2, 2, 256, 1024], P('win', None, 'lat', 'lon'), may hold values from -0.3 to 0.3
- reaction: float32 [2, 3, 3], P('win'), may hold values from -1 to 1
- obs_cells: int32 [2, 4, 4, 1024], P('win', 'lat', 'lon'), may hold values from 0 to 16383
- obs_weight: float32 [2, 3, 4, 4, 1024], P('win', None, 'lat', 'lon'), may hold values from 0.5 to 8
Outputs:
- hess_vec: float32 [2, 3, 256, 1024], P('win', None, 'lat', 'lon')
Inputs may be any that keep to these rules, and one draw needn't show every extreme that they name: `obs_cells`: an index row * 256 + column within its tile.
All inputs are finite; a program needn't handle non-finite values.
Results may differ from a plain program's by a relative error of at most 0.00002.
Values sent between devices are 32-bit elements; how exact they have to be, the bound alone decides.
No kernel may reach another device: no remote copies, remote signals or barrier semaphores. Data moves between devices by JAX's collectives and lax.ppermute only.
A program may use at most 64 MiB of HBM per device.

v0:
```python
import jax
import jax.numpy as jnp
from jax import lax
from jax.sharding import PartitionSpec as P

DIFFUSION = 0.15


def from_behind(value, axis, steps):
    count = lax.axis_size(axis)
    first, last = (max(0, -steps), min(count, count - steps))
    return lax.ppermute(value, axis, [(source, source + steps) for source in range(first, last)])


def extended_2(block, sides, width):
    for axis, dim in sides:
        count = lax.axis_size(axis)
        forward = [(i, i + 1) for i in range(count - 1)]
        forward.append((count - 1, 0))
        backward = [(target, source) for source, target in forward]
        low = lax.ppermute(
            lax.slice_in_dim(block, block.shape[dim] - width, None, axis=dim), axis, forward
        )
        high = lax.ppermute(lax.slice_in_dim(block, 0, width, axis=dim), axis, backward)
        block = jnp.concatenate([low, block, high], axis=dim)
    return block


def send_ahead(field):
    return from_behind(field, "win", 1)


def send_behind(field):
    return from_behind(field, "win", -1)


def sides(extended):
    center = extended[:, 1:-1, 1:-1]
    north_side = extended[:, 2:, 1:-1]
    south_side = extended[:, :-2, 1:-1]
    east_side = extended[:, 1:-1, 2:]
    west_side = extended[:, 1:-1, :-2]
    return (center, north_side, south_side, east_side, west_side)


def crop_to(array, row_count, column_count):
    row_off = (array.shape[-2] - row_count) // 2
    col_off = (array.shape[-1] - column_count) // 2
    return array[..., row_off : row_off + row_count, col_off : col_off + column_count]


def mixing(reaction, field):
    return jnp.sum(reaction[:, :, None, None] * field[None], axis=1)


def per_device(increment, model_weight, winds, reaction, obs_cells, obs_weight):
    field = increment[0]
    weight = model_weight[0]
    wind_now = winds[0]
    mixer = reaction[0]
    cells = obs_cells[0, 0, 0]
    obs_scale = obs_weight[0, :, 0, 0]
    count_fields = field.shape[0]
    rows_here = field.shape[1]
    lat_start = lax.axis_index("lat") * rows_here
    lat_total = rows_here * lax.axis_size("lat")
    depth = 2

    def clear_rims(extended):
        margin = (extended.shape[1] - rows_here) // 2
        if margin == 0:
            return extended
        global_rows = lat_start - margin + jnp.arange(extended.shape[1], dtype=jnp.int32)
        inside = (global_rows >= 0) & (global_rows < lat_total)
        return jnp.where(inside[None, :, None], extended, 0.0)

    def extend_double(state):
        return clear_rims(extended_2(state, (("lat", 1), ("lon", 2)), 2))

    wind_ext = clear_rims(extended_2(wind_now, (("lat", 1), ("lon", 2)), depth))

    def tangent_core(extended):
        center, north_side, south_side, east_side, west_side = sides(extended)
        wind_here = crop_to(wind_ext, center.shape[1], center.shape[2])
        spread = north_side + south_side + east_side + west_side
        result = (1.0 - 4.0 * DIFFUSION) * center + DIFFUSION * spread
        result = (
            result
            - wind_here[0] * (east_side - west_side)
            - wind_here[1] * (north_side - south_side)
        )
        return clear_rims(result + mixing(mixer, center))

    def adjoint_core(extended):
        center, north_side, south_side, east_side, west_side = sides(extended)
        wind_here = crop_to(wind_ext, extended.shape[1], extended.shape[2])
        spread = north_side + south_side + east_side + west_side
        lon_flux = sides(wind_here[0][None] * extended)
        lat_flux = sides(wind_here[1][None] * extended)
        result = (1.0 - 4.0 * DIFFUSION) * center + DIFFUSION * spread
        result = result + (lon_flux[3] - lon_flux[4]) + (lat_flux[1] - lat_flux[2])
        return clear_rims(result + mixing(mixer.T, center))

    forward = tangent_core(tangent_core(extend_double(field)))
    flat = forward.reshape(count_fields, -1)
    picked = jnp.take(flat, cells, axis=1)
    placed = jnp.zeros_like(flat).at[:, cells].add(obs_scale * picked)
    observed = placed.reshape(forward.shape)
    earlier = send_ahead(forward)
    jump = weight * (field - earlier)
    later = send_behind(jump)
    back = adjoint_core(adjoint_core(extend_double(observed - later)))
    return (jump + back)[None]


def solution(mesh):
    in_specs = (
        P("win", None, "lat", "lon"),
        P("win", None, "lat", "lon"),
        P("win", None, "lat", "lon"),
        P("win", None, None),
        P("win", "lat", "lon", None),
        P("win", None, "lat", "lon", None),
    )
    out_specs = P("win", None, "lat", "lon")
    return jax.shard_map(
        per_device, mesh=mesh, in_specs=in_specs, out_specs=out_specs, check_vma=False
    )
```

profile of v0, /device:TPU:0, one launch (start us, length us, event | category | flops | bytes accessed | tf_op | source)
XLA Modules:
  0.0 76.4 jit_solution(4466276807434979780)
XLA Ops:
  0.0 0.0 copy-start
  0.0 0.8 %fusion.27 = (f32[2,2,256]{2,1,0:T(2,128)S(1)}, f32[2,2,256]{2,1,0:T(2,128)S(1)}) fusion(f32[2,64,256]{2,1,0:T(8,128)} %bitcast.49), kind=kLoop, calls=%fused_computation.69 | loop fusion | bytes 16384 | tf_op jit(solution)/shard_map/slice | solution.py:22
  0.8 0.5 collective-permute-start.4
  1.3 2.0 %collective-permute-start.5 = (f32[2,2,256]{2,1,0:T(2,128)S(1)}, f32[2,2,256]{2,1,0:T(2,128)S(1)}, u32[]{:S(2)}, u32[]{:S(2)}) collective-permute-start(f32[2,2,256]{2,1,0:T(2,128)S(1)} %get-tuple-element.26), channel_id=1, source_target_pairs={{4,0},{8,4},{12,8},{0,12},{5,1},{9,5},{13,9},{1,13},{6,2},{10,6},{... | collective-permute-start | bytes 12296 | tf_op jit(solution)/shard_map/ppermute | solution.py:24
  3.3 0.8 fusion.25
  4.1 0.6 collective-permute-start
  4.7 1.1 %collective-permute-start.1 = (f32[3,2,256]{2,1,0:T(2,128)S(1)}, f32[3,2,256]{2,1,0:T(2,128)S(1)}, u32[]{:S(2)}, u32[]{:S(2)}) collective-permute-start(f32[3,2,256]{2,1,0:T(2,128)S(1)} %get-tuple-element.22), channel_id=1, source_target_pairs={{4,0},{8,4},{12,8},{0,12},{5,1},{9,5},{13,9},{1,13},{6,2},{10,6},{... | collective-permute-start | bytes 18440 | tf_op jit(solution)/shard_map/ppermute | solution.py:24
  5.8 0.7 compare_select_fusion
  6.5 0.0 collective-permute-done.4
  6.5 0.0 collective-permute-done.5
  6.5 0.9 %pad_maximum_fusion.2 = f32[2,68,256]{2,1,0:T(8,128)S(1)} fusion(f32[2,2,256]{2,1,0:T(2,128)S(1)} %collective-permute-done.5, f32[2,64,256]{2,1,0:T(8,128)} %bitcast.50, f32[2,2,256]{2,1,0:T(2,128)S(1)} %collective-permute-done.4), kind=kLoop, calls=%fused_computation.49 | loop fusion | flops 69632 | bytes 278528 | tf_op jit(solution)/shard_map/concatenate | solution.py:25
  7.5 0.1 fusion.26
  7.5 2.4 %collective-permute-start.6 = (f32[2,68,2]{2,1,0:T(8,128)S(1)}, f32[2,68,2]{2,1,0:T(8,128)S(1)}, u32[]{:S(2)}, u32[]{:S(2)}) collective-permute-start(f32[2,68,2]{2,1,0:T(8,128)S(1)} %get-tuple-element.23), channel_id=1, source_target_pairs={{0,1},{1,2},{2,3},{3,0},{4,5},{5,6},{6,7},{7,4},{8,9},{9,10},{10,1... | collective-permute-start | bytes 3272 | tf_op jit(solution)/shard_map/ppermute | solution.py:21
  9.9 2.1 %collective-permute-start.7 = (f32[2,68,2]{2,1,0:T(8,128)S(1)}, f32[2,68,2]{2,1,0:T(8,128)S(1)}, u32[]{:S(2)}, u32[]{:S(2)}) collective-permute-start(f32[2,68,2]{2,1,0:T(8,128)S(1)} %get-tuple-element.24), channel_id=1, source_target_pairs={{1,0},{2,1},{3,2},{0,3},{5,4},{6,5},{7,6},{4,7},{9,8},{10,9},{11,1... | collective-permute-start | bytes 3272 | tf_op jit(solution)/shard_map/ppermute | solution.py:24
  12.0 0.7 copy.25
  12.7 0.9 %copy.17 = f32[1,3,1,1,1024]{1,4,3,2,0:T(8,128)S(1)} copy(f32[1,3,1,1,1024]{4,3,2,1,0:T(1,128)} %param.11) | data formatting | bytes 24576 | tf_op args[5]
  13.6 0.8 %collective-permute-done.6 = f32[2,68,2]{2,1,0:T(8,128)S(1)} collective-permute-done((f32[2,68,2]{2,1,0:T(8,128)S(1)}, f32[2,68,2]{2,1,0:T(8,128)S(1)}, u32[]{:S(2)}, u32[]{:S(2)}) %collective-permute-start.6) | collective-permute-done | bytes 1120 | tf_op jit(solution)/shard_map/ppermute | solution.py:21
  14.4 0.9 %collective-permute-done.7 = f32[2,68,2]{2,1,0:T(8,128)S(1)} collective-permute-done((f32[2,68,2]{2,1,0:T(8,128)S(1)}, f32[2,68,2]{2,1,0:T(8,128)S(1)}, u32[]{:S(2)}, u32[]{:S(2)}) %collective-permute-start.7) | collective-permute-done | bytes 1120 | tf_op jit(solution)/shard_map/ppermute | solution.py:24
  15.3 1.1 %maximum_select_fusion.2 = f32[2,68,260]{2,1,0:T(8,128)S(1)} fusion(f32[2,68,2]{2,1,0:T(8,128)S(1)} %collective-permute-done.7, f32[2,2,256]{2,1,0:T(2,128)S(1)} %collective-permute-done.5, f32[2,64,256]{2,1,0:T(8,128)} %bitcast.51, f32[2,2,256]{2,1,0:T(2,128)S(1)} %collective-permute-done.4, f32[2,68,2]{2,1,0:T(8,128)S(1)} %collective-permute-done.6, ...), kind=kLoop, calls=%fused_computation.29 | loop fusion | flops 176800 | bytes 282948 | tf_op jit(solution)/shard_map/jit(_where)/select_n | solution.py:75
  16.3 0.1 slice_bitcast_fusion.3
  16.5 0.0 collective-permute-done
  16.5 0.0 collective-permute-done.1
  16.5 1.0 %pad_maximum_fusion = f32[3,68,256]{2,1,0:T(8,128)S(1)} fusion(f32[3,2,256]{2,1,0:T(2,128)S(1)} %collective-permute-done.1, f32[3,64,256]{2,1,0:T(8,128)} %bitcast.47, f32[3,2,256]{2,1,0:T(2,128)S(1)} %collective-permute-done), kind=kLoop, calls=%fused_computation.28 | loop fusion | flops 104448 | bytes 417792 | tf_op jit(solution)/shard_map/concatenate | solution.py:25
  17.4 0.1 fusion.23
  17.5 1.2 %collective-permute-start.2 = (f32[3,68,2]{2,1,0:T(8,128)S(1)}, f32[3,68,2]{2,1,0:T(8,128)S(1)}, u32[]{:S(2)}, u32[]{:S(2)}) collective-permute-start(f32[3,68,2]{2,1,0:T(8,128)S(1)} %get-tuple-element.17), channel_id=1, source_target_pairs={{0,1},{1,2},{2,3},{3,0},{4,5},{5,6},{6,7},{7,4},{8,9},{9,10},{10,1... | collective-permute-start | bytes 4904 | tf_op jit(solution)/shard_map/ppermute | solution.py:21
  18.7 2.7 %collective-permute-start.3 = (f32[3,68,2]{2,1,0:T(8,128)S(1)}, f32[3,68,2]{2,1,0:T(8,128)S(1)}, u32[]{:S(2)}, u32[]{:S(2)}) collective-permute-start(f32[3,68,2]{2,1,0:T(8,128)S(1)} %get-tuple-element.18), channel_id=1, source_target_pairs={{1,0},{2,1},{3,2},{0,3},{5,4},{6,5},{7,6},{4,7},{9,8},{10,9},{11,1... | collective-permute-start | bytes 4904 | tf_op jit(solution)/shard_map/ppermute | solution.py:24
  21.4 0.1 slice_bitcast_fusion.5
  21.5 3.5 %collective-permute-done.2 = f32[3,68,2]{2,1,0:T(8,128)S(1)} collective-permute-done((f32[3,68,2]{2,1,0:T(8,128)S(1)}, f32[3,68,2]{2,1,0:T(8,128)S(1)}, u32[]{:S(2)}, u32[]{:S(2)}) %collective-permute-start.2) | collective-permute-done | bytes 1664 | tf_op jit(solution)/shard_map/ppermute | solution.py:21
  25.0 0.7 collective-permute-done.3
  25.7 1.1 %maximum_select_fusion = f32[3,68,260]{2,1,0:T(8,128)S(1)} fusion(f32[3,68,2]{2,1,0:T(8,128)S(1)} %collective-permute-done.3, f32[3,2,256]{2,1,0:T(2,128)S(1)} %collective-permute-done.1, f32[3,64,256]{2,1,0:T(8,128)} %bitcast.48, f32[3,2,256]{2,1,0:T(2,128)S(1)} %collective-permute-done, f32[3,68,2]{2,1,0:T(8,128)S(1)} %collective-permute-done.2, ...), kind=kLoop, calls=%fused_computation.23 | loop fusion | flops 265200 | bytes 424388 | tf_op jit(solution)/shard_map/jit(_where)/select_n | solution.py:75
  26.8 0.2 slice.199
  27.0 0.2 multiply_reduce_fusion.1
  27.2 0.4 add_select_fusion
  27.6 0.1 slice.210
  27.7 0.1 multiply_reduce_fusion.3
  27.8 0.3 subtract_add_fusion
  28.1 3.2 %collective-permute-start.8 = (f32[3,64,256]{2,1,0:T(8,128)S(1)}, f32[3,64,256]{2,1,0:T(8,128)S(1)}, u32[]{:S(2)}, u32[]{:S(2)}) collective-permute-start(f32[3,64,256]{2,1,0:T(8,128)S(1)} %subtract_add_fusion), channel_id=1, source_target_pairs={{0,16},{1,17},{2,18},{3,19},{4,20},{5,21},{6,22},{7,23},{8,24},{9,... | collective-permute-start | bytes 589832 | tf_op jit(solution)/shard_map/ppermute | solution.py:12
  31.3 3.3 %collective-permute-done.8 = f32[3,64,256]{2,1,0:T(8,128)S(1)} collective-permute-done((f32[3,64,256]{2,1,0:T(8,128)S(1)}, f32[3,64,256]{2,1,0:T(8,128)S(1)}, u32[]{:S(2)}, u32[]{:S(2)}) %collective-permute-start.8) | collective-permute-done | bytes 196640 | tf_op jit(solution)/shard_map/ppermute | solution.py:12
  34.7 0.0 copy-done
  34.7 0.0 copy-done.1
  34.7 1.3 %collective-permute-start.9 = (f32[3,64,256]{2,1,0:T(8,128)S(1)}, f32[3,64,256]{2,1,0:T(8,128)S(1)}, u32[]{:S(2)}, u32[]{:S(2)}) collective-permute-start(f32[3,64,256]{2,1,0:T(8,128)S(1)} %bitcast_multiply_fusion.2), channel_id=1, source_target_pairs={{16,0},{17,1},{18,2},{19,3},{20,4},{21,5},{22,6},{23,7},{24,8},{25... | collective-permute-start | bytes 589832 | tf_op jit(solution)/shard_map/ppermute | solution.py:12
  36.0 0.0 copy-done.2
  36.0 4.6 %copy.18 = f32[3,64,256]{0,2,1:T(8,128)} copy(f32[3,64,256]{2,1,0:T(8,128)S(1)} %subtract_add_fusion) | data formatting | bytes 393216 | tf_op jit(solution)/shard_map/add | solution.py:92
  40.7 16.1 %scatter_custom_fusion = f32[3,16384]{0,1:T(8,128)} fusion(s32[1024]{0:T(1024)S(1)} %bitcast.58, f32[]{:T(128)} %constant.20.clone.1, f32[1,3,1,1,1024]{1,4,3,2,0:T(8,128)S(1)} %copy.17, f32[]{:T(128)} %constant.44.clone.1, pred[1024]{0:T(1024)(128)(4,1)S(1)} %compare_and_fusion, f32[3,16384]{0,1:T(8,128)} %bitcast.44, s32[1024]{0:T(1024)S(1)} %broadcast_clamp_fusion), kind=kCustom, calls=%fused_computation.2 | custom fusion | flops 9216 | bytes 922632 | tf_op jit(solution)/shard_map/scatter-add | solution.py:107
  56.8 5.2 %copy.19 = f32[3,64,256]{2,1,0:T(8,128)S(1)} copy(f32[3,64,256]{0,2,1:T(8,128)} %bitcast.45) | data formatting | bytes 393216 | tf_op jit(solution)/shard_map/reshape | solution.py:108
  62.0 0.0 collective-permute-done.9
  62.1 0.1 collective-permute-start.10
  62.2 1.7 %collective-permute-start.11 = (f32[3,2,256]{2,1,0:T(2,128)S(1)}, f32[3,2,256]{2,1,0:T(2,128)S(1)}, u32[]{:S(2)}, u32[]{:S(2)}) collective-permute-start(f32[3,2,256]{2,1,0:T(2,128)S(1)} %get-tuple-element.20), channel_id=1, source_target_pairs={{4,0},{8,4},{12,8},{0,12},{5,1},{9,5},{13,9},{1,13},{6,2},{10,6},{... | collective-permute-start | bytes 18440 | tf_op jit(solution)/shard_map/ppermute | solution.py:24
  63.9 0.0 copy-done.3
  63.9 0.1 copy.23
  64.0 1.2 %collective-permute-done.10 = f32[3,2,256]{2,1,0:T(2,128)S(1)} collective-permute-done((f32[3,2,256]{2,1,0:T(2,128)S(1)}, f32[3,2,256]{2,1,0:T(2,128)S(1)}, u32[]{:S(2)}, u32[]{:S(2)}) %collective-permute-start.10) | collective-permute-done | bytes 6176 | tf_op jit(solution)/shard_map/ppermute | solution.py:21
  65.2 0.0 collective-permute-done.11
  65.3 0.1 fusion.22
  65.4 0.2 collective-permute-start.12
  65.6 3.7 %collective-permute-start.13 = (f32[3,68,2]{2,1,0:T(8,128)S(1)}, f32[3,68,2]{2,1,0:T(8,128)S(1)}, u32[]{:S(2)}, u32[]{:S(2)}) collective-permute-start(f32[3,68,2]{2,1,0:T(8,128)S(1)} %get-tuple-element.12), channel_id=1, source_target_pairs={{1,0},{2,1},{3,2},{0,3},{5,4},{6,5},{7,6},{4,7},{9,8},{10,9},{11,1... | collective-permute-start | bytes 4904 | tf_op jit(solution)/shard_map/ppermute | solution.py:24
  69.3 3.9 %collective-permute-done.12 = f32[3,68,2]{2,1,0:T(8,128)S(1)} collective-permute-done((f32[3,68,2]{2,1,0:T(8,128)S(1)}, f32[3,68,2]{2,1,0:T(8,128)S(1)}, u32[]{:S(2)}, u32[]{:S(2)}) %collective-permute-start.12) | collective-permute-done | bytes 1664 | tf_op jit(solution)/shard_map/ppermute | solution.py:21
  73.2 0.5 collective-permute-done.13
  73.7 0.2 broadcast_multiply_fusion.1
  74.0 0.2 slice.221
  74.2 0.2 multiply_reduce_fusion
  74.3 0.7 broadcast_multiply_fusion.3
  75.1 0.1 slice.232
  75.2 0.1 multiply_reduce_fusion.2
  75.3 1.1 %fusion.16 = f32[1,3,64,256]{3,2,1,0:T(8,128)} fusion(f32[3,64,256]{2,1,0:T(8,128)S(1)} %bitcast_multiply_fusion.2, f32[3,64,256]{2,1,0:T(8,128)S(1)} %multiply_reduce_fusion.2, f32[3,66,258]{2,1,0:T(8,128)S(1)} %broadcast_multiply_fusion.2, f32[3,66,258]{2,1,0:T(8,128)S(1)} %get-tuple-element.5, f32[3,66,258]{2,1,0:T(8,128)S(1)} %get-tuple-element.6), kind=kLoop, calls=%fused_computation.35 | loop fusion | flops 589824 | bytes 2359296 | tf_op jit(solution)/shard_map/broadcast_in_dim | solution.py:113
  (14 shorter events, 0.2 us)
Async XLA Ops:
  0.0 34.7 %copy-start = (f32[1,3,64,256]{3,2,1,0:T(8,128)S(1)}, f32[1,3,64,256]{3,2,1,0:T(8,128)}, u32[]{:S(2)}) copy-start(f32[1,3,64,256]{3,2,1,0:T(8,128)} %param.6) | copy-start | bytes 589828
  0.0 36.0 %copy-start.2 = (s32[1,1,1,1024]{3,2,1,0:T(1,128)S(1)}, s32[1,1,1,1024]{3,2,1,0:T(1,128)}, u32[]{:S(2)}) copy-start(s32[1,1,1,1024]{3,2,1,0:T(1,128)} %param.10) | copy-start | bytes 12292
  0.0 34.7 %copy-start.1 = (f32[1,3,64,256]{3,2,1,0:T(8,128)S(1)}, f32[1,3,64,256]{3,2,1,0:T(8,128)}, u32[]{:S(2)}) copy-start(f32[1,3,64,256]{3,2,1,0:T(8,128)} %param.7) | copy-start | bytes 589828
  0.8 5.7 %collective-permute-start.4 = (f32[2,2,256]{2,1,0:T(2,128)S(1)}, f32[2,2,256]{2,1,0:T(2,128)S(1)}, u32[]{:S(2)}, u32[]{:S(2)}) collective-permute-start(f32[2,2,256]{2,1,0:T(2,128)S(1)} %get-tuple-element.25), channel_id=1, source_target_pairs={{0,4},{4,8},{8,12},{12,0},{1,5},{5,9},{9,13},{13,1},{2,6},{6,10},{... | collective-permute-start | bytes 12296 | tf_op jit(solution)/shard_map/ppermute | solution.py:21
  1.3 5.2 %collective-permute-start.5 = (f32[2,2,256]{2,1,0:T(2,128)S(1)}, f32[2,2,256]{2,1,0:T(2,128)S(1)}, u32[]{:S(2)}, u32[]{:S(2)}) collective-permute-start(f32[2,2,256]{2,1,0:T(2,128)S(1)} %get-tuple-element.26), channel_id=1, source_target_pairs={{4,0},{8,4},{12,8},{0,12},{5,1},{9,5},{13,9},{1,13},{6,2},{10,6},{... | collective-permute-start | bytes 12296 | tf_op jit(solution)/shard_map/ppermute | solution.py:24
  4.1 12.4 %collective-permute-start = (f32[3,2,256]{2,1,0:T(2,128)S(1)}, f32[3,2,256]{2,1,0:T(2,128)S(1)}, u32[]{:S(2)}, u32[]{:S(2)}) collective-permute-start(f32[3,2,256]{2,1,0:T(2,128)S(1)} %get-tuple-element.21), channel_id=1, source_target_pairs={{0,4},{4,8},{8,12},{12,0},{1,5},{5,9},{9,13},{13,1},{2,6},{6,10},{... | collective-permute-start | bytes 18440 | tf_op jit(solution)/shard_map/ppermute | solution.py:21
  4.7 11.8 %collective-permute-start.1 = (f32[3,2,256]{2,1,0:T(2,128)S(1)}, f32[3,2,256]{2,1,0:T(2,128)S(1)}, u32[]{:S(2)}, u32[]{:S(2)}) collective-permute-start(f32[3,2,256]{2,1,0:T(2,128)S(1)} %get-tuple-element.22), channel_id=1, source_target_pairs={{4,0},{8,4},{12,8},{0,12},{5,1},{9,5},{13,9},{1,13},{6,2},{10,6},{... | collective-permute-start | bytes 18440 | tf_op jit(solution)/shard_map/ppermute | solution.py:24
  7.5 6.9 %collective-permute-start.6 = (f32[2,68,2]{2,1,0:T(8,128)S(1)}, f32[2,68,2]{2,1,0:T(8,128)S(1)}, u32[]{:S(2)}, u32[]{:S(2)}) collective-permute-start(f32[2,68,2]{2,1,0:T(8,128)S(1)} %get-tuple-element.23), channel_id=1, source_target_pairs={{0,1},{1,2},{2,3},{3,0},{4,5},{5,6},{6,7},{7,4},{8,9},{9,10},{10,1... | collective-permute-start | bytes 3272 | tf_op jit(solution)/shard_map/ppermute | solution.py:21
  9.9 5.4 %collective-permute-start.7 = (f32[2,68,2]{2,1,0:T(8,128)S(1)}, f32[2,68,2]{2,1,0:T(8,128)S(1)}, u32[]{:S(2)}, u32[]{:S(2)}) collective-permute-start(f32[2,68,2]{2,1,0:T(8,128)S(1)} %get-tuple-element.24), channel_id=1, source_target_pairs={{1,0},{2,1},{3,2},{0,3},{5,4},{6,5},{7,6},{4,7},{9,8},{10,9},{11,1... | collective-permute-start | bytes 3272 | tf_op jit(solution)/shard_map/ppermute | solution.py:24
  17.5 7.5 %collective-permute-start.2 = (f32[3,68,2]{2,1,0:T(8,128)S(1)}, f32[3,68,2]{2,1,0:T(8,128)S(1)}, u32[]{:S(2)}, u32[]{:S(2)}) collective-permute-start(f32[3,68,2]{2,1,0:T(8,128)S(1)} %get-tuple-element.17), channel_id=1, source_target_pairs={{0,1},{1,2},{2,3},{3,0},{4,5},{5,6},{6,7},{7,4},{8,9},{9,10},{10,1... | collective-permute-start | bytes 4904 | tf_op jit(solution)/shard_map/ppermute | solution.py:21
  18.7 7.0 %collective-permute-start.3 = (f32[3,68,2]{2,1,0:T(8,128)S(1)}, f32[3,68,2]{2,1,0:T(8,128)S(1)}, u32[]{:S(2)}, u32[]{:S(2)}) collective-permute-start(f32[3,68,2]{2,1,0:T(8,128)S(1)} %get-tuple-element.18), channel_id=1, source_target_pairs={{1,0},{2,1},{3,2},{0,3},{5,4},{6,5},{7,6},{4,7},{9,8},{10,9},{11,1... | collective-permute-start | bytes 4904 | tf_op jit(solution)/shard_map/ppermute | solution.py:24
  28.1 6.5 %collective-permute-start.8 = (f32[3,64,256]{2,1,0:T(8,128)S(1)}, f32[3,64,256]{2,1,0:T(8,128)S(1)}, u32[]{:S(2)}, u32[]{:S(2)}) collective-permute-start(f32[3,64,256]{2,1,0:T(8,128)S(1)} %subtract_add_fusion), channel_id=1, source_target_pairs={{0,16},{1,17},{2,18},{3,19},{4,20},{5,21},{6,22},{7,23},{8,24},{9,... | collective-permute-start | bytes 589832 | tf_op jit(solution)/shard_map/ppermute | solution.py:12
  34.7 27.3 %collective-permute-start.9 = (f32[3,64,256]{2,1,0:T(8,128)S(1)}, f32[3,64,256]{2,1,0:T(8,128)S(1)}, u32[]{:S(2)}, u32[]{:S(2)}) collective-permute-start(f32[3,64,256]{2,1,0:T(8,128)S(1)} %bitcast_multiply_fusion.2), channel_id=1, source_target_pairs={{16,0},{17,1},{18,2},{19,3},{20,4},{21,5},{22,6},{23,7},{24,8},{25... | collective-permute-start | bytes 589832 | tf_op jit(solution)/shard_map/ppermute | solution.py:12
  56.8 7.1 %copy-start.3 = (f32[1,3,3]{2,0,1:T(1,128)S(1)}, f32[1,3,3]{2,0,1:T(1,128)}, u32[]{:S(2)}) copy-start(f32[1,3,3]{2,0,1:T(1,128)} %param.9) | copy-start | bytes 112
  62.1 3.1 %collective-permute-start.10 = (f32[3,2,256]{2,1,0:T(2,128)S(1)}, f32[3,2,256]{2,1,0:T(2,128)S(1)}, u32[]{:S(2)}, u32[]{:S(2)}) collective-permute-start(f32[3,2,256]{2,1,0:T(2,128)S(1)} %get-tuple-element.19), channel_id=1, source_target_pairs={{0,4},{4,8},{8,12},{12,0},{1,5},{5,9},{9,13},{13,1},{2,6},{6,10},{... | collective-permute-start | bytes 18440 | tf_op jit(solution)/shard_map/ppermute | solution.py:21
  62.2 3.1 %collective-permute-start.11 = (f32[3,2,256]{2,1,0:T(2,128)S(1)}, f32[3,2,256]{2,1,0:T(2,128)S(1)}, u32[]{:S(2)}, u32[]{:S(2)}) collective-permute-start(f32[3,2,256]{2,1,0:T(2,128)S(1)} %get-tuple-element.20), channel_id=1, source_target_pairs={{4,0},{8,4},{12,8},{0,12},{5,1},{9,5},{13,9},{1,13},{6,2},{10,6},{... | collective-permute-start | bytes 18440 | tf_op jit(solution)/shard_map/ppermute | solution.py:24
  65.4 7.8 %collective-permute-start.12 = (f32[3,68,2]{2,1,0:T(8,128)S(1)}, f32[3,68,2]{2,1,0:T(8,128)S(1)}, u32[]{:S(2)}, u32[]{:S(2)}) collective-permute-start(f32[3,68,2]{2,1,0:T(8,128)S(1)} %get-tuple-element.11), channel_id=1, source_target_pairs={{0,1},{1,2},{2,3},{3,0},{4,5},{5,6},{6,7},{7,4},{8,9},{9,10},{10,1... | collective-permute-start | bytes 4904 | tf_op jit(solution)/shard_map/ppermute | solution.py:21
  65.6 8.2 %collective-permute-start.13 = (f32[3,68,2]{2,1,0:T(8,128)S(1)}, f32[3,68,2]{2,1,0:T(8,128)S(1)}, u32[]{:S(2)}, u32[]{:S(2)}) collective-permute-start(f32[3,68,2]{2,1,0:T(8,128)S(1)} %get-tuple-element.12), channel_id=1, source_target_pairs={{1,0},{2,1},{3,2},{0,3},{5,4},{6,5},{7,6},{4,7},{9,8},{10,9},{11,1... | collective-permute-start | bytes 4904 | tf_op jit(solution)/shard_map/ppermute | solution.py:24
where the time goes:
time: 76.9 us; the launch traced here: 76.4 us
  other arithmetic  24.4 us (32%)
  starting transfers between devices  22.7 us (30%)
  waiting for transfers between devices  14.9 us (19%)
  local copies, waits for them, and re-layouts  14.1 us (18%)
    scatter-add x1, other arithmetic, per_device(): placed = jnp.zeros_like(flat).at[:, cells].add(obs_scale * picked)  16.1 us
    ppermute x6, starting transfers between devices, extended_2(): lax.ppermute(lax.slice_in_dim(block, 0, width, axis=dim), axis, backward)  13.3 us
    ppermute x6, waiting for transfers between devices, extended_2(): lax.ppermute(lax.slice_in_dim(block, block.shape[dim] - width, None, axis...  9.45 us
    reshape x1, local copies, waits for them, and re-layouts, per_device(): observed = placed.reshape(forward.shape)  5.23 us
    ppermute x6, starting transfers between devices, extended_2(): lax.ppermute(lax.slice_in_dim(block, block.shape[dim] - width, None, axis...  4.98 us
    add x1, local copies, waits for them, and re-layouts, tangent_core(): return clear_rims(result + mixing(mixer, center))  4.63 us
    ppermute x2, starting transfers between devices, from_behind(): lax.ppermute(value, axis, [(source, source + steps) for source in range(f...  4.49 us
    ppermute x2, waiting for transfers between devices, from_behind(): lax.ppermute(value, axis, [(source, source + steps) for source in range(f...  3.33 us
  transfers between devices with their start and end apart: 14, of which 8 were waited for; matrix products, arithmetic and copies ran while one was open for 41% of the time, Pallas kernels for 0%

commit v1 on v0

v1 whole, which is shorter than its diff:
```python
import functools

import jax
import jax.numpy as jnp
from jax import lax
from jax.experimental import pallas as pl
from jax.experimental.pallas import tpu as pltpu
from jax.sharding import PartitionSpec as P

DIFFUSION = 0.15
HALO = 4
LANES = 128
F32 = jnp.float32


def even_pairs(n):
    return [(i, i ^ 1) for i in range(n)]


def odd_pairs(n):
    return [(i, (i + 1 if i % 2 else i - 1) % n) for i in range(n)]


def ring(n, step):
    return [(i, (i + step) % n) for i in range(n)]


def neighbour_swap(even_msg, odd_msg, axis):
    n = lax.axis_size(axis)
    return (
        lax.ppermute(even_msg, axis, even_pairs(n)),
        lax.ppermute(odd_msg, axis, odd_pairs(n)),
    )


def window_swap(down, up):
    n = lax.axis_size("win")
    if n == 2:
        got = lax.ppermute(down, "win", even_pairs(n))
        return got, got
    return lax.ppermute(down, "win", ring(n, -1)), lax.ppermute(up, "win", ring(n, 1))


def sub_iota(shape):
    return lax.broadcasted_iota(jnp.int32, shape, len(shape) - 2)


def lane_iota(shape):
    return lax.broadcasted_iota(jnp.int32, shape, len(shape) - 1)


def pack_columns(planes, low):
    out = None
    for j, plane in enumerate(planes):
        block = plane[:, :LANES] if low else plane[:, -LANES:]
        shift = (HALO * j if low else HALO * j + HALO) % LANES
        if shift:
            block = pltpu.roll(block, shift, 1)
        lane = lane_iota(block.shape)
        out = block if out is None else jnp.where(lane >= HALO * j, block, out)
    return out


def start_kernel(swap2, inc, wgt, wind, mix, cells, scale, hmap, row_even, row_odd, col_low, col_high, *bulk):
    fields, rows, cols = inc.shape
    nobs = cells.shape[-1]
    index = cells[...]
    row_hot = sub_iota((rows, nobs)) == index // cols
    col_hot = (sub_iota((cols, nobs)) == index % cols).astype(F32).astype(jnp.bfloat16)
    terms = []
    for f in range(fields):
        rest = scale[f]
        for _ in range(3):
            part = rest.astype(jnp.bfloat16)
            rest = rest - part.astype(F32)
            terms.append(jnp.where(row_hot, part.astype(F32), 0.0).astype(jnp.bfloat16))
    sums = lax.dot_general(
        jnp.concatenate(terms, axis=0), col_hot, (((1,), (1,)), ((), ())), preferred_element_type=F32
    )
    planes = [inc[f] for f in range(fields)] + [wind[0], wind[1]]
    for f in range(fields):
        base = 3 * f * rows
        value = sums[base : base + rows] + (
            sums[base + rows : base + 2 * rows] + sums[base + 2 * rows : base + 3 * rows]
        )
        hmap[f] = value
        planes.append(value)
    planes += [wgt[f] for f in range(fields)]
    col_low[...] = pack_columns(planes, True)
    col_high[...] = pack_columns(planes, False)
    is_even = lax.axis_index("lat") % 2 == 0
    upper = sub_iota((8, cols)) < HALO
    for m in range((len(planes) + 1) // 2):
        one, two = planes[2 * m], planes[min(2 * m + 1, len(planes) - 1)]
        first = jnp.where(upper, one[:8], pltpu.roll(two[:8], HALO, 0))
        last = jnp.where(upper, pltpu.roll(one[-8:], HALO, 0), two[-8:])
        row_even[pl.ds(8 * m, 8), :] = jnp.where(is_even, last, first)
        row_odd[pl.ds(8 * m, 8), :] = jnp.where(is_even, first, last)
    mixrows = jnp.zeros((rows, cols), F32)
    which = sub_iota((rows, cols))
    for f in range(fields):
        for g in range(fields):
            mixrows = jnp.where(which == f * fields + g, mix[f, g], mixrows)
    up = [wind[0], wind[1], mixrows]
    for f in range(fields):
        if swap2:
            sends_up = lax.axis_index("win") == 0
            bulk[0][f] = inc[f]
            bulk[0][fields + f] = jnp.where(sends_up, up[f], wgt[f])
        else:
            bulk[0][f] = inc[f]
            bulk[0][fields + f] = wgt[f]
            bulk[1][f] = inc[f]
            bulk[1][fields + f] = up[f]


def rows_kernel(count, got_even, got_odd, col_low, col_high, halo_rows, msg_even, msg_odd):
    cols = got_even.shape[-1]
    rows = col_low.shape[0]
    here = lax.axis_index("lat")
    is_even = here % 2 == 0
    upper = sub_iota((8, cols)) < HALO
    from_high = (here < lax.axis_size("lat") - 1).astype(jnp.int32)
    from_low = (here > 0).astype(jnp.int32)
    inside = jnp.where(upper, from_high, from_low) > 0
    blocks = []
    for m in range((count + 1) // 2):
        a = got_even[pl.ds(8 * m, 8), :]
        b = got_odd[pl.ds(8 * m, 8), :]
        high = jnp.where(is_even, a, b)
        low = jnp.where(is_even, b, a)
        one = jnp.where(upper, high, pltpu.roll(low, HALO, 0))
        two = jnp.where(upper, pltpu.roll(high, HALO, 0), low)
        blocks += [jnp.where(inside, one, 0.0), jnp.where(inside, two, 0.0)]
    blocks = blocks[:count]
    for j, block in enumerate(blocks):
        halo_rows[j] = block
    lon_even = lax.axis_index("lon") % 2 == 0
    low_tail = pack_columns(blocks, True)
    high_tail = pack_columns(blocks, False)
    msg_even[pl.ds(0, rows), :] = jnp.where(lon_even, col_high[...], col_low[...])
    msg_odd[pl.ds(0, rows), :] = jnp.where(lon_even, col_low[...], col_high[...])
    msg_even[pl.ds(rows, 8), :] = jnp.where(lon_even, high_tail, low_tail)
    msg_odd[pl.ds(rows, 8), :] = jnp.where(lon_even, low_tail, high_tail)


def columns_kernel(swap2, fields, count, got_even, got_odd, halo_rows, halo_cols, *msgs):
    lon_even = lax.axis_index("lon") % 2 == 0
    a = got_even[...]
    b = got_odd[...]
    east = jnp.where(lon_even, a, b)
    west = jnp.where(lon_even, b, a)
    lane = lane_iota(a.shape)
    cols = []
    for j in range(count):
        right = pltpu.roll(east, (LANES - HALO * j) % LANES, 1) if j else east
        left = pltpu.roll(west, (LANES - HALO - HALO * j) % LANES, 1)
        block = jnp.where(lane < HALO, right, jnp.where(lane >= LANES - HALO, left, 0.0))
        halo_cols[j] = block
        cols.append(block)
    first = list(range(fields))
    down = first + list(range(count - fields, count))
    up = first + [fields, fields + 1, fields + 1]
    total = a.shape[0]
    sub = sub_iota((8, halo_rows.shape[-1]))
    keep = (sub < 2) | (sub >= 6)

    def packed(chosen):
        rows = []
        for m in range(fields):
            one, two = halo_rows[chosen[2 * m]], halo_rows[chosen[2 * m + 1]]
            rows.append(jnp.where(keep, one, pltpu.roll(two, 4, 0)))
        out = cols[chosen[0]]
        for j in range(1, 2 * fields):
            moved = pltpu.roll(cols[chosen[j]], 4 * j, 1)
            out = jnp.where((lane >= 4 * j - 2) & (lane < 4 * j + 2), moved, out)
        return rows, out

    def store(ref, rows, out):
        for m, block in enumerate(rows):
            for half in range(block.shape[-1] // LANES):
                ref[pl.ds(total + 8 * (m * (block.shape[-1] // LANES) + half), 8), :] = block[
                    :, half * LANES : (half + 1) * LANES
                ]
        ref[pl.ds(0, total), :] = out

    down_rows, down_cols = packed(down)
    up_rows, up_cols = packed(up)
    if swap2:
        sends_up = lax.axis_index("win") == 0
        store(
            msgs[0],
            [jnp.where(sends_up, u, d) for u, d in zip(up_rows, down_rows)],
            jnp.where(sends_up, up_cols, down_cols),
        )
    else:
        store(msgs[0], down_rows, down_cols)
        store(msgs[1], up_rows, up_cols)


def extended(tile, rows, cols):
    return jnp.concatenate([jnp.concatenate([tile, rows], axis=0), cols], axis=1)


def row_mask(rows, width):
    here = lax.axis_index("lat")
    upper = sub_iota((8, width)) < HALO
    from_high = (here < lax.axis_size("lat") - 1).astype(jnp.int32)
    from_low = (here > 0).astype(jnp.int32)
    inside = jnp.where(upper, from_high, from_low) > 0

    def clear(field):
        return jnp.concatenate([field[:rows], jnp.where(inside, field[rows:], 0.0)], axis=0)

    return clear


def north(x):
    return pltpu.roll(x, x.shape[0] - 1, 0)


def south(x):
    return pltpu.roll(x, 1, 0)


def east_of(x):
    return pltpu.roll(x, x.shape[1] - 1, 1)


def west_of(x):
    return pltpu.roll(x, 1, 1)


def blend(mix, field, f):
    total = None
    for g in range(len(field)):
        factor = mix(f, g)
        if f == g:
            factor = factor + (1.0 - 4.0 * DIFFUSION)
        term = factor * field[g]
        total = term if total is None else total + term
    return total


def tangent(field, u, v, mix):
    kn, ks, ke, kw = DIFFUSION - v, DIFFUSION + v, DIFFUSION - u, DIFFUSION + u
    return [
        blend(mix, field, f)
        + (kn * north(x) + ks * south(x))
        + (ke * east_of(x) + kw * west_of(x))
        for f, x in enumerate(field)
    ]


def adjoint(field, u, v, mix):
    kn, ks, ke, kw = DIFFUSION + v, DIFFUSION - v, DIFFUSION + u, DIFFUSION - u
    return [
        blend(lambda a, b: mix(b, a), field, f)
        + (north(kn * x) + south(ks * x))
        + (east_of(ke * x) + west_of(kw * x))
        for f, x in enumerate(field)
    ]


def forward_kernel(inc, wind, mix, halo_rows, halo_cols, fwd):
    fields, rows, _ = inc.shape
    field = [extended(inc[f], halo_rows[f], halo_cols[f]) for f in range(fields)]
    u, v = [extended(wind[i], halo_rows[fields + i], halo_cols[fields + i]) for i in range(2)]
    clear = row_mask(rows, field[0].shape[1])
    mixer = lambda f, g: mix[f, g]
    field = [clear(x) for x in tangent(field, u, v, mixer)]
    field = tangent(field, u, v, mixer)
    for f in range(fields):
        fwd[f] = field[f]


def finish_kernel(fwd, inc, wgt, wind, mix, hmap, halo_rows, halo_cols, above, below, ring_above, ring_below, out):
    fields, rows, cols = inc.shape
    blocks = cols // LANES
    total = halo_cols.shape[1]
    here = lax.axis_index("win")
    clear = row_mask(rows, cols + LANES)

    def unpack(bulk, msg, j):
        m, second = j // 2, j % 2
        base = total + 8 * m * blocks
        block = jnp.concatenate([msg[pl.ds(base + 8 * h, 8), :] for h in range(blocks)], axis=1)
        if second:
            block = pltpu.roll(block, 4, 0)
        side = msg[pl.ds(0, total), :]
        if j:
            side = pltpu.roll(side, LANES - 4 * j, 1)
        return extended(bulk[j], block, side)

    has_later = here < lax.axis_size("win") - 1
    source = []
    for f in range(fields):
        x = fwd[f]
        later = unpack(above, ring_above, fields + f) * (unpack(above, ring_above, f) - x)
        h = extended(hmap[f], halo_rows[fields + 2 + f], halo_cols[fields + 2 + f])
        source.append(clear(h * x - jnp.where(has_later, later, 0.0)))
    u, v = [extended(wind[i], halo_rows[fields + i], halo_cols[fields + i]) for i in range(2)]
    mixer = lambda f, g: mix[f, g]
    back = [clear(x) for x in adjoint(source, u, v, mixer)]
    back = adjoint(back, u, v, mixer)

    has_earlier = here > 0
    prior = [clear(unpack(below, ring_below, f)) for f in range(fields)]
    u, v = [unpack(below, ring_below, fields + i) for i in range(2)]
    mixrows = below[2 * fields - 1]

    def prior_mix(f, g):
        return mixrows[f * fields + g : f * fields + g + 1, 0:1]

    prior = [clear(x) for x in tangent(prior, u, v, prior_mix)]
    prior = tangent(prior, u, v, prior_mix)
    for f in range(fields):
        earlier = jnp.where(has_earlier, prior[f][:rows, :cols], 0.0)
        out[f] = wgt[f] * (inc[f] - earlier) + back[f][:rows, :cols]


def vmem():
    return pl.BlockSpec(memory_space=pltpu.VMEM)


def smem():
    return pl.BlockSpec(memory_space=pltpu.SMEM)


def call(kernel, name, in_specs, shapes, flops):
    return pl.pallas_call(
        kernel,
        name=name,
        out_shape=[jax.ShapeDtypeStruct(s, F32) for s in shapes],
        in_specs=in_specs,
        out_specs=[vmem()] * len(shapes),
        cost_estimate=pl.CostEstimate(flops=flops, bytes_accessed=1 << 20, transcendentals=0),
    )


def per_device(increment, model_weight, winds, reaction, obs_cells, obs_weight):
    inc = increment[0]
    wgt = model_weight[0]
    wind = winds[0]
    mix = reaction[0]
    fields, rows, cols = inc.shape
    nobs = obs_cells.shape[-1]
    cells = obs_cells.reshape(1, nobs)
    scale = obs_weight.reshape(fields, 1, nobs)
    count = 3 * fields + 2
    pairs = (count + 1) // 2
    tall = rows + 2 * HALO
    swap2 = lax.axis_size("win") == 2
    copies = 1 if swap2 else 2

    hmap, row_even, row_odd, col_low, col_high, *bulk = call(
        functools.partial(start_kernel, swap2),
        "start",
        [vmem(), vmem(), vmem(), smem(), vmem(), vmem()],
        [(fields, rows, cols)] + [(8 * pairs, cols)] * 2 + [(rows, LANES)] * 2 + [(2 * fields, rows, cols)] * copies,
        1 << 24,
    )(inc, wgt, wind, mix, cells, scale)
    got_even, got_odd = neighbour_swap(row_even, row_odd, "lat")
    above, below = window_swap(bulk[0], bulk[-1])

    halo_rows, msg_even, msg_odd = call(
        functools.partial(rows_kernel, count),
        "rows",
        [vmem()] * 4,
        [(count, 8, cols), (tall, LANES), (tall, LANES)],
        1 << 16,
    )(got_even, got_odd, col_low, col_high)
    got_even, got_odd = neighbour_swap(msg_even, msg_odd, "lon")

    ring_shape = (tall + 8 * fields * (cols // LANES), LANES)
    halo_cols, *rings = call(
        functools.partial(columns_kernel, swap2, fields, count),
        "columns",
        [vmem()] * 3,
        [(count, tall, LANES)] + [ring_shape] * copies,
        1 << 16,
    )(got_even, got_odd, halo_rows)
    ring_above, ring_below = window_swap(rings[0], rings[-1])

    (fwd,) = call(
        forward_kernel,
        "forward",
        [vmem(), vmem(), smem(), vmem(), vmem()],
        [(fields, tall, cols + LANES)],
        1 << 24,
    )(inc, wind, mix, halo_rows, halo_cols)

    (out,) = call(
        finish_kernel,
        "finish",
        [vmem()] * 4 + [smem()] + [vmem()] * 7,
        [(fields, rows, cols)],
        1 << 25,
    )(fwd, inc, wgt, wind, mix, hmap, halo_rows, halo_cols, above, below, ring_above, ring_below)
    return out[None]


def solution(mesh):
    in_specs = (
        P("win", None, "lat", "lon"),
        P("win", None, "lat", "lon"),
        P("win", None, "lat", "lon"),
        P("win", None, None),
        P("win", "lat", "lon", None),
        P("win", None, "lat", "lon", None),
    )
    out_specs = P("win", None, "lat", "lon")
    return jax.shard_map(
        per_device, mesh=mesh, in_specs=in_specs, out_specs=out_specs, check_vma=False
    )
```

time: 76.9 us -> 31.6 us (0.41)
  other arithmetic: 24.4 us -> 0 us
  starting transfers between devices: 22.7 us -> 9.19 us
  Pallas kernels: 0 us -> 11.8 us
  local copies, waits for them, and re-layouts: 14.1 us -> 3.28 us
  waiting for transfers between devices: 14.9 us -> 6.99 us
    scatter-add x1 -> x0, other arithmetic: 16.1 us -> none  [per_device(): placed = jnp.zeros_like(flat).at[:, cells].add(obs_scale * picked)]
    ppermute x14 -> x6, starting transfers between devices: 22.7 us -> 9.19 us  [the longest x2 4.11 us: neighbour_swap(): lax.ppermute(odd_msg, axis, odd_pairs(n))]
    pallas_call x0 -> x5, Pallas kernels: none -> 11.8 us  [the longest x1 3.32 us: per_device(): call(finish_kernel, 'finish', [vmem()] * 4 + [smem()] + [vmem()] * 7, [(f...]
    ppermute x14 -> x6, waiting for transfers between devices: 14.9 us -> 6.99 us  [the longest x2 5.23 us: neighbour_swap(): lax.ppermute(odd_msg, axis, odd_pairs(n))]
    reshape x1 -> x0, local copies, waits for them, and re-layouts: 5.23 us -> none  [per_device(): observed = placed.reshape(forward.shape)]
    add x1 -> x0, local copies, waits for them, and re-layouts: 4.63 us -> none  [tangent_core(): return clear_rims(result + mixing(mixer, center))]
    select_n x4 -> x0, other arithmetic: 3.33 us -> none  [the longest x3 2.64 us: clear_rims(): return jnp.where(inside[None, :, None], extended, 0.0)]
    slice x10 -> x0, local copies, waits for them, and re-layouts: 2.35 us -> none  [the longest x6 1.81 us: extended_2(): lax.slice_in_dim(block, block.shape[dim] - width, None, axis=dim)]
  transfers between devices with their start and end apart: 14 -> 6, of which waited for: 8 -> 4; matrix products, arithmetic and copies ran while one was open for 41% -> 0% of each run, Pallas kernels for 0% -> 19%
where the time goes in v1:
time: 31.6 us; the launch traced here: 31.3 us
  Pallas kernels  11.8 us (37%)
  starting transfers between devices  9.19 us (29%)
  waiting for transfers between devices  6.99 us (22%)
  local copies, waits for them, and re-layouts  3.28 us (10%)
    ppermute x2, waiting for transfers between devices, neighbour_swap(): lax.ppermute(odd_msg, axis, odd_pairs(n))  5.23 us
    ppermute x2, starting transfers between devices, neighbour_swap(): lax.ppermute(odd_msg, axis, odd_pairs(n))  4.11 us
    ppermute x2, starting transfers between devices, window_swap(): got = lax.ppermute(down, 'win', even_pairs(n))  3.5 us
    pallas_call x1, Pallas kernels, per_device(): call(finish_kernel, 'finish', [vmem()] * 4 + [smem()] + [vmem()] * 7, [(f...  3.32 us
    unnamed x13, local copies, waits for them, and re-layouts  3.28 us
    pallas_call x1, Pallas kernels, per_device(): call(functools.partial(start_kernel, swap2), 'start', [vmem(), vmem(), vm...  2.5 us
    pallas_call x1, Pallas kernels, per_device(): call(forward_kernel, 'forward', [vmem(), vmem(), smem(), vmem(), vmem()],...  2.49 us
    pallas_call x1, Pallas kernels, per_device(): call(functools.partial(columns_kernel, swap2, fields, count), 'columns',...  1.97 us
  transfers between devices with their start and end apart: 6, of which 4 were waited for; matrix products, arithmetic and copies ran while one was open for 0% of the time, Pallas kernels for 19%

profile of v1, /device:TPU:0, one launch (start us, length us, event | category | flops | bytes accessed | tf_op | source)
XLA Modules:
  0.0 31.3 jit_solution(9873758806952425426)
XLA Ops:
  0.0 1.3 %copy.9 = f32[1,3,3]{2,1,0:T(4,128)} copy(f32[1,3,3]{2,0,1:T(1,128)} %param.9) | data formatting | bytes 72
  1.3 2.5 %start.1 = (f32[3,64,256]{2,1,0:T(8,128)}, f32[48,256]{1,0:T(8,128)}, f32[48,256]{1,0:T(8,128)}, f32[64,128]{1,0:T(8,128)}, f32[64,128]{1,0:T(8,128)}, /*index=5*/f32[6,64,256]{2,1,0:T(8,128)}) custom-call(f32[3,64,256]{2,1,0:T(8,128)} %bitcast.9, f32[3,64,256]{2,1,0:T(8,128)} %bitcast.15, f32[2,64,256]{2,1,0:T(8,128)} %bitcast.12, f32[3,3]{1,0:T(4,128)} %bitcast.17, ...), custom_call_target="tpu_custom_call" | custom-call | flops 16777216 | bytes 1048576 | tf_op jit(solution)/shard_map/start/pallas_call | solution.py:356
  3.8 3.0 %collective-permute-start.4 = (f32[6,64,256]{2,1,0:T(8,128)}, f32[6,64,256]{2,1,0:T(8,128)S(1)}, u32[]{:S(2)}, u32[]{:S(2)}) collective-permute-start(f32[6,64,256]{2,1,0:T(8,128)} %get-tuple-element.25), channel_id=1, source_target_pairs={{0,16},{16,0},{1,17},{17,1},{2,18},{18,2},{3,19},{19,3},{4,20},{20... | collective-permute-start | bytes 1179656 | tf_op jit(solution)/shard_map/ppermute | solution.py:39
  6.7 0.0 collective-permute-start
  6.7 1.6 %collective-permute-start.1 = (f32[48,256]{1,0:T(8,128)}, f32[48,256]{1,0:T(8,128)S(1)}, u32[]{:S(2)}, u32[]{:S(2)}) collective-permute-start(f32[48,256]{1,0:T(8,128)} %get-tuple-element.17), channel_id=1, source_target_pairs={{0,12},{4,8},{8,4},{12,0},{1,13},{5,9},{9,5},{13,1},{2,14},{6,10},... | collective-permute-start | bytes 147464 | tf_op jit(solution)/shard_map/ppermute | solution.py:32
  8.4 0.0 collective-permute-done.got_even
  8.4 0.0 copy-start.2
  8.4 2.1 %collective-permute-done.1.got_odd = f32[48,256]{1,0:T(8,128)S(1)} collective-permute-done((f32[48,256]{1,0:T(8,128)}, f32[48,256]{1,0:T(8,128)S(1)}, u32[]{:S(2)}, u32[]{:S(2)}) %collective-permute-start.1) | collective-permute-done | bytes 49184 | tf_op jit(solution)/shard_map/ppermute | solution.py:32
  10.5 0.0 copy-start.3
  10.5 0.0 copy-done.2
  10.5 0.6 %copy-done.3 = f32[48,256]{1,0:T(8,128)} copy-done((f32[48,256]{1,0:T(8,128)}, f32[48,256]{1,0:T(8,128)S(1)}, u32[]{:S(2)}) %copy-start.3) | copy-done | bytes 49176
  11.1 1.6 %rows.1 = (f32[11,8,256]{2,1,0:T(8,128)}, f32[72,128]{1,0:T(8,128)}, f32[72,128]{1,0:T(8,128)}) custom-call(f32[48,256]{1,0:T(8,128)} %copy-done.2, f32[48,256]{1,0:T(8,128)} %copy-done.3, f32[64,128]{1,0:T(8,128)} %get-tuple-element.18.col_low, f32[64,128]{1,0:T(8,128)} %get-tuple-element.19.col_high), custom_call_target="tpu_custom_call" | custom-call | flops 65536 | bytes 1048576 | tf_op jit(solution)/shard_map/rows/pallas_call | solution.py:366
  12.6 1.6 %collective-permute-start.2 = (f32[72,128]{1,0:T(8,128)}, f32[72,128]{1,0:T(8,128)S(1)}, u32[]{:S(2)}, u32[]{:S(2)}) collective-permute-start(f32[72,128]{1,0:T(8,128)} %get-tuple-element.21), channel_id=1, source_target_pairs={{0,1},{1,0},{2,3},{3,2},{4,5},{5,4},{6,7},{7,6},{8,9},{9,8},{10,11... | collective-permute-start | bytes 110600 | tf_op jit(solution)/shard_map/ppermute | solution.py:31
  14.2 2.5 %collective-permute-start.3 = (f32[72,128]{1,0:T(8,128)}, f32[72,128]{1,0:T(8,128)S(1)}, u32[]{:S(2)}, u32[]{:S(2)}) collective-permute-start(f32[72,128]{1,0:T(8,128)} %get-tuple-element.22), channel_id=1, source_target_pairs={{0,3},{1,2},{2,1},{3,0},{4,7},{5,6},{6,5},{7,4},{8,11},{9,10},{10,... | collective-permute-start | bytes 110600 | tf_op jit(solution)/shard_map/ppermute | solution.py:32
  16.7 0.3 %collective-permute-done.2.got_even = f32[72,128]{1,0:T(8,128)S(1)} collective-permute-done((f32[72,128]{1,0:T(8,128)}, f32[72,128]{1,0:T(8,128)S(1)}, u32[]{:S(2)}, u32[]{:S(2)}) %collective-permute-start.2) | collective-permute-done | bytes 36896 | tf_op jit(solution)/shard_map/ppermute | solution.py:31
  17.0 0.0 copy-start.4
  17.0 3.1 %collective-permute-done.3.got_odd = f32[72,128]{1,0:T(8,128)S(1)} collective-permute-done((f32[72,128]{1,0:T(8,128)}, f32[72,128]{1,0:T(8,128)S(1)}, u32[]{:S(2)}, u32[]{:S(2)}) %collective-permute-start.3) | collective-permute-done | bytes 36896 | tf_op jit(solution)/shard_map/ppermute | solution.py:32
  20.2 0.0 copy-start.5
  20.2 0.0 copy-done.4
  20.2 0.6 %copy-done.5 = f32[72,128]{1,0:T(8,128)} copy-done((f32[72,128]{1,0:T(8,128)}, f32[72,128]{1,0:T(8,128)S(1)}, u32[]{:S(2)}) %copy-start.5) | copy-done | bytes 36888
  20.8 2.0 %columns.1 = (f32[11,72,128]{2,1,0:T(8,128)}, f32[120,128]{1,0:T(8,128)}) custom-call(f32[72,128]{1,0:T(8,128)} %copy-done.4, f32[72,128]{1,0:T(8,128)} %copy-done.5, f32[11,8,256]{2,1,0:T(8,128)} %get-tuple-element.20.halo_rows), custom_call_target="tpu_custom_call" | custom-call | flops 65536 | bytes 1048576 | tf_op jit(solution)/shard_map/columns/pallas_call | solution.py:376
  22.8 0.5 %collective-permute-start.5 = (f32[120,128]{1,0:T(8,128)}, f32[120,128]{1,0:T(8,128)S(1)}, u32[]{:S(2)}, u32[]{:S(2)}) collective-permute-start(f32[120,128]{1,0:T(8,128)} %get-tuple-element.26), channel_id=1, source_target_pairs={{0,16},{16,0},{1,17},{17,1},{2,18},{18,2},{3,19},{19,3},{4,20},{20... | collective-permute-start | bytes 184328 | tf_op jit(solution)/shard_map/ppermute | solution.py:39
  23.3 2.5 %forward.1.fwd = f32[3,72,384]{2,1,0:T(8,128)} custom-call(f32[3,64,256]{2,1,0:T(8,128)} %bitcast.10, f32[2,64,256]{2,1,0:T(8,128)} %bitcast.13, f32[3,3]{1,0:T(4,128)} %bitcast.18, f32[11,8,256]{2,1,0:T(8,128)} %get-tuple-element.20.halo_rows, f32[11,72,128]{2,1,0:T(8,128)} %get-tuple-element.23.halo_cols), custom_call_target="tpu_custom_call" | custom-call | flops 16777216 | bytes 1048576 | tf_op jit(solution)/shard_map/forward/pallas_call | solution.py:385
  25.8 1.4 %collective-permute-done.5.ring_above.ring_below = f32[120,128]{1,0:T(8,128)S(1)} collective-permute-done((f32[120,128]{1,0:T(8,128)}, f32[120,128]{1,0:T(8,128)S(1)}, u32[]{:S(2)}, u32[]{:S(2)}) %collective-permute-start.5) | collective-permute-done | bytes 61472 | tf_op jit(solution)/shard_map/ppermute | solution.py:39
  27.2 0.0 copy-start.1
  27.2 0.0 collective-permute-done.4.above.below
  27.2 0.0 copy-start
  27.2 0.6 %copy-done.1 = f32[120,128]{1,0:T(8,128)} copy-done((f32[120,128]{1,0:T(8,128)}, f32[120,128]{1,0:T(8,128)S(1)}, u32[]{:S(2)}) %copy-start.1) | copy-done | bytes 61464
  27.8 0.2 copy-done
  28.0 3.3 %finish.1 = f32[3,64,256]{2,1,0:T(8,128)} custom-call(f32[3,72,384]{2,1,0:T(8,128)} %forward.1.fwd, f32[3,64,256]{2,1,0:T(8,128)} %bitcast.11, f32[3,64,256]{2,1,0:T(8,128)} %bitcast.16, f32[2,64,256]{2,1,0:T(8,128)} %bitcast.14, f32[3,3]{1,0:T(4,128)} %bitcast.19, f32[3,64,256]{2,1,0:T(8,128)} %get-tuple-element.24.hmap, ...), custom_call_target="tpu_custom_call" | custom-call | flops 33554432 | bytes 1048576 | tf_op jit(solution)/shard_map/finish/pallas_call | solution.py:393
Async XLA Ops:
  3.8 23.4 %collective-permute-start.4 = (f32[6,64,256]{2,1,0:T(8,128)}, f32[6,64,256]{2,1,0:T(8,128)S(1)}, u32[]{:S(2)}, u32[]{:S(2)}) collective-permute-start(f32[6,64,256]{2,1,0:T(8,128)} %get-tuple-element.25), channel_id=1, source_target_pairs={{0,16},{16,0},{1,17},{17,1},{2,18},{18,2},{3,19},{19,3},{4,20},{20... | collective-permute-start | bytes 1179656 | tf_op jit(solution)/shard_map/ppermute | solution.py:39
  6.7 1.6 %collective-permute-start = (f32[48,256]{1,0:T(8,128)}, f32[48,256]{1,0:T(8,128)S(1)}, u32[]{:S(2)}, u32[]{:S(2)}) collective-permute-start(f32[48,256]{1,0:T(8,128)} %get-tuple-element.16), channel_id=1, source_target_pairs={{0,4},{4,0},{8,12},{12,8},{1,5},{5,1},{9,13},{13,9},{2,6},{6,2},{1... | collective-permute-start | bytes 147464 | tf_op jit(solution)/shard_map/ppermute | solution.py:31
  6.7 3.7 %collective-permute-start.1 = (f32[48,256]{1,0:T(8,128)}, f32[48,256]{1,0:T(8,128)S(1)}, u32[]{:S(2)}, u32[]{:S(2)}) collective-permute-start(f32[48,256]{1,0:T(8,128)} %get-tuple-element.17), channel_id=1, source_target_pairs={{0,12},{4,8},{8,4},{12,0},{1,13},{5,9},{9,5},{13,1},{2,14},{6,10},... | collective-permute-start | bytes 147464 | tf_op jit(solution)/shard_map/ppermute | solution.py:32
  8.4 2.1 %copy-start.2 = (f32[48,256]{1,0:T(8,128)}, f32[48,256]{1,0:T(8,128)S(1)}, u32[]{:S(2)}) copy-start(f32[48,256]{1,0:T(8,128)S(1)} %collective-permute-done.got_even) | copy-start | bytes 147460
  10.5 0.6 %copy-start.3 = (f32[48,256]{1,0:T(8,128)}, f32[48,256]{1,0:T(8,128)S(1)}, u32[]{:S(2)}) copy-start(f32[48,256]{1,0:T(8,128)S(1)} %collective-permute-done.1.got_odd) | copy-start | bytes 147460
  12.6 4.4 %collective-permute-start.2 = (f32[72,128]{1,0:T(8,128)}, f32[72,128]{1,0:T(8,128)S(1)}, u32[]{:S(2)}, u32[]{:S(2)}) collective-permute-start(f32[72,128]{1,0:T(8,128)} %get-tuple-element.21), channel_id=1, source_target_pairs={{0,1},{1,0},{2,3},{3,2},{4,5},{5,4},{6,7},{7,6},{8,9},{9,8},{10,11... | collective-permute-start | bytes 110600 | tf_op jit(solution)/shard_map/ppermute | solution.py:31
  14.2 6.0 %collective-permute-start.3 = (f32[72,128]{1,0:T(8,128)}, f32[72,128]{1,0:T(8,128)S(1)}, u32[]{:S(2)}, u32[]{:S(2)}) collective-permute-start(f32[72,128]{1,0:T(8,128)} %get-tuple-element.22), channel_id=1, source_target_pairs={{0,3},{1,2},{2,1},{3,0},{4,7},{5,6},{6,5},{7,4},{8,11},{9,10},{10,... | collective-permute-start | bytes 110600 | tf_op jit(solution)/shard_map/ppermute | solution.py:32
  17.0 3.2 %copy-start.4 = (f32[72,128]{1,0:T(8,128)}, f32[72,128]{1,0:T(8,128)S(1)}, u32[]{:S(2)}) copy-start(f32[72,128]{1,0:T(8,128)S(1)} %collective-permute-done.2.got_even) | copy-start | bytes 110596
  20.2 0.6 %copy-start.5 = (f32[72,128]{1,0:T(8,128)}, f32[72,128]{1,0:T(8,128)S(1)}, u32[]{:S(2)}) copy-start(f32[72,128]{1,0:T(8,128)S(1)} %collective-permute-done.3.got_odd) | copy-start | bytes 110596
  22.8 4.4 %collective-permute-start.5 = (f32[120,128]{1,0:T(8,128)}, f32[120,128]{1,0:T(8,128)S(1)}, u32[]{:S(2)}, u32[]{:S(2)}) collective-permute-start(f32[120,128]{1,0:T(8,128)} %get-tuple-element.26), channel_id=1, source_target_pairs={{0,16},{16,0},{1,17},{17,1},{2,18},{18,2},{3,19},{19,3},{4,20},{20... | collective-permute-start | bytes 184328 | tf_op jit(solution)/shard_map/ppermute | solution.py:39
  27.2 0.6 %copy-start.1 = (f32[120,128]{1,0:T(8,128)}, f32[120,128]{1,0:T(8,128)S(1)}, u32[]{:S(2)}) copy-start(f32[120,128]{1,0:T(8,128)S(1)} %collective-permute-done.5.ring_above.ring_below) | copy-start | bytes 184324
  27.2 0.8 %copy-start = (f32[6,64,256]{2,1,0:T(8,128)}, f32[6,64,256]{2,1,0:T(8,128)S(1)}, u32[]{:S(2)}) copy-start(f32[6,64,256]{2,1,0:T(8,128)S(1)} %collective-permute-done.4.above.below) | copy-start | bytes 1179652

commit v2 on v1

--- a/solution.py
+++ b/solution.py
@@ -61,13 +61,27 @@
     return out
 
 
-def start_kernel(swap2, inc, wgt, wind, mix, cells, scale, hmap, row_even, row_odd, col_low, col_high, *bulk):
+def start_kernel(swap2, copies, *refs):
+    inc_far, wgt_far, wind_far, mix_far, cells_far, scale_far, inc, wgt, wind, hmap = refs[:10]
+    row_even, row_odd, col_low, col_high, mixrows = refs[10:15]
+    bulk = refs[15 : 15 + copies]
+    cells, scale, mix, sems = refs[15 + copies :]
+    moves = [
+        pltpu.make_async_copy(far, near, sems.at[i])
+        for i, (far, near) in enumerate(
+            [(cells_far, cells), (scale_far, scale), (inc_far, inc), (wind_far, wind), (wgt_far, wgt), (mix_far, mix)]
+        )
+    ]
+    for move in moves:
+        move.start()
     fields, rows, cols = inc.shape
     nobs = cells.shape[-1]
+    moves[0].wait()
     index = cells[...]
     row_hot = sub_iota((rows, nobs)) == index // cols
     col_hot = (sub_iota((cols, nobs)) == index % cols).astype(F32).astype(jnp.bfloat16)
     terms = []
+    moves[1].wait()
     for f in range(fields):
         rest = scale[f]
         for _ in range(3):
@@ -77,6 +91,8 @@
     sums = lax.dot_general(
         jnp.concatenate(terms, axis=0), col_hot, (((1,), (1,)), ((), ())), preferred_element_type=F32
     )
+    for move in moves[2:]:
+        move.wait()
     planes = [inc[f] for f in range(fields)] + [wind[0], wind[1]]
     for f in range(fields):
         base = 3 * f * rows
@@ -96,12 +112,14 @@
         last = jnp.where(upper, pltpu.roll(one[-8:], HALO, 0), two[-8:])
         row_even[pl.ds(8 * m, 8), :] = jnp.where(is_even, last, first)
         row_odd[pl.ds(8 * m, 8), :] = jnp.where(is_even, first, last)
-    mixrows = jnp.zeros((rows, cols), F32)
-    which = sub_iota((rows, cols))
+    which = sub_iota(mixrows.shape)
+    spread = jnp.zeros(mixrows.shape, F32)
     for f in range(fields):
         for g in range(fields):
-            mixrows = jnp.where(which == f * fields + g, mix[f, g], mixrows)
-    up = [wind[0], wind[1], mixrows]
+            spread = jnp.where(which == f * fields + g, mix[f, 0, g], spread)
+    mixrows[...] = spread
+    used = mixrows.shape[0]
+    up = [wind[0], wind[1], jnp.concatenate([spread[:, :cols], wgt[fields - 1, used:]], axis=0)]
     for f in range(fields):
         if swap2:
             sends_up = lax.axis_index("win") == 0
@@ -231,6 +249,10 @@
     return pltpu.roll(x, 1, 1)
 
 
+def mixing(spread, fields):
+    return lambda f, g: spread[f * fields + g : f * fields + g + 1]
+
+
 def blend(mix, field, f):
     total = None
     for g in range(len(field)):
@@ -262,19 +284,19 @@
     ]
 
 
-def forward_kernel(inc, wind, mix, halo_rows, halo_cols, fwd):
+def forward_kernel(inc, wind, mixrows, halo_rows, halo_cols, fwd):
     fields, rows, _ = inc.shape
     field = [extended(inc[f], halo_rows[f], halo_cols[f]) for f in range(fields)]
     u, v = [extended(wind[i], halo_rows[fields + i], halo_cols[fields + i]) for i in range(2)]
     clear = row_mask(rows, field[0].shape[1])
-    mixer = lambda f, g: mix[f, g]
+    mixer = mixing(mixrows[...], fields)
     field = [clear(x) for x in tangent(field, u, v, mixer)]
     field = tangent(field, u, v, mixer)
     for f in range(fields):
         fwd[f] = field[f]
 
 
-def finish_kernel(fwd, inc, wgt, wind, mix, hmap, halo_rows, halo_cols, above, below, ring_above, ring_below, out):
+def finish_kernel(fwd, inc, wgt, wind, mixrows, hmap, halo_rows, halo_cols, above, below, ring_above, ring_below, out):
     fields, rows, cols = inc.shape
     blocks = cols // LANES
     total = halo_cols.shape[1]
@@ -300,18 +322,15 @@
         h = extended(hmap[f], halo_rows[fields + 2 + f], halo_cols[fields + 2 + f])
         source.append(clear(h * x - jnp.where(has_later, later, 0.0)))
     u, v = [extended(wind[i], halo_rows[fields + i], halo_cols[fields + i]) for i in range(2)]
-    mixer = lambda f, g: mix[f, g]
+    mixer = mixing(mixrows[...], fields)
     back = [clear(x) for x in adjoint(source, u, v, mixer)]
     back = adjoint(back, u, v, mixer)
 
     has_earlier = here > 0
     prior = [clear(unpack(below, ring_below, f)) for f in range(fields)]
     u, v = [unpack(below, ring_below, fields + i) for i in range(2)]
-    mixrows = below[2 * fields - 1]
-
-    def prior_mix(f, g):
-        return mixrows[f * fields + g : f * fields + g + 1, 0:1]
-
+    spread = below[2 * fields - 1, :16]
+    prior_mix = mixing(jnp.concatenate([spread, spread[:, :LANES]], axis=1), fields)
     prior = [clear(x) for x in tangent(prior, u, v, prior_mix)]
     prior = tangent(prior, u, v, prior_mix)
     for f in range(fields):
@@ -323,14 +342,20 @@
     return pl.BlockSpec(memory_space=pltpu.VMEM)
 
 
-def smem():
-    return pl.BlockSpec(memory_space=pltpu.SMEM)
-
-
-def call(kernel, name, in_specs, shapes, flops):
+def hbm():
+    return pl.BlockSpec(memory_space=pltpu.HBM)
+
+
+def far(array):
+    return pltpu.with_memory_space_constraint(array, pltpu.HBM)
+
+
+def call(kernel, name, in_specs, shapes, flops, scratch=()):
     return pl.pallas_call(
         kernel,
         name=name,
+        scratch_shapes=scratch,
+        compiler_params=pltpu.CompilerParams(vmem_limit_bytes=8 << 20),
         out_shape=[jax.ShapeDtypeStruct(s, F32) for s in shapes],
         in_specs=in_specs,
         out_specs=[vmem()] * len(shapes),
@@ -342,7 +367,7 @@
     inc = increment[0]
     wgt = model_weight[0]
     wind = winds[0]
-    mix = reaction[0]
+    mix = reaction.transpose(1, 0, 2)
     fields, rows, cols = inc.shape
     nobs = obs_cells.shape[-1]
     cells = obs_cells.reshape(1, nobs)
@@ -353,13 +378,19 @@
     swap2 = lax.axis_size("win") == 2
     copies = 1 if swap2 else 2
 
-    hmap, row_even, row_odd, col_low, col_high, *bulk = call(
-        functools.partial(start_kernel, swap2),
+    tile = (fields, rows, cols)
+    inc, wgt, wind, hmap, row_even, row_odd, col_low, col_high, mixrows, *bulk = call(
+        functools.partial(start_kernel, swap2, copies),
         "start",
-        [vmem(), vmem(), vmem(), smem(), vmem(), vmem()],
-        [(fields, rows, cols)] + [(8 * pairs, cols)] * 2 + [(rows, LANES)] * 2 + [(2 * fields, rows, cols)] * copies,
+        [hbm()] * 6,
+        [tile, tile, (2, rows, cols), tile]
+        + [(8 * pairs, cols)] * 2
+        + [(rows, LANES)] * 2
+        + [(16, cols + LANES)]
+        + [(2 * fields, rows, cols)] * copies,
         1 << 24,
-    )(inc, wgt, wind, mix, cells, scale)
+        [pltpu.VMEM((1, nobs), jnp.int32), pltpu.VMEM((fields, 1, nobs), F32), pltpu.SMEM(mix.shape, F32), pltpu.SemaphoreType.DMA((6,))],
+    )(far(inc), far(wgt), far(wind), far(mix), far(cells), far(scale))
     got_even, got_odd = neighbour_swap(row_even, row_odd, "lat")
     above, below = window_swap(bulk[0], bulk[-1])
 
@@ -385,18 +416,18 @@
     (fwd,) = call(
         forward_kernel,
         "forward",
-        [vmem(), vmem(), smem(), vmem(), vmem()],
+        [vmem()] * 5,
         [(fields, tall, cols + LANES)],
         1 << 24,
-    )(inc, wind, mix, halo_rows, halo_cols)
+    )(inc, wind, mixrows, halo_rows, halo_cols)
 
     (out,) = call(
         finish_kernel,
         "finish",
-        [vmem()] * 4 + [smem()] + [vmem()] * 7,
+        [vmem()] * 12,
         [(fields, rows, cols)],
         1 << 25,
-    )(fwd, inc, wgt, wind, mix, hmap, halo_rows, halo_cols, above, below, ring_above, ring_below)
+    )(fwd, inc, wgt, wind, mixrows, hmap, halo_rows, halo_cols, above, below, ring_above, ring_below)
     return out[None]
 
 

time: 31.6 us -> 22.3 us (0.71)
  Pallas kernels: 11.8 us -> 4.42 us
  local copies, waits for them, and re-layouts: 3.28 us -> 0 us
  waiting for transfers between devices: 6.99 us -> 8.27 us
    pallas_call x3, Pallas kernels: 8.31 us -> 3.96 us  [the longest x1 1.7 us: per_device(): call(finish_kernel, 'finish', [vmem()] * 12, [(fields, rows, cols)], 1 <<...]
    unnamed x13 -> x0, local copies, waits for them, and re-layouts: 3.28 us -> none
    ppermute x2, waiting for transfers between devices: 1.41 us -> 3.11 us  [window_swap(): got = lax.ppermute(down, 'win', even_pairs(n))]
    pallas_call x1, Pallas kernels: 1.97 us -> 0.37 us  [per_device(): call(functools.partial(columns_kernel, swap2, fields, count), 'columns',...]
    pallas_call x1, Pallas kernels: 1.56 us -> 0.1 us  [per_device(): call(functools.partial(rows_kernel, count), 'rows', [vmem()] * 4, [(count...]
  transfers between devices with their start and end apart: 6 -> 6, of which waited for: 4 -> 4; matrix products, arithmetic and copies ran while one was open for 0% -> 0% of each run, Pallas kernels for 19% -> 5%
where the time goes in v2:
time: 22.3 us; the launch traced here: 22.1 us
  starting transfers between devices  9.38 us (42%)
  waiting for transfers between devices  8.27 us (37%)
  Pallas kernels  4.42 us (20%)
    ppermute x2, waiting for transfers between devices, neighbour_swap(): lax.ppermute(odd_msg, axis, odd_pairs(n))  5.03 us
    ppermute x2, starting transfers between devices, neighbour_swap(): lax.ppermute(odd_msg, axis, odd_pairs(n))  4.11 us
    ppermute x2, starting transfers between devices, window_swap(): got = lax.ppermute(down, 'win', even_pairs(n))  3.63 us
    ppermute x2, waiting for transfers between devices, window_swap(): got = lax.ppermute(down, 'win', even_pairs(n))  3.11 us
    pallas_call x1, Pallas kernels, per_device(): call(finish_kernel, 'finish', [vmem()] * 12, [(fields, rows, cols)], 1 <<...  1.7 us
    pallas_call x1, Pallas kernels, per_device(): call(functools.partial(start_kernel, swap2, copies), 'start', [hbm()] * 6...  1.68 us
    ppermute x2, starting transfers between devices, neighbour_swap(): lax.ppermute(even_msg, axis, even_pairs(n))  1.64 us
    pallas_call x1, Pallas kernels, per_device(): call(forward_kernel, 'forward', [vmem()] * 5, [(fields, tall, cols + LANE...  0.58 us
  transfers between devices with their start and end apart: 6, of which 4 were waited for; matrix products, arithmetic and copies ran while one was open for 0% of the time, Pallas kernels for 5%

profile of v2, /device:TPU:0, one launch (start us, length us, event | category | flops | bytes accessed | tf_op | source)
XLA Modules:
  0.0 22.1 jit_solution(8734725855490540372)
XLA Ops:
  0.0 1.7 %start.1 = (f32[3,64,256]{2,1,0:T(8,128)S(1)}, f32[3,64,256]{2,1,0:T(8,128)S(1)}, f32[2,64,256]{2,1,0:T(8,128)S(1)}, f32[3,64,256]{2,1,0:T(8,128)S(1)}, f32[48,2...) custom-call(f32[3,64,256]{2,1,0:T(8,128)} %bitcast.7, ...), custom_call_target="tpu_custom_call" | custom-call | flops 16777216 | bytes 1048576 | tf_op jit(solution)/shard_map/start/pallas_call | solution.py:382
  1.7 3.0 %collective-permute-start.4 = (f32[6,64,256]{2,1,0:T(8,128)S(1)}, f32[6,64,256]{2,1,0:T(8,128)S(1)}, u32[]{:S(2)}, u32[]{:S(2)}) collective-permute-start(f32[6,64,256]{2,1,0:T(8,128)S(1)} %get-tuple-element.33), channel_id=1, source_target_pairs={{0,16},{16,0},{1,17},{17,1},{2,18},{18,2},{3,19},{19,3},{4,20},{20... | collective-permute-start | bytes 1179656 | tf_op jit(solution)/shard_map/ppermute | solution.py:39
  4.7 0.0 collective-permute-start
  4.7 1.6 %collective-permute-start.1 = (f32[48,256]{1,0:T(8,128)S(1)}, f32[48,256]{1,0:T(8,128)S(1)}, u32[]{:S(2)}, u32[]{:S(2)}) collective-permute-start(f32[48,256]{1,0:T(8,128)S(1)} %get-tuple-element.24), channel_id=1, source_target_pairs={{0,12},{4,8},{8,4},{12,0},{1,13},{5,9},{9,5},{13,1},{2,14},{6,10},... | collective-permute-start | bytes 147464 | tf_op jit(solution)/shard_map/ppermute | solution.py:32
  6.4 0.0 collective-permute-done.got_even
  6.4 1.9 %collective-permute-done.1.got_odd = f32[48,256]{1,0:T(8,128)S(1)} collective-permute-done((f32[48,256]{1,0:T(8,128)S(1)}, f32[48,256]{1,0:T(8,128)S(1)}, u32[]{:S(2)}, u32[]{:S(2)}) %collective-permute-start.1) | collective-permute-done | bytes 49184 | tf_op jit(solution)/shard_map/ppermute | solution.py:32
  8.2 0.1 rows.1
  8.3 1.6 %collective-permute-start.2 = (f32[72,128]{1,0:T(8,128)S(1)}, f32[72,128]{1,0:T(8,128)S(1)}, u32[]{:S(2)}, u32[]{:S(2)}) collective-permute-start(f32[72,128]{1,0:T(8,128)S(1)} %get-tuple-element.28), channel_id=1, source_target_pairs={{0,1},{1,0},{2,3},{3,2},{4,5},{5,4},{6,7},{7,6},{8,9},{9,8},{10,11... | collective-permute-start | bytes 110600 | tf_op jit(solution)/shard_map/ppermute | solution.py:31
  10.0 2.5 %collective-permute-start.3 = (f32[72,128]{1,0:T(8,128)S(1)}, f32[72,128]{1,0:T(8,128)S(1)}, u32[]{:S(2)}, u32[]{:S(2)}) collective-permute-start(f32[72,128]{1,0:T(8,128)S(1)} %get-tuple-element.29), channel_id=1, source_target_pairs={{0,3},{1,2},{2,1},{3,0},{4,7},{5,6},{6,5},{7,4},{8,11},{9,10},{10,... | collective-permute-start | bytes 110600 | tf_op jit(solution)/shard_map/ppermute | solution.py:32
  12.4 0.1 collective-permute-done.2.got_even
  12.6 3.1 %collective-permute-done.3.got_odd = f32[72,128]{1,0:T(8,128)S(1)} collective-permute-done((f32[72,128]{1,0:T(8,128)S(1)}, f32[72,128]{1,0:T(8,128)S(1)}, u32[]{:S(2)}, u32[]{:S(2)}) %collective-permute-start.3) | collective-permute-done | bytes 36896 | tf_op jit(solution)/shard_map/ppermute | solution.py:32
  15.7 0.4 %columns.1 = (f32[11,72,128]{2,1,0:T(8,128)S(1)}, f32[120,128]{1,0:T(8,128)S(1)}) custom-call(f32[72,128]{1,0:T(8,128)S(1)} %collective-permute-done.2.got_even, f32[72,128]{1,0:T(8,128)S(1)} %collective-permute-done.3.got_odd, f32[11,8,256]{2,1,0:T(8,128)S(1)} %get-tuple-element.27.halo_rows), custom_call_target="tpu_custom_call" | custom-call | flops 65536 | bytes 1048576 | tf_op jit(solution)/shard_map/columns/pallas_call | solution.py:407
  16.1 0.6 %collective-permute-start.5 = (f32[120,128]{1,0:T(8,128)S(1)}, f32[120,128]{1,0:T(8,128)S(1)}, u32[]{:S(2)}, u32[]{:S(2)}) collective-permute-start(f32[120,128]{1,0:T(8,128)S(1)} %get-tuple-element.34), channel_id=1, source_target_pairs={{0,16},{16,0},{1,17},{17,1},{2,18},{18,2},{3,19},{19,3},{4,20},{20... | collective-permute-start | bytes 184328 | tf_op jit(solution)/shard_map/ppermute | solution.py:39
  16.7 0.6 %forward.1.fwd = f32[3,72,384]{2,1,0:T(8,128)S(1)} custom-call(f32[3,64,256]{2,1,0:T(8,128)S(1)} %get-tuple-element.20.inc, f32[2,64,256]{2,1,0:T(8,128)S(1)} %get-tuple-element.21.wind, f32[16,384]{1,0:T(8,128)S(1)} %get-tuple-element.22.mixrows, f32[11,8,256]{2,1,0:T(8,128)S(1)} %get-tuple-element.27.halo_rows, f32[11,72,128]{2,1,0:T(8,128)S(1)} %get-tuple-element.30.halo_cols), custom_call_target="tpu_custom_call" | custom-call | flops 16777216 | bytes 1048576 | tf_op jit(solution)/shard_map/forward/pallas_call | solution.py:416
  17.3 3.1 %collective-permute-done.5.ring_above.ring_below = f32[120,128]{1,0:T(8,128)S(1)} collective-permute-done((f32[120,128]{1,0:T(8,128)S(1)}, f32[120,128]{1,0:T(8,128)S(1)}, u32[]{:S(2)}, u32[]{:S(2)}) %collective-permute-start.5) | collective-permute-done | bytes 61472 | tf_op jit(solution)/shard_map/ppermute | solution.py:39
  20.4 0.0 collective-permute-done.4.above.below
  20.4 1.7 %finish.1 = f32[3,64,256]{2,1,0:T(8,128)} custom-call(f32[3,72,384]{2,1,0:T(8,128)S(1)} %forward.1.fwd, f32[3,64,256]{2,1,0:T(8,128)S(1)} %get-tuple-element.20.inc, f32[3,64,256]{2,1,0:T(8,128)S(1)} %get-tuple-element.31.wgt, f32[2,64,256]{2,1,0:T(8,128)S(1)} %get-tuple-element.21.wind, f32[16,384]{1,0:T(8,128)S(1)} %get-tuple-element.22.mixrows, ...), custom_call_target="tpu_custom_call" | custom-call | flops 33554432 | bytes 1048576 | tf_op jit(solution)/shard_map/finish/pallas_call | solution.py:424
Async XLA Ops:
  1.7 18.7 %collective-permute-start.4 = (f32[6,64,256]{2,1,0:T(8,128)S(1)}, f32[6,64,256]{2,1,0:T(8,128)S(1)}, u32[]{:S(2)}, u32[]{:S(2)}) collective-permute-start(f32[6,64,256]{2,1,0:T(8,128)S(1)} %get-tuple-element.33), channel_id=1, source_target_pairs={{0,16},{16,0},{1,17},{17,1},{2,18},{18,2},{3,19},{19,3},{4,20},{20... | collective-permute-start | bytes 1179656 | tf_op jit(solution)/shard_map/ppermute | solution.py:39
  4.7 1.6 %collective-permute-start = (f32[48,256]{1,0:T(8,128)S(1)}, f32[48,256]{1,0:T(8,128)S(1)}, u32[]{:S(2)}, u32[]{:S(2)}) collective-permute-start(f32[48,256]{1,0:T(8,128)S(1)} %get-tuple-element.23), channel_id=1, source_target_pairs={{0,4},{4,0},{8,12},{12,8},{1,5},{5,1},{9,13},{13,9},{2,6},{6,2},{1... | collective-permute-start | bytes 147464 | tf_op jit(solution)/shard_map/ppermute | solution.py:31
  4.7 3.5 %collective-permute-start.1 = (f32[48,256]{1,0:T(8,128)S(1)}, f32[48,256]{1,0:T(8,128)S(1)}, u32[]{:S(2)}, u32[]{:S(2)}) collective-permute-start(f32[48,256]{1,0:T(8,128)S(1)} %get-tuple-element.24), channel_id=1, source_target_pairs={{0,12},{4,8},{8,4},{12,0},{1,13},{5,9},{9,5},{13,1},{2,14},{6,10},... | collective-permute-start | bytes 147464 | tf_op jit(solution)/shard_map/ppermute | solution.py:32
  8.3 4.2 %collective-permute-start.2 = (f32[72,128]{1,0:T(8,128)S(1)}, f32[72,128]{1,0:T(8,128)S(1)}, u32[]{:S(2)}, u32[]{:S(2)}) collective-permute-start(f32[72,128]{1,0:T(8,128)S(1)} %get-tuple-element.28), channel_id=1, source_target_pairs={{0,1},{1,0},{2,3},{3,2},{4,5},{5,4},{6,7},{7,6},{8,9},{9,8},{10,11... | collective-permute-start | bytes 110600 | tf_op jit(solution)/shard_map/ppermute | solution.py:31
  10.0 5.8 %collective-permute-start.3 = (f32[72,128]{1,0:T(8,128)S(1)}, f32[72,128]{1,0:T(8,128)S(1)}, u32[]{:S(2)}, u32[]{:S(2)}) collective-permute-start(f32[72,128]{1,0:T(8,128)S(1)} %get-tuple-element.29), channel_id=1, source_target_pairs={{0,3},{1,2},{2,1},{3,0},{4,7},{5,6},{6,5},{7,4},{8,11},{9,10},{10,... | collective-permute-start | bytes 110600 | tf_op jit(solution)/shard_map/ppermute | solution.py:32
  16.1 4.3 %collective-permute-start.5 = (f32[120,128]{1,0:T(8,128)S(1)}, f32[120,128]{1,0:T(8,128)S(1)}, u32[]{:S(2)}, u32[]{:S(2)}) collective-permute-start(f32[120,128]{1,0:T(8,128)S(1)} %get-tuple-element.34), channel_id=1, source_target_pairs={{0,16},{16,0},{1,17},{17,1},{2,18},{18,2},{3,19},{19,3},{4,20},{20... | collective-permute-start | bytes 184328 | tf_op jit(solution)/shard_map/ppermute | solution.py:39

commit v3 on v0

v3 whole, which is shorter than its diff:
```python
import functools

import jax
import jax.numpy as jnp
from jax import lax
from jax.experimental import pallas as pl
from jax.experimental.pallas import tpu as pltpu
from jax.sharding import PartitionSpec as P


DIFFUSION = 0.15
HALO = 4
RIM = 2
LANES = 128
F32 = jnp.float32


def even_pairs(n):
    return [(i, i ^ 1) for i in range(n)]


def odd_pairs(n):
    return [(i, (i + 1 if i % 2 else i - 1) % n) for i in range(n)]


def ring(n, step):
    return [(i, (i + step) % n) for i in range(n)]


def neighbour_swap(even_msg, odd_msg, axis):
    n = lax.axis_size(axis)
    from_even = lax.ppermute(even_msg, axis, even_pairs(n))
    from_odd = lax.ppermute(odd_msg, axis, odd_pairs(n))
    return from_even, from_odd


def window_swap(down, up):
    n = lax.axis_size("win")
    if n == 2:
        got = lax.ppermute(down, "win", even_pairs(n))
        return got, got
    return lax.ppermute(down, "win", ring(n, -1)), lax.ppermute(up, "win", ring(n, 1))


def sub_iota(shape):
    return lax.broadcasted_iota(jnp.int32, shape, len(shape) - 2)


def lane_iota(shape):
    return lax.broadcasted_iota(jnp.int32, shape, len(shape) - 1)


def turn(x, shift, axis):
    shift %= x.shape[axis]
    return pltpu.roll(x, shift, axis) if shift else x


def axis_even(axis):
    return lax.axis_index(axis) % 2 == 0


class Layout:
    def __init__(self, fields, copies):
        self.fields, self.copies = fields, copies
        self.own = 2 + 2 * fields
        self.packet = 2 * fields
        self.depths = [HALO] * (fields + 2) + [RIM] * (fields + self.packet * copies)
        self.count = len(self.depths)
        self.starts = [sum(self.depths[:j]) for j in range(self.count)]
        self.used = sum(self.depths)
        self.row_blocks = -(-self.used // 8)

    def groups(self, blocks, width):
        per = -(-blocks // (LANES // width))
        return -(-blocks // per), per


def squeeze_lanes(wide, width, lay):
    blocks = wide.shape[0] // 8
    groups, per = lay.groups(blocks, width)
    lane = lane_iota((8, LANES))
    out = []
    for i in range(per):
        block = None
        for g in range(groups):
            if g * per + i < blocks:
                part = turn(wide[8 * (g * per + i) : 8 * (g * per + i) + 8], width * g, 1)
                block = part if block is None else jnp.where(lane >= width * g, part, block)
        out.append(block)
    return out


def spread_lanes(tight, blocks, width, lay):
    _, per = lay.groups(blocks, width)
    out = []
    for b in range(blocks):
        g, i = b // per, b % per
        out.append(turn(tight[i], -width * g, 1))
    return jnp.concatenate(out, axis=0)


def pack_rows(pieces, blocks):
    out = [None] * blocks
    for block, first, at, depth in pieces:
        b, s = at // 8, at % 8
        moved = turn(block, s - first, 0)
        sub = sub_iota(moved.shape)
        out[b] = moved if out[b] is None else jnp.where((sub >= s) & (sub < s + depth), moved, out[b])
    return out


def pack_lanes(pieces, out=None):
    for block, first, at, depth in pieces:
        moved = turn(block, at - first, 1)
        lane = lane_iota(moved.shape)
        out = moved if out is None else jnp.where((lane >= at) & (lane < at + depth), moved, out)
    return out


def load_kernel(swap2, copies, *refs):
    inc_far, wgt_far, wind_far, mix_far, cells_far, scale_far = refs[:6]
    inc, wgt, wind, cells, scale, mixrows = refs[6:12]
    bulk = refs[12 : 12 + copies]
    strips = refs[12 + copies : 12 + 2 * copies]
    mix, sems = refs[12 + 2 * copies :]
    fields, rows, cols = inc.shape
    lay = Layout(fields, copies)
    sends_up = lax.axis_index("win") == 0
    moves = [
        pltpu.make_async_copy(src, dst, sems.at[i])
        for i, (src, dst) in enumerate(
            [
                (inc_far, inc),
                (wgt_far, wgt),
                (wind_far, wind),
                (mix_far, mix),
                (cells_far, cells),
                (scale_far, scale),
                (inc_far, bulk[0].at[pl.ds(0, fields)]),
            ]
        )
    ]
    to_down = pltpu.make_async_copy(wgt_far, bulk[0].at[pl.ds(fields, fields)], sems.at[7])
    to_up = pltpu.make_async_copy(wind_far, bulk[-1].at[pl.ds(fields, 2)], sems.at[8])
    for move in moves:
        move.start()
    if swap2:

        @pl.when(sends_up)
        def _():
            to_up.start()

        @pl.when(jnp.logical_not(sends_up))
        def _():
            to_down.start()

    else:
        moves.append(pltpu.make_async_copy(inc_far, bulk[1].at[pl.ds(0, fields)], sems.at[9]))
        moves[-1].start()
        to_up.start()
        to_down.start()
    for move in moves[:4]:
        move.wait()

    first = [inc[f] for f in range(fields)]
    down = first + [wgt[f] for f in range(fields)]
    up = first + [wind[0], wind[1]] + [wind[1]] * (fields - 2)

    def choose(a, b):
        return jnp.where(sends_up, a, b) if swap2 else b

    for k, ref in enumerate(strips):
        planes = [choose(u, d) for u, d in zip(up, down)] if k == 0 else up
        pieces = []
        for j, x in enumerate(planes):
            pieces.append((x[:8], 0, 4 * j, RIM))
            pieces.append((x[-8:], 8 - RIM, 4 * j + 2, RIM))
        blocks = pack_rows(pieces, -(-4 * lay.packet // 8))
        halves = cols // LANES
        for m, block in enumerate(blocks):
            for h in range(halves):
                ref[pl.ds(8 * (m * halves + h), 8), :] = block[:, h * LANES : (h + 1) * LANES]
        pieces = []
        for j, x in enumerate(planes):
            pieces.append((x[:, :LANES], 0, 4 * j, RIM))
            pieces.append((x[:, -LANES:], LANES - RIM, 4 * j + 2, RIM))
        for m, block in enumerate(squeeze_lanes(pack_lanes(pieces), 4 * lay.packet, lay)):
            ref[pl.ds(8 * (len(blocks) * halves + m), 8), :] = block

    which = sub_iota(mixrows.shape)
    spread = jnp.zeros(mixrows.shape, F32)
    for f in range(fields):
        for g in range(fields):
            spread = jnp.where(which == f * fields + g, mix[f, 0, g], spread)
    mixrows[...] = spread

    def finish_up():
        to_up.wait()
        used = mixrows.shape[0]
        bulk[-1][2 * fields - 1, pl.ds(0, used), :] = spread[:, :cols]
        bulk[-1][2 * fields - 1, pl.ds(used, rows - used), :] = jnp.zeros((rows - used, cols), F32)

    if swap2:

        @pl.when(sends_up)
        def _():
            finish_up()

        @pl.when(jnp.logical_not(sends_up))
        def _():
            to_down.wait()

    else:
        to_down.wait()
        finish_up()
    for move in moves[4:]:
        move.wait()


def own_kernel(copies, inc, wind, cells, scale, hmap, row_first, row_last, col_low, col_high):
    fields, rows, cols = inc.shape
    lay = Layout(fields, copies)
    nobs = cells.shape[-1]
    index = cells[...]
    row_hot = sub_iota((rows, nobs)) == index // cols
    col_hot = (sub_iota((cols, nobs)) == index % cols).astype(F32).astype(jnp.bfloat16)
    terms = []
    for f in range(fields):
        rest = scale[f]
        for _ in range(3):
            part = rest.astype(jnp.bfloat16)
            rest = rest - part.astype(F32)
            terms.append(jnp.where(row_hot, part.astype(F32), 0.0).astype(jnp.bfloat16))
    sums = lax.dot_general(
        jnp.concatenate(terms, axis=0), col_hot, (((1,), (1,)), ((), ())), preferred_element_type=F32
    )
    planes = [inc[f] for f in range(fields)] + [wind[0], wind[1]]
    for f in range(fields):
        base = 3 * f * rows
        value = sums[base : base + rows] + (
            sums[base + rows : base + 2 * rows] + sums[base + 2 * rows : base + 3 * rows]
        )
        hmap[f] = value
        planes.append(value)
    where = list(zip(planes, lay.starts, lay.depths))
    first = pack_rows([(x[:8], 0, at, d) for x, at, d in where], lay.row_blocks)
    last = pack_rows([(x[-8:], 8 - d, at, d) for x, at, d in where], lay.row_blocks)
    for m in range(lay.row_blocks):
        blank = jnp.zeros((8, cols), F32)
        row_first[pl.ds(8 * m, 8), :] = blank if first[m] is None else first[m]
        row_last[pl.ds(8 * m, 8), :] = blank if last[m] is None else last[m]
    col_low[...] = pack_lanes([(x[:, :LANES], 0, at, d) for x, at, d in where])
    col_high[...] = pack_lanes([(x[:, -LANES:], LANES - d, at, d) for x, at, d in where])


def join_kernel(fields, copies, *refs):
    row_first, row_last, col_low, col_high = refs[:4]
    strips = refs[4 : 4 + copies]
    row_even, row_odd, low_out, high_out = refs[4 + copies :]
    lay = Layout(fields, copies)
    rows, cols = col_low.shape[0], row_first.shape[1]
    halves = cols // LANES
    strip_blocks = -(-4 * lay.packet // 8)
    first_pieces, last_pieces, low_pieces, high_pieces = [], [], [], []
    for k, ref in enumerate(strips):
        blocks = [
            jnp.concatenate([ref[pl.ds(8 * (m * halves + h), 8), :] for h in range(halves)], axis=1)
            for m in range(strip_blocks)
        ]
        _, per = lay.groups(rows // 8, 4 * lay.packet)
        base = 8 * strip_blocks * halves
        tight = [ref[pl.ds(base + 8 * i, 8), :] for i in range(per)]
        wide = spread_lanes(tight, rows // 8, 4 * lay.packet, lay)
        for j in range(lay.packet):
            at = lay.starts[lay.own + k * lay.packet + j]
            first_pieces.append((blocks[4 * j // 8], 4 * j % 8, at, RIM))
            last_pieces.append((blocks[4 * j // 8], 4 * j % 8 + 2, at, RIM))
            low_pieces.append((wide, 4 * j, at, RIM))
            high_pieces.append((wide, 4 * j + 2, at, RIM))
    is_even = axis_even("lat")
    own_used = lay.starts[lay.own]
    first = pack_rows(first_pieces, lay.row_blocks)
    last = pack_rows(last_pieces, lay.row_blocks)
    for m in range(lay.row_blocks):
        a, b = row_first[pl.ds(8 * m, 8), :], row_last[pl.ds(8 * m, 8), :]
        if first[m] is not None:
            other = sub_iota(a.shape) + 8 * m >= own_used
            a, b = jnp.where(other, first[m], a), jnp.where(other, last[m], b)
        row_even[pl.ds(8 * m, 8), :] = jnp.where(is_even, b, a)
        row_odd[pl.ds(8 * m, 8), :] = jnp.where(is_even, a, b)
    low_out[...] = pack_lanes(low_pieces, col_low[...])
    high_out[...] = pack_lanes(high_pieces, col_high[...])


def lat_inside(width):
    here = lax.axis_index("lat")
    upper = sub_iota((8, width)) < HALO
    from_high = (here < lax.axis_size("lat") - 1).astype(jnp.int32)
    from_low = (here > 0).astype(jnp.int32)
    return jnp.where(upper, from_high, from_low) > 0


def rows_kernel(fields, copies, got_even, got_odd, col_low, col_high, halo_rows, msg_even, msg_odd):
    lay = Layout(fields, copies)
    cols = got_even.shape[-1]
    is_even = axis_even("lat")
    inside = lat_inside(cols)
    sub = sub_iota((8, cols))
    high, low = [], []
    for m in range(lay.row_blocks):
        a = got_even[pl.ds(8 * m, 8), :]
        b = got_odd[pl.ds(8 * m, 8), :]
        high.append(jnp.where(is_even, a, b))
        low.append(jnp.where(is_even, b, a))
    blocks = []
    for j, (at, d) in enumerate(zip(lay.starts, lay.depths)):
        above = turn(high[at // 8], -(at % 8), 0)
        below = turn(low[at // 8], 8 - d - at % 8, 0)
        block = jnp.where(sub < d, above, jnp.where(sub >= 8 - d, below, 0.0))
        block = jnp.where(inside, block, 0.0)
        halo_rows[j] = block
        blocks.append(block)
    where = list(zip(blocks, lay.starts, lay.depths))
    low_tail = pack_lanes([(x[:, :LANES], 0, at, d) for x, at, d in where])
    high_tail = pack_lanes([(x[:, -LANES:], LANES - d, at, d) for x, at, d in where])
    low_all = squeeze_lanes(jnp.concatenate([col_low[...], low_tail], axis=0), lay.used, lay)
    high_all = squeeze_lanes(jnp.concatenate([col_high[...], high_tail], axis=0), lay.used, lay)
    lon_even = axis_even("lon")
    for m, (a, b) in enumerate(zip(low_all, high_all)):
        msg_even[pl.ds(8 * m, 8), :] = jnp.where(lon_even, b, a)
        msg_odd[pl.ds(8 * m, 8), :] = jnp.where(lon_even, a, b)


def row_mask(rows, width):
    inside = lat_inside(width)

    def clear(field):
        return jnp.concatenate([field[:rows], jnp.where(inside, field[rows:], 0.0)], axis=0)

    return clear


def north(x):
    return pltpu.roll(x, x.shape[0] - 1, 0)


def south(x):
    return pltpu.roll(x, 1, 0)


def east_of(x):
    return pltpu.roll(x, x.shape[1] - 1, 1)


def west_of(x):
    return pltpu.roll(x, 1, 1)


def mixing(spread, fields):
    return lambda f, g: spread[f * fields + g : f * fields + g + 1]


def blend(mix, field, f):
    total = None
    for g in range(len(field)):
        factor = mix(f, g)
        if f == g:
            factor = factor + (1.0 - 4.0 * DIFFUSION)
        term = factor * field[g]
        total = term if total is None else total + term
    return total


def tangent(field, u, v, mix):
    kn, ks, ke, kw = DIFFUSION - v, DIFFUSION + v, DIFFUSION - u, DIFFUSION + u
    return [
        blend(mix, field, f)
        + (kn * north(x) + ks * south(x))
        + (ke * east_of(x) + kw * west_of(x))
        for f, x in enumerate(field)
    ]


def adjoint(field, u, v, mix):
    kn, ks, ke, kw = DIFFUSION + v, DIFFUSION - v, DIFFUSION + u, DIFFUSION - u
    return [
        blend(lambda a, b: mix(b, a), field, f)
        + (north(kn * x) + south(ks * x))
        + (east_of(ke * x) + west_of(kw * x))
        for f, x in enumerate(field)
    ]


def product(own, above, below, wgt, mix, prior_mix, fields, rows):
    clear = row_mask(rows, own[0].shape[1])
    here = lax.axis_index("win")
    has_later = here < lax.axis_size("win") - 1
    has_earlier = here > 0
    inc, wind, hmap = own[:fields], own[fields : fields + 2], own[fields + 2 :]
    fwd = [clear(x) for x in tangent(inc, *wind, mix)]
    fwd = tangent(fwd, *wind, mix)
    source = []
    for f in range(fields):
        later = above[fields + f] * (above[f] - fwd[f])
        source.append(clear(hmap[f] * fwd[f] - jnp.where(has_later, later, 0.0)))
    back = [clear(x) for x in adjoint(source, *wind, mix)]
    back = adjoint(back, *wind, mix)
    prior_wind = below[fields : fields + 2]
    prior = [clear(x) for x in tangent(below[:fields], *prior_wind, prior_mix)]
    prior = tangent(prior, *prior_wind, prior_mix)
    return [
        wgt[f] * (inc[f][:rows] - jnp.where(has_earlier, prior[f][:rows], 0.0)) + back[f][:rows]
        for f in range(fields)
    ]


EDGE = 12


def edge_lanes(block_low, block_high):
    low = turn(block_low, HALO, 1)
    high = turn(block_high, HALO + 2 * EDGE, 1)
    return jnp.where(lane_iota(low.shape) < HALO + EDGE, low, high)


def inner_kernel(copies, inc, wgt, wind, hmap, mixrows, halo_rows, *refs):
    bulk = refs[:copies]
    part, edges, wgt_edges, prior_rows = refs[copies:]
    fields, rows, cols = inc.shape
    lay = Layout(fields, copies)
    tiles = [inc[f] for f in range(fields)] + [wind[0], wind[1]] + [hmap[f] for f in range(fields)]
    for ref in bulk:
        tiles += [ref[j] for j in range(lay.packet)]
    planes = []
    for j, tile in enumerate(tiles):
        planes.append(jnp.concatenate([tile, halo_rows[j]], axis=0))
        edges[j] = edge_lanes(planes[-1][:, :LANES], planes[-1][:, -LANES:])
    for f in range(fields):
        wgt_edges[f] = edge_lanes(wgt[f, :, :LANES], wgt[f, :, cols - LANES :])
    above = planes[lay.own : lay.own + lay.packet]
    below = planes[-lay.packet :]
    spread = bulk[-1][2 * fields - 1, :16]
    prior_rows[...] = spread[:, :LANES]
    mix = mixing(mixrows[:, :cols], fields)
    result = product(planes[: lay.own], above, below, wgt, mix, mixing(spread, fields), fields, rows)
    for f in range(fields):
        part[f] = result[f]


def edge_kernel(copies, got_even, got_odd, edges, wgt_edges, part, mixrows, prior_rows, out):
    fields, rows, cols = part.shape
    lay = Layout(fields, copies)
    blocks = rows // 8 + 1
    _, per = lay.groups(blocks, lay.used)
    lon_even = axis_even("lon")
    even = [got_even[pl.ds(8 * i, 8), :] for i in range(per)]
    odd = [got_odd[pl.ds(8 * i, 8), :] for i in range(per)]
    east = spread_lanes([jnp.where(lon_even, a, b) for a, b in zip(even, odd)], blocks, lay.used, lay)
    west = spread_lanes([jnp.where(lon_even, b, a) for a, b in zip(even, odd)], blocks, lay.used, lay)
    lane = lane_iota(east.shape)
    end = HALO + 2 * EDGE
    planes = []
    for j, (at, d) in enumerate(zip(lay.starts, lay.depths)):
        left = turn(west, HALO - d - at, 1)
        right = turn(east, end - at, 1)
        planes.append(
            jnp.where(lane < HALO, left, jnp.where((lane >= end) & (lane < end + d), right, edges[j]))
        )
    above = planes[lay.own : lay.own + lay.packet]
    below = planes[-lay.packet :]
    mix = mixing(mixrows[:, :LANES], fields)
    result = product(
        planes[: lay.own], above, below, wgt_edges, mix, mixing(prior_rows[...], fields), fields, rows
    )
    lane = lane_iota((rows, LANES))
    for f in range(fields):
        low = turn(result[f], -HALO, 1)
        high = turn(result[f], -(HALO + 2 * EDGE), 1)
        whole = part[f]
        if cols == LANES:
            out[f] = jnp.where(lane < HALO, low, jnp.where(lane >= LANES - HALO, high, whole))
        else:
            out[f, :, pl.ds(0, LANES)] = jnp.where(lane < HALO, low, whole[:, :LANES])
            for h in range(1, cols // LANES - 1):
                out[f, :, pl.ds(h * LANES, LANES)] = whole[:, h * LANES : (h + 1) * LANES]
            out[f, :, pl.ds(cols - LANES, LANES)] = jnp.where(lane >= LANES - HALO, high, whole[:, -LANES:])


def vmem():
    return pl.BlockSpec(memory_space=pltpu.VMEM)


def hbm():
    return pl.BlockSpec(memory_space=pltpu.HBM)


def far(array):
    return pltpu.with_memory_space_constraint(array, pltpu.HBM)


def call(kernel, in_specs, shapes, flops, scratch=()):
    return pl.pallas_call(
        kernel,
        scratch_shapes=scratch,
        compiler_params=pltpu.CompilerParams(vmem_limit_bytes=VMEM_LIMIT),
        out_shape=[s if isinstance(s, jax.ShapeDtypeStruct) else jax.ShapeDtypeStruct(s, F32) for s in shapes],
        in_specs=in_specs,
        out_specs=[vmem()] * len(shapes),
        cost_estimate=pl.CostEstimate(flops=flops, bytes_accessed=1 << 20, transcendentals=0),
    )


VMEM_LIMIT = 12 << 20


def per_device(increment, model_weight, winds, reaction, obs_cells, obs_weight):
    inc = increment[0]
    wgt = model_weight[0]
    wind = winds[0]
    mix = reaction.transpose(1, 0, 2)
    fields, rows, cols = inc.shape
    nobs = obs_cells.shape[-1]
    cells = obs_cells.reshape(1, nobs)
    scale = obs_weight.reshape(fields, 1, nobs)
    tall = rows + 2 * HALO
    swap2 = lax.axis_size("win") == 2
    copies = 1 if swap2 else 2
    lay = Layout(fields, copies)
    tile = (fields, rows, cols)
    packet = (lay.packet, rows, cols)
    strip_rows = 8 * (-(-4 * lay.packet // 8) * (cols // LANES) + lay.groups(rows // 8, 4 * lay.packet)[1])
    row_msg = (8 * lay.row_blocks, cols)
    col_msg = (8 * lay.groups(tall // 8, lay.used)[1], LANES)

    inc, wgt, wind, cells, scale, mixrows, *rest = call(
        functools.partial(load_kernel, swap2, copies),
        [hbm()] * 6,
        [tile, tile, wind.shape, jax.ShapeDtypeStruct(cells.shape, jnp.int32), scale.shape, (16, cols)]
        + [packet] * copies
        + [(strip_rows, LANES)] * copies,
        1 << 20,
        [pltpu.SMEM(mix.shape, F32), pltpu.SemaphoreType.DMA((10,))],
    )(far(inc), far(wgt), far(wind), far(mix), far(cells), far(scale))
    bulk, strips = rest[:copies], rest[copies:]
    strips = window_swap(strips[0], strips[-1])[:copies]
    bulk = window_swap(bulk[0], bulk[-1])[:copies]

    hmap, row_first, row_last, col_low, col_high = call(
        functools.partial(own_kernel, copies),
        [vmem()] * 4,
        [tile, row_msg, row_msg, (rows, LANES), (rows, LANES)],
        1 << 29,
    )(inc, wind, cells, scale)

    row_even, row_odd, col_low, col_high = call(
        functools.partial(join_kernel, fields, copies),
        [vmem()] * (4 + copies),
        [row_msg, row_msg, (rows, LANES), (rows, LANES)],
        1 << 16,
    )(row_first, row_last, col_low, col_high, *strips)
    got_even, got_odd = neighbour_swap(row_even, row_odd, "lat")

    halo_rows, msg_even, msg_odd = call(
        functools.partial(rows_kernel, fields, copies), [vmem()] * 4, [(lay.count, 8, cols), col_msg, col_msg], 1 << 16
    )(got_even, got_odd, col_low, col_high)
    got_even, got_odd = neighbour_swap(msg_even, msg_odd, "lon")

    part, edges, wgt_edges, prior_rows = call(
        functools.partial(inner_kernel, copies),
        [vmem()] * (6 + copies),
        [tile, (lay.count, tall, LANES), (fields, rows, LANES), (16, LANES)],
        1 << 29,
    )(inc, wgt, wind, hmap, mixrows, halo_rows, *bulk)

    (out,) = call(
        functools.partial(edge_kernel, copies), [vmem()] * 7, [tile], 1 << 25
    )(got_even, got_odd, edges, wgt_edges, part, mixrows, prior_rows)
    return out[None]


def solution(mesh):
    in_specs = (
        P("win", None, "lat", "lon"),
        P("win", None, "lat", "lon"),
        P("win", None, "lat", "lon"),
        P("win", None, None),
        P("win", "lat", "lon", None),
        P("win", None, "lat", "lon", None),
    )
    out_specs = P("win", None, "lat", "lon")

    return jax.shard_map(per_device, mesh=mesh, in_specs=in_specs, out_specs=out_specs, check_vma=False)
```

time: 76.9 us -> 27.3 us (0.36)
  other arithmetic: 24.4 us -> 0 us
  local copies, waits for them, and re-layouts: 14.1 us -> 0 us
  starting transfers between devices: 22.7 us -> 9.31 us
  Pallas kernels: 0 us -> 5.42 us
  waiting for transfers between devices: 14.9 us -> 12.4 us
    scatter-add x1 -> x0, other arithmetic: 16.1 us -> none  [per_device(): placed = jnp.zeros_like(flat).at[:, cells].add(obs_scale * picked)]
    ppermute x14 -> x6, starting transfers between devices: 22.7 us -> 9.31 us  [the longest x2 4.35 us: neighbour_swap(): from_odd = lax.ppermute(odd_msg, axis, odd_pairs(n))]
    pallas_call x0 -> x6, Pallas kernels: none -> 5.42 us  [the longest x1 1.62 us: per_device(): call(functools.partial(edge_kernel, copies), [vmem()] * 7, [tile], 1 << 25)]
    reshape x1 -> x0, local copies, waits for them, and re-layouts: 5.23 us -> none  [per_device(): observed = placed.reshape(forward.shape)]
    add x1 -> x0, local copies, waits for them, and re-layouts: 4.63 us -> none  [tangent_core(): return clear_rims(result + mixing(mixer, center))]
    select_n x4 -> x0, other arithmetic: 3.33 us -> none  [the longest x3 2.64 us: clear_rims(): return jnp.where(inside[None, :, None], extended, 0.0)]
    ppermute x14 -> x6, waiting for transfers between devices: 14.9 us -> 12.4 us  [the longest x2 9.14 us: window_swap(): got = lax.ppermute(down, 'win', even_pairs(n))]
    slice x10 -> x0, local copies, waits for them, and re-layouts: 2.35 us -> none  [the longest x6 1.81 us: extended_2(): lax.slice_in_dim(block, block.shape[dim] - width, None, axis=dim)]
  transfers between devices with their start and end apart: 14 -> 6, of which waited for: 8 -> 3; matrix products, arithmetic and copies ran while one was open for 41% -> 0% of each run, Pallas kernels for 0% -> 9%
where the time goes in v3:
time: 27.3 us; the launch traced here: 27.2 us
  waiting for transfers between devices  12.4 us (45%)
  starting transfers between devices  9.31 us (34%)
  Pallas kernels  5.42 us (20%)
    ppermute x2, waiting for transfers between devices, window_swap(): got = lax.ppermute(down, 'win', even_pairs(n))  9.14 us
    ppermute x2, starting transfers between devices, neighbour_swap(): from_odd = lax.ppermute(odd_msg, axis, odd_pairs(n))  4.35 us
    ppermute x2, waiting for transfers between devices, neighbour_swap(): from_odd = lax.ppermute(odd_msg, axis, odd_pairs(n))  3.23 us
    ppermute x2, starting transfers between devices, window_swap(): got = lax.ppermute(down, 'win', even_pairs(n))  3.11 us
    ppermute x2, starting transfers between devices, neighbour_swap(): from_even = lax.ppermute(even_msg, axis, even_pairs(n))  1.85 us
    pallas_call x1, Pallas kernels, per_device(): call(functools.partial(edge_kernel, copies), [vmem()] * 7, [tile], 1 << 25)  1.62 us
    pallas_call x1, Pallas kernels, per_device(): call(functools.partial(inner_kernel, copies), [vmem()] * (6 + copies), [t...  1.45 us
    pallas_call x1, Pallas kernels, per_device(): call(functools.partial(load_kernel, swap2, copies), [hbm()] * 6, [tile, t...  1.41 us
  transfers between devices with their start and end apart: 6, of which 3 were waited for; matrix products, arithmetic and copies ran while one was open for 0% of the time, Pallas kernels for 9%

profile of v3, /device:TPU:0, one launch (start us, length us, event | category | flops | bytes accessed | tf_op | source)
XLA Modules:
  0.0 27.2 jit_solution(6309800515204223949)
XLA Ops:
  0.0 1.4 %shard_map.64 = (f32[3,64,256]{2,1,0:T(8,128)S(1)}, f32[3,64,256]{2,1,0:T(8,128)S(1)}, f32[2,64,256]{2,1,0:T(8,128)S(1)}, s32[1,1024]{1,0:T(1,128)S(1)}, f32[3,1...) custom-call(f32[3,64,256]{2,1,0:T(8,128)} %bitcast.7, ...), custom_call_target="tpu_custom_call" | custom-call | flops 1048576 | bytes 1048576 | tf_op jit(solution)/shard_map/pallas_call | solution.py:535
  1.4 3.0 %collective-permute-start.5 = (f32[6,64,256]{2,1,0:T(8,128)S(1)}, f32[6,64,256]{2,1,0:T(8,128)S(1)}, u32[]{:S(2)}, u32[]{:S(2)}) collective-permute-start(f32[6,64,256]{2,1,0:T(8,128)S(1)} %get-tuple-element.48), channel_id=1, source_target_pairs={{0,16},{16,0},{1,17},{17,1},{2,18},{18,2},{3,19},{19,3},{4,20},{20... | collective-permute-start | bytes 1179656 | tf_op jit(solution)/shard_map/ppermute | solution.py:40
  4.4 0.1 collective-permute-start
  4.5 0.6 %shard_map.65 = (f32[3,64,256]{2,1,0:T(8,128)S(1)}, f32[40,256]{1,0:T(8,128)S(1)}, f32[40,256]{1,0:T(8,128)S(1)}, f32[64,128]{1,0:T(8,128)S(1)}, f32[64,128]{1,0:T(8,128)S(1)}) custom-call(f32[3,64,256]{2,1,0:T(8,128)S(1)} %get-tuple-element.29.inc, f32[2,64,256]{2,1,0:T(8,128)S(1)} %get-tuple-element.30.wind, s32[1,1024]{1,0:T(1,128)S(1)} %get-tuple-element.31.cells, ...), custom_call_target="tpu_custom_call" | custom-call | flops 536870912 | bytes 1048576 | tf_op jit(solution)/shard_map/pallas_call | solution.py:548
  5.1 9.1 %collective-permute-done.refs_4_ = f32[64,128]{1,0:T(8,128)S(1)} collective-permute-done((f32[64,128]{1,0:T(8,128)S(1)}, f32[64,128]{1,0:T(8,128)S(1)}, u32[]{:S(2)}, u32[]{:S(2)}) %collective-permute-start) | collective-permute-done | bytes 32800 | tf_op jit(solution)/shard_map/ppermute | solution.py:40
  14.3 0.2 shard_map.66
  14.4 0.1 collective-permute-start.1
  14.5 1.9 %collective-permute-start.2 = (f32[40,256]{1,0:T(8,128)S(1)}, f32[40,256]{1,0:T(8,128)S(1)}, u32[]{:S(2)}, u32[]{:S(2)}) collective-permute-start(f32[40,256]{1,0:T(8,128)S(1)} %get-tuple-element.39), channel_id=1, source_target_pairs={{0,12},{4,8},{8,4},{12,0},{1,13},{5,9},{9,5},{13,1},{2,14},{6,10},... | collective-permute-start | bytes 122888 | tf_op jit(solution)/shard_map/ppermute | solution.py:33
  16.4 0.0 collective-permute-done.1.got_even
  16.4 1.7 %collective-permute-done.2.got_odd = f32[40,256]{1,0:T(8,128)S(1)} collective-permute-done((f32[40,256]{1,0:T(8,128)S(1)}, f32[40,256]{1,0:T(8,128)S(1)}, u32[]{:S(2)}, u32[]{:S(2)}) %collective-permute-start.2) | collective-permute-done | bytes 40992 | tf_op jit(solution)/shard_map/ppermute | solution.py:33
  18.1 0.2 shard_map.67
  18.3 1.8 %collective-permute-start.3 = (f32[24,128]{1,0:T(8,128)S(1)}, f32[24,128]{1,0:T(8,128)S(1)}, u32[]{:S(2)}, u32[]{:S(2)}) collective-permute-start(f32[24,128]{1,0:T(8,128)S(1)} %get-tuple-element.42), channel_id=1, source_target_pairs={{0,1},{1,0},{2,3},{3,2},{4,5},{5,4},{6,7},{7,6},{8,9},{9,8},{10,11... | collective-permute-start | bytes 36872 | tf_op jit(solution)/shard_map/ppermute | solution.py:32
  20.0 2.5 %collective-permute-start.4 = (f32[24,128]{1,0:T(8,128)S(1)}, f32[24,128]{1,0:T(8,128)S(1)}, u32[]{:S(2)}, u32[]{:S(2)}) collective-permute-start(f32[24,128]{1,0:T(8,128)S(1)} %get-tuple-element.43), channel_id=1, source_target_pairs={{0,3},{1,2},{2,1},{3,0},{4,7},{5,6},{6,5},{7,4},{8,11},{9,10},{10,... | collective-permute-start | bytes 36872 | tf_op jit(solution)/shard_map/ppermute | solution.py:33
  22.5 0.0 collective-permute-done.5.refs_0_
  22.5 1.4 %shard_map.68 = (f32[3,64,256]{2,1,0:T(8,128)S(1)}, f32[14,72,128]{2,1,0:T(8,128)S(1)}, f32[3,64,128]{2,1,0:T(8,128)S(1)}, f32[16,128]{1,0:T(8,128)S(1)}) custom-call(f32[3,64,256]{2,1,0:T(8,128)S(1)} %get-tuple-element.29.inc, f32[3,64,256]{2,1,0:T(8,128)S(1)} %get-tuple-element.44.wgt, f32[2,64,256]{2,1,0:T(8,128)S(1)} %get-tuple-element.30.wind, ...), custom_call_target="tpu_custom_call" | custom-call | flops 536870912 | bytes 1048576 | tf_op jit(solution)/shard_map/pallas_call | solution.py:568
  24.0 0.0 collective-permute-done.3.got_even
  24.0 1.5 %collective-permute-done.4.got_odd = f32[24,128]{1,0:T(8,128)S(1)} collective-permute-done((f32[24,128]{1,0:T(8,128)S(1)}, f32[24,128]{1,0:T(8,128)S(1)}, u32[]{:S(2)}, u32[]{:S(2)}) %collective-permute-start.4) | collective-permute-done | bytes 12320 | tf_op jit(solution)/shard_map/ppermute | solution.py:33
  25.5 1.6 %shard_map.69 = f32[3,64,256]{2,1,0:T(8,128)} custom-call(f32[24,128]{1,0:T(8,128)S(1)} %collective-permute-done.3.got_even, f32[24,128]{1,0:T(8,128)S(1)} %collective-permute-done.4.got_odd, f32[14,72,128]{2,1,0:T(8,128)S(1)} %get-tuple-element.49.edges, f32[3,64,128]{2,1,0:T(8,128)S(1)} %get-tuple-element.50.wgt_edges, ...), custom_call_target="tpu_custom_call" | custom-call | flops 33554432 | bytes 1048576 | tf_op jit(solution)/shard_map/pallas_call | solution.py:575
Async XLA Ops:
  1.4 21.1 %collective-permute-start.5 = (f32[6,64,256]{2,1,0:T(8,128)S(1)}, f32[6,64,256]{2,1,0:T(8,128)S(1)}, u32[]{:S(2)}, u32[]{:S(2)}) collective-permute-start(f32[6,64,256]{2,1,0:T(8,128)S(1)} %get-tuple-element.48), channel_id=1, source_target_pairs={{0,16},{16,0},{1,17},{17,1},{2,18},{18,2},{3,19},{19,3},{4,20},{20... | collective-permute-start | bytes 1179656 | tf_op jit(solution)/shard_map/ppermute | solution.py:40
  4.4 9.8 %collective-permute-start = (f32[64,128]{1,0:T(8,128)S(1)}, f32[64,128]{1,0:T(8,128)S(1)}, u32[]{:S(2)}, u32[]{:S(2)}) collective-permute-start(f32[64,128]{1,0:T(8,128)S(1)} %get-tuple-element.37), channel_id=1, source_target_pairs={{0,16},{16,0},{1,17},{17,1},{2,18},{18,2},{3,19},{19,3},{4,20},{20... | collective-permute-start | bytes 98312 | tf_op jit(solution)/shard_map/ppermute | solution.py:40
  14.4 2.0 %collective-permute-start.1 = (f32[40,256]{1,0:T(8,128)S(1)}, f32[40,256]{1,0:T(8,128)S(1)}, u32[]{:S(2)}, u32[]{:S(2)}) collective-permute-start(f32[40,256]{1,0:T(8,128)S(1)} %get-tuple-element.38), channel_id=1, source_target_pairs={{0,4},{4,0},{8,12},{12,8},{1,5},{5,1},{9,13},{13,9},{2,6},{6,2},{1... | collective-permute-start | bytes 122888 | tf_op jit(solution)/shard_map/ppermute | solution.py:32
  14.5 3.6 %collective-permute-start.2 = (f32[40,256]{1,0:T(8,128)S(1)}, f32[40,256]{1,0:T(8,128)S(1)}, u32[]{:S(2)}, u32[]{:S(2)}) collective-permute-start(f32[40,256]{1,0:T(8,128)S(1)} %get-tuple-element.39), channel_id=1, source_target_pairs={{0,12},{4,8},{8,4},{12,0},{1,13},{5,9},{9,5},{13,1},{2,14},{6,10},... | collective-permute-start | bytes 122888 | tf_op jit(solution)/shard_map/ppermute | solution.py:33
  18.3 5.7 %collective-permute-start.3 = (f32[24,128]{1,0:T(8,128)S(1)}, f32[24,128]{1,0:T(8,128)S(1)}, u32[]{:S(2)}, u32[]{:S(2)}) collective-permute-start(f32[24,128]{1,0:T(8,128)S(1)} %get-tuple-element.42), channel_id=1, source_target_pairs={{0,1},{1,0},{2,3},{3,2},{4,5},{5,4},{6,7},{7,6},{8,9},{9,8},{10,11... | collective-permute-start | bytes 36872 | tf_op jit(solution)/shard_map/ppermute | solution.py:32
  20.0 5.5 %collective-permute-start.4 = (f32[24,128]{1,0:T(8,128)S(1)}, f32[24,128]{1,0:T(8,128)S(1)}, u32[]{:S(2)}, u32[]{:S(2)}) collective-permute-start(f32[24,128]{1,0:T(8,128)S(1)} %get-tuple-element.43), channel_id=1, source_target_pairs={{0,3},{1,2},{2,1},{3,0},{4,7},{5,6},{6,5},{7,4},{8,11},{9,10},{10,... | collective-permute-start | bytes 36872 | tf_op jit(solution)/shard_map/ppermute | solution.py:33

commit v4 on v3

--- a/solution.py
+++ b/solution.py
@@ -57,6 +57,15 @@
 
 def axis_even(axis):
     return lax.axis_index(axis) % 2 == 0
+
+
+def line_planes(lay):
+    fields = lay.fields
+    lines = [range(fields), range(fields, fields + 2), range(fields + 2, lay.own)]
+    for k in range(lay.copies):
+        base = lay.own + k * lay.packet
+        lines += [range(base, base + fields), range(base + fields, base + lay.packet)]
+    return lines
 
 
 class Layout:
@@ -69,6 +78,14 @@
         self.starts = [sum(self.depths[:j]) for j in range(self.count)]
         self.used = sum(self.depths)
         self.row_blocks = -(-self.used // 8)
+        spots = [0, HALO] + [2 * HALO + RIM * k for k in range(1 + 2 * copies)]
+        self.group = 2 * HALO + RIM * (1 + 2 * copies)
+        self.wide = self.group * fields
+        self.lanes = [0] * self.count
+        for spot, members in zip(spots, line_planes(self)):
+            for f, j in enumerate(members):
+                self.lanes[j] = self.group * f + spot
+        self.spots = spots
 
     def groups(self, blocks, width):
         per = -(-blocks // (LANES // width))
@@ -118,59 +135,51 @@
 
 
 def load_kernel(swap2, copies, *refs):
-    inc_far, wgt_far, wind_far, mix_far, cells_far, scale_far = refs[:6]
-    inc, wgt, wind, cells, scale, mixrows = refs[6:12]
-    bulk = refs[12 : 12 + copies]
-    strips = refs[12 + copies : 12 + 2 * copies]
-    mix, sems = refs[12 + 2 * copies :]
-    fields, rows, cols = inc.shape
+    inc_far, wgt_far, wind_far, mix_far, mixrows = refs[:5]
+    bulk = refs[5 : 5 + copies]
+    strips = refs[5 + copies : 5 + 2 * copies]
+    mix, sems = refs[5 + 2 * copies :]
+    packet, rows, cols = bulk[0].shape
+    fields = packet // 2
     lay = Layout(fields, copies)
     sends_up = lax.axis_index("win") == 0
     moves = [
-        pltpu.make_async_copy(src, dst, sems.at[i])
-        for i, (src, dst) in enumerate(
-            [
-                (inc_far, inc),
-                (wgt_far, wgt),
-                (wind_far, wind),
-                (mix_far, mix),
-                (cells_far, cells),
-                (scale_far, scale),
-                (inc_far, bulk[0].at[pl.ds(0, fields)]),
-            ]
-        )
+        pltpu.make_async_copy(inc_far, ref.at[pl.ds(0, fields)], sems.at[i]) for i, ref in enumerate(bulk)
     ]
-    to_down = pltpu.make_async_copy(wgt_far, bulk[0].at[pl.ds(fields, fields)], sems.at[7])
-    to_up = pltpu.make_async_copy(wind_far, bulk[-1].at[pl.ds(fields, 2)], sems.at[8])
+    moves.append(pltpu.make_async_copy(mix_far, mix, sems.at[2]))
+    to_down = pltpu.make_async_copy(wgt_far, bulk[0].at[pl.ds(fields, fields)], sems.at[3])
+    to_up = pltpu.make_async_copy(wind_far, bulk[-1].at[pl.ds(fields, 2)], sems.at[4])
+
+    def on(condition, action):
+        if swap2:
+            pl.when(condition)(action)
+        else:
+            action()
+
     for move in moves:
         move.start()
-    if swap2:
-
-        @pl.when(sends_up)
-        def _():
-            to_up.start()
-
-        @pl.when(jnp.logical_not(sends_up))
-        def _():
-            to_down.start()
-
-    else:
-        moves.append(pltpu.make_async_copy(inc_far, bulk[1].at[pl.ds(0, fields)], sems.at[9]))
-        moves[-1].start()
-        to_up.start()
-        to_down.start()
-    for move in moves[:4]:
+    on(sends_up, lambda: to_up.start())
+    on(jnp.logical_not(sends_up), lambda: to_down.start())
+    for move in moves:
         move.wait()
-
-    first = [inc[f] for f in range(fields)]
-    down = first + [wgt[f] for f in range(fields)]
-    up = first + [wind[0], wind[1]] + [wind[1]] * (fields - 2)
-
-    def choose(a, b):
-        return jnp.where(sends_up, a, b) if swap2 else b
+    which = sub_iota(mixrows.shape)
+    spread = jnp.zeros(mixrows.shape, F32)
+    for f in range(fields):
+        for g in range(fields):
+            spread = jnp.where(which == f * fields + g, mix[f, 0, g], spread)
+    mixrows[...] = spread
+
+    def fill_up():
+        to_up.wait()
+        used = mixrows.shape[0]
+        bulk[-1][packet - 1, pl.ds(0, used), :] = spread[:, :cols]
+        bulk[-1][packet - 1, pl.ds(used, rows - used), :] = jnp.zeros((rows - used, cols), F32)
+
+    on(sends_up, fill_up)
+    on(jnp.logical_not(sends_up), lambda: to_down.wait())
 
     for k, ref in enumerate(strips):
-        planes = [choose(u, d) for u, d in zip(up, down)] if k == 0 else up
+        planes = [bulk[k][j] for j in range(packet)]
         pieces = []
         for j, x in enumerate(planes):
             pieces.append((x[:8], 0, 4 * j, RIM))
@@ -187,39 +196,23 @@
         for m, block in enumerate(squeeze_lanes(pack_lanes(pieces), 4 * lay.packet, lay)):
             ref[pl.ds(8 * (len(blocks) * halves + m), 8), :] = block
 
-    which = sub_iota(mixrows.shape)
-    spread = jnp.zeros(mixrows.shape, F32)
-    for f in range(fields):
-        for g in range(fields):
-            spread = jnp.where(which == f * fields + g, mix[f, 0, g], spread)
-    mixrows[...] = spread
-
-    def finish_up():
-        to_up.wait()
-        used = mixrows.shape[0]
-        bulk[-1][2 * fields - 1, pl.ds(0, used), :] = spread[:, :cols]
-        bulk[-1][2 * fields - 1, pl.ds(used, rows - used), :] = jnp.zeros((rows - used, cols), F32)
-
-    if swap2:
-
-        @pl.when(sends_up)
-        def _():
-            finish_up()
-
-        @pl.when(jnp.logical_not(sends_up))
-        def _():
-            to_down.wait()
-
-    else:
-        to_down.wait()
-        finish_up()
-    for move in moves[4:]:
-        move.wait()
-
-
-def own_kernel(copies, inc, wind, cells, scale, hmap, row_first, row_last, col_low, col_high):
-    fields, rows, cols = inc.shape
+
+def own_kernel(copies, bulk, wind_far, wgt_far, cells_far, scale_far, *refs):
+    wind, wgt, hmap, row_first, row_last, col_low, col_high, cells, scale, sems = refs
+    moves = [
+        pltpu.make_async_copy(src, dst, sems.at[i])
+        for i, (src, dst) in enumerate(
+            [(cells_far, cells), (scale_far, scale), (wind_far, wind), (wgt_far, wgt)]
+        )
+    ]
+    for move in moves:
+        move.start()
+    packet, rows, cols = bulk.shape
+    fields = packet // 2
+    inc = bulk
     lay = Layout(fields, copies)
+    moves[0].wait()
+    moves[1].wait()
     nobs = cells.shape[-1]
     index = cells[...]
     row_hot = sub_iota((rows, nobs)) == index // cols
@@ -234,6 +227,7 @@
     sums = lax.dot_general(
         jnp.concatenate(terms, axis=0), col_hot, (((1,), (1,)), ((), ())), preferred_element_type=F32
     )
+    moves[2].wait()
     planes = [inc[f] for f in range(fields)] + [wind[0], wind[1]]
     for f in range(fields):
         base = 3 * f * rows
@@ -249,8 +243,10 @@
         blank = jnp.zeros((8, cols), F32)
         row_first[pl.ds(8 * m, 8), :] = blank if first[m] is None else first[m]
         row_last[pl.ds(8 * m, 8), :] = blank if last[m] is None else last[m]
+    where = list(zip(planes, lay.lanes, lay.depths))
     col_low[...] = pack_lanes([(x[:, :LANES], 0, at, d) for x, at, d in where])
     col_high[...] = pack_lanes([(x[:, -LANES:], LANES - d, at, d) for x, at, d in where])
+    moves[3].wait()
 
 
 def join_kernel(fields, copies, *refs):
@@ -275,6 +271,7 @@
             at = lay.starts[lay.own + k * lay.packet + j]
             first_pieces.append((blocks[4 * j // 8], 4 * j % 8, at, RIM))
             last_pieces.append((blocks[4 * j // 8], 4 * j % 8 + 2, at, RIM))
+            at = lay.lanes[lay.own + k * lay.packet + j]
             low_pieces.append((wide, 4 * j, at, RIM))
             high_pieces.append((wide, 4 * j + 2, at, RIM))
     is_even = axis_even("lat")
@@ -320,11 +317,11 @@
         block = jnp.where(inside, block, 0.0)
         halo_rows[j] = block
         blocks.append(block)
-    where = list(zip(blocks, lay.starts, lay.depths))
+    where = list(zip(blocks, lay.lanes, lay.depths))
     low_tail = pack_lanes([(x[:, :LANES], 0, at, d) for x, at, d in where])
     high_tail = pack_lanes([(x[:, -LANES:], LANES - d, at, d) for x, at, d in where])
-    low_all = squeeze_lanes(jnp.concatenate([col_low[...], low_tail], axis=0), lay.used, lay)
-    high_all = squeeze_lanes(jnp.concatenate([col_high[...], high_tail], axis=0), lay.used, lay)
+    low_all = squeeze_lanes(jnp.concatenate([col_low[...], low_tail], axis=0), lay.wide, lay)
+    high_all = squeeze_lanes(jnp.concatenate([col_high[...], high_tail], axis=0), lay.wide, lay)
     lon_even = axis_even("lon")
     for m, (a, b) in enumerate(zip(low_all, high_all)):
         msg_even[pl.ds(8 * m, 8), :] = jnp.where(lon_even, b, a)
@@ -414,68 +411,149 @@
     ]
 
 
-EDGE = 12
-
-
-def edge_lanes(block_low, block_high):
-    low = turn(block_low, HALO, 1)
-    high = turn(block_high, HALO + 2 * EDGE, 1)
-    return jnp.where(lane_iota(low.shape) < HALO + EDGE, low, high)
+SIDE = LANES // 2
+
+
+def edge_line(tiles, group):
+    out = None
+    lane = None
+    for f, x in enumerate(tiles):
+        base = group * f
+        low = turn(x[:, :LANES], base + HALO, 1)
+        high = turn(x[:, -LANES:], SIDE + base + group - HALO, 1)
+        if lane is None:
+            lane = lane_iota(low.shape)
+        both = jnp.where(lane < SIDE, low, high)
+        out = both if out is None else jnp.where(lane % SIDE >= base, both, out)
+    return out
+
+
+def line_offsets(fields):
+    return [o for o in range(1 - fields, fields)]
+
+
+def line_factors(mix, fields, group):
+    lane = lane_iota((1, LANES)) % SIDE
+    rows = []
+    for o in line_offsets(fields):
+        row = jnp.zeros((1, LANES), F32)
+        for f in range(fields):
+            if 0 <= f - o < fields:
+                factor = mix(f, f - o)[:, :LANES]
+                if o == 0:
+                    factor = factor + (1.0 - 4.0 * DIFFUSION)
+                row = jnp.where((lane >= group * f) & (lane < group * (f + 1)), factor, row)
+        rows.append(row)
+    return rows
+
+
+def line_blend(factors, x, fields, group):
+    total = None
+    for o, factor in zip(line_offsets(fields), factors):
+        term = factor * turn(x, group * o, 1)
+        total = term if total is None else total + term
+    return total
+
+
+def line_wind(pair, group):
+    lane = lane_iota(pair.shape) % SIDE
+    up, down = turn(pair, group, 1), turn(pair, -group, 1)
+    far_up = turn(pair, 2 * group, 1)
+    u = jnp.where(lane < group, pair, jnp.where(lane < 2 * group, up, far_up))
+    v = jnp.where(lane < group, down, jnp.where(lane < 2 * group, pair, up))
+    return u, v
+
+
+def line_tangent(x, u, v, factors, fields, group):
+    kn, ks, ke, kw = DIFFUSION - v, DIFFUSION + v, DIFFUSION - u, DIFFUSION + u
+    return (
+        line_blend(factors, x, fields, group)
+        + (kn * north(x) + ks * south(x))
+        + (ke * east_of(x) + kw * west_of(x))
+    )
+
+
+def line_adjoint(x, u, v, factors, fields, group):
+    kn, ks, ke, kw = DIFFUSION + v, DIFFUSION - v, DIFFUSION + u, DIFFUSION - u
+    return (
+        line_blend(factors, x, fields, group)
+        + (north(kn * x) + south(ks * x))
+        + (east_of(ke * x) + west_of(kw * x))
+    )
 
 
 def inner_kernel(copies, inc, wgt, wind, hmap, mixrows, halo_rows, *refs):
     bulk = refs[:copies]
-    part, edges, wgt_edges, prior_rows = refs[copies:]
-    fields, rows, cols = inc.shape
+    part, edges, wgt_edges, factors = refs[copies:]
+    fields, rows, cols = wgt.shape
     lay = Layout(fields, copies)
     tiles = [inc[f] for f in range(fields)] + [wind[0], wind[1]] + [hmap[f] for f in range(fields)]
     for ref in bulk:
         tiles += [ref[j] for j in range(lay.packet)]
-    planes = []
-    for j, tile in enumerate(tiles):
-        planes.append(jnp.concatenate([tile, halo_rows[j]], axis=0))
-        edges[j] = edge_lanes(planes[-1][:, :LANES], planes[-1][:, -LANES:])
-    for f in range(fields):
-        wgt_edges[f] = edge_lanes(wgt[f, :, :LANES], wgt[f, :, cols - LANES :])
+    planes = [jnp.concatenate([tile, halo_rows[j]], axis=0) for j, tile in enumerate(tiles)]
+    for k, members in enumerate(line_planes(lay)):
+        edges[k] = edge_line([planes[j] for j in members], lay.group)
+    wgt_edges[...] = edge_line([wgt[f] for f in range(fields)], lay.group)
     above = planes[lay.own : lay.own + lay.packet]
     below = planes[-lay.packet :]
     spread = bulk[-1][2 * fields - 1, :16]
-    prior_rows[...] = spread[:, :LANES]
-    mix = mixing(mixrows[:, :cols], fields)
-    result = product(planes[: lay.own], above, below, wgt, mix, mixing(spread, fields), fields, rows)
+    mix, prior_mix = mixing(mixrows[:, :cols], fields), mixing(spread, fields)
+    lists = []
+    for maker in (mix, lambda f, g: mix(g, f), prior_mix):
+        lists += line_factors(maker, fields, lay.group)
+    for i, row in enumerate(lists):
+        factors[i : i + 1] = row
+    result = product(planes[: lay.own], above, below, wgt, mix, prior_mix, fields, rows)
     for f in range(fields):
         part[f] = result[f]
 
 
-def edge_kernel(copies, got_even, got_odd, edges, wgt_edges, part, mixrows, prior_rows, out):
+def edge_kernel(copies, got_even, got_odd, edges, wgt_edges, factors, part, out):
     fields, rows, cols = part.shape
     lay = Layout(fields, copies)
     blocks = rows // 8 + 1
-    _, per = lay.groups(blocks, lay.used)
+    group = lay.group
+    _, per = lay.groups(blocks, lay.wide)
     lon_even = axis_even("lon")
     even = [got_even[pl.ds(8 * i, 8), :] for i in range(per)]
     odd = [got_odd[pl.ds(8 * i, 8), :] for i in range(per)]
-    east = spread_lanes([jnp.where(lon_even, a, b) for a, b in zip(even, odd)], blocks, lay.used, lay)
-    west = spread_lanes([jnp.where(lon_even, b, a) for a, b in zip(even, odd)], blocks, lay.used, lay)
+    east = spread_lanes([jnp.where(lon_even, a, b) for a, b in zip(even, odd)], blocks, lay.wide, lay)
+    west = spread_lanes([jnp.where(lon_even, b, a) for a, b in zip(even, odd)], blocks, lay.wide, lay)
     lane = lane_iota(east.shape)
-    end = HALO + 2 * EDGE
-    planes = []
-    for j, (at, d) in enumerate(zip(lay.starts, lay.depths)):
-        left = turn(west, HALO - d - at, 1)
-        right = turn(east, end - at, 1)
-        planes.append(
-            jnp.where(lane < HALO, left, jnp.where((lane >= end) & (lane < end + d), right, edges[j]))
-        )
-    above = planes[lay.own : lay.own + lay.packet]
-    below = planes[-lay.packet :]
-    mix = mixing(mixrows[:, :LANES], fields)
-    result = product(
-        planes[: lay.own], above, below, wgt_edges, mix, mixing(prior_rows[...], fields), fields, rows
-    )
+    within = lane % SIDE % group
+    on_west = (lane < SIDE) & (within < HALO)
+    on_east = (lane >= SIDE) & (within >= group - HALO)
+    lines = []
+    for k, (spot, members) in enumerate(zip(lay.spots, line_planes(lay))):
+        depth = lay.depths[members[0]]
+        left = turn(west, HALO - depth - spot, 1)
+        right = turn(east, SIDE + group - HALO - spot, 1)
+        lines.append(jnp.where(on_west, left, jnp.where(on_east, right, edges[k])))
+    clear = row_mask(rows, LANES)
+    here = lax.axis_index("win")
+    has_later = here < lax.axis_size("win") - 1
+    has_earlier = here > 0
+    count = 2 * fields - 1
+    every = factors[...]
+    mix, mix_back, mix_prior = [
+        [every[g * count + i : g * count + i + 1] for i in range(count)] for g in range(3)
+    ]
+    inc, hmap = lines[0], lines[2]
+    u, v = line_wind(lines[1], group)
+    fwd = clear(line_tangent(inc, u, v, mix, fields, group))
+    fwd = line_tangent(fwd, u, v, mix, fields, group)
+    later = lines[4] * (lines[3] - fwd)
+    back = clear(hmap * fwd - jnp.where(has_later, later, 0.0))
+    back = clear(line_adjoint(back, u, v, mix_back, fields, group))
+    back = line_adjoint(back, u, v, mix_back, fields, group)
+    u, v = line_wind(lines[-1], group)
+    prior = clear(line_tangent(lines[-2], u, v, mix_prior, fields, group))
+    prior = line_tangent(prior, u, v, mix_prior, fields, group)[:rows]
+    result = wgt_edges[...] * (inc[:rows] - jnp.where(has_earlier, prior, 0.0)) + back[:rows]
     lane = lane_iota((rows, LANES))
     for f in range(fields):
-        low = turn(result[f], -HALO, 1)
-        high = turn(result[f], -(HALO + 2 * EDGE), 1)
+        low = turn(result, -(group * f + HALO), 1)
+        high = turn(result, LANES - HALO - (SIDE + group * f + group - 2 * HALO), 1)
         whole = part[f]
         if cols == LANES:
             out[f] = jnp.where(lane < HALO, low, jnp.where(lane >= LANES - HALO, high, whole))
@@ -530,27 +608,26 @@
     packet = (lay.packet, rows, cols)
     strip_rows = 8 * (-(-4 * lay.packet // 8) * (cols // LANES) + lay.groups(rows // 8, 4 * lay.packet)[1])
     row_msg = (8 * lay.row_blocks, cols)
-    col_msg = (8 * lay.groups(tall // 8, lay.used)[1], LANES)
-
-    inc, wgt, wind, cells, scale, mixrows, *rest = call(
+    col_msg = (8 * lay.groups(tall // 8, lay.wide)[1], LANES)
+
+    mixrows, *rest = call(
         functools.partial(load_kernel, swap2, copies),
-        [hbm()] * 6,
-        [tile, tile, wind.shape, jax.ShapeDtypeStruct(cells.shape, jnp.int32), scale.shape, (16, cols)]
-        + [packet] * copies
-        + [(strip_rows, LANES)] * copies,
+        [hbm()] * 4,
+        [(16, cols)] + [packet] * copies + [(strip_rows, LANES)] * copies,
         1 << 20,
-        [pltpu.SMEM(mix.shape, F32), pltpu.SemaphoreType.DMA((10,))],
-    )(far(inc), far(wgt), far(wind), far(mix), far(cells), far(scale))
-    bulk, strips = rest[:copies], rest[copies:]
+        [pltpu.SMEM(mix.shape, F32), pltpu.SemaphoreType.DMA((5,))],
+    )(far(inc), far(wgt), far(wind), far(mix))
+    sent, strips = rest[:copies], rest[copies:]
     strips = window_swap(strips[0], strips[-1])[:copies]
-    bulk = window_swap(bulk[0], bulk[-1])[:copies]
-
-    hmap, row_first, row_last, col_low, col_high = call(
+    bulk = window_swap(sent[0], sent[-1])[:copies]
+
+    wind_near, wgt_near, hmap, row_first, row_last, col_low, col_high = call(
         functools.partial(own_kernel, copies),
-        [vmem()] * 4,
-        [tile, row_msg, row_msg, (rows, LANES), (rows, LANES)],
+        [vmem()] + [hbm()] * 4,
+        [wind.shape, tile, tile, row_msg, row_msg, (rows, LANES), (rows, LANES)],
         1 << 29,
-    )(inc, wind, cells, scale)
+        [pltpu.VMEM(cells.shape, jnp.int32), pltpu.VMEM(scale.shape, F32), pltpu.SemaphoreType.DMA((4,))],
+    )(sent[0], far(wind), far(wgt), far(cells), far(scale))
 
     row_even, row_odd, col_low, col_high = call(
         functools.partial(join_kernel, fields, copies),
@@ -565,16 +642,17 @@
     )(got_even, got_odd, col_low, col_high)
     got_even, got_odd = neighbour_swap(msg_even, msg_odd, "lon")
 
-    part, edges, wgt_edges, prior_rows = call(
+    lines = len(line_planes(lay))
+    part, edges, wgt_edges, factors = call(
         functools.partial(inner_kernel, copies),
         [vmem()] * (6 + copies),
-        [tile, (lay.count, tall, LANES), (fields, rows, LANES), (16, LANES)],
+        [tile, (lines, tall, LANES), (rows, LANES), (8 * -(-3 * (2 * fields - 1) // 8), LANES)],
         1 << 29,
-    )(inc, wgt, wind, hmap, mixrows, halo_rows, *bulk)
+    )(sent[0], wgt_near, wind_near, hmap, mixrows, halo_rows, *bulk)
 
     (out,) = call(
-        functools.partial(edge_kernel, copies), [vmem()] * 7, [tile], 1 << 25
-    )(got_even, got_odd, edges, wgt_edges, part, mixrows, prior_rows)
+        functools.partial(edge_kernel, copies), [vmem()] * 6, [tile], 1 << 25
+    )(got_even, got_odd, edges, wgt_edges, factors, part)
     return out[None]
 
 

time: 27.3 us -> 27.2 us (level)
  waiting for transfers between devices: 12.4 us -> 11.5 us
  Pallas kernels: 5.42 us -> 6.15 us
    ppermute x2, waiting for transfers between devices: 9.14 us -> 8.26 us  [window_swap(): got = lax.ppermute(down, 'win', even_pairs(n))]
    pallas_call x3, Pallas kernels: 3.62 us -> 4.35 us  [the longest x1 1.62 us: per_device(): call(functools.partial(edge_kernel, copies), [vmem()] * 6, [tile], 1 << 25)]
  transfers between devices with their start and end apart: 6 -> 6, of which waited for: 3 -> 3; matrix products, arithmetic and copies ran while one was open for 0% -> 0% of each run, Pallas kernels for 9% -> 12%
where the time goes in v4:
time: 27.2 us; the launch traced here: 27 us
  waiting for transfers between devices  11.5 us (42%)
  starting transfers between devices  9.31 us (34%)
  Pallas kernels  6.15 us (23%)
    ppermute x2, waiting for transfers between devices, window_swap(): got = lax.ppermute(down, 'win', even_pairs(n))  8.26 us
    ppermute x2, starting transfers between devices, neighbour_swap(): from_odd = lax.ppermute(odd_msg, axis, odd_pairs(n))  4.33 us
    ppermute x2, waiting for transfers between devices, neighbour_swap(): from_odd = lax.ppermute(odd_msg, axis, odd_pairs(n))  3.23 us
    ppermute x2, starting transfers between devices, window_swap(): got = lax.ppermute(down, 'win', even_pairs(n))  3.13 us
    ppermute x2, starting transfers between devices, neighbour_swap(): from_even = lax.ppermute(even_msg, axis, even_pairs(n))  1.85 us
    pallas_call x1, Pallas kernels, per_device(): call(functools.partial(edge_kernel, copies), [vmem()] * 6, [tile], 1 << 25)  1.62 us
    pallas_call x1, Pallas kernels, per_device(): call(functools.partial(own_kernel, copies), [vmem()] + [hbm()] * 4, [wind...  1.48 us
    pallas_call x1, Pallas kernels, per_device(): call(functools.partial(inner_kernel, copies), [vmem()] * (6 + copies), [t...  1.45 us
  transfers between devices with their start and end apart: 6, of which 3 were waited for; matrix products, arithmetic and copies ran while one was open for 0% of the time, Pallas kernels for 12%

profile of v4, /device:TPU:0, one launch (start us, length us, event | category | flops | bytes accessed | tf_op | source)
XLA Modules:
  0.0 27.0 jit_solution(11043788232177665216)
XLA Ops:
  0.0 1.3 %shard_map.64 = (f32[16,256]{1,0:T(8,128)S(1)}, f32[6,64,256]{2,1,0:T(8,128)S(1)}, f32[64,128]{1,0:T(8,128)S(1)}) custom-call(f32[3,64,256]{2,1,0:T(8,128)} %bitcast.7, f32[3,64,256]{2,1,0:T(8,128)} %bitcast.8, f32[2,64,256]{2,1,0:T(8,128)} %bitcast.10, f32[3,1,3]{2,1,0:T(1,128)} %bitcast.12), custom_call_target="tpu_custom_call" | custom-call | flops 1048576 | bytes 1048576 | tf_op jit(solution)/shard_map/pallas_call | solution.py:613
  1.3 3.0 %collective-permute-start.5 = (f32[6,64,256]{2,1,0:T(8,128)S(1)}, f32[6,64,256]{2,1,0:T(8,128)S(1)}, u32[]{:S(2)}, u32[]{:S(2)}) collective-permute-start(f32[6,64,256]{2,1,0:T(8,128)S(1)} %get-tuple-element.26.bulk.inc), channel_id=1, source_target_pairs={{0,16},{16,0},{1,17},{17,1},{2,18},{18,2},{3,19},{19,3},{4,20},{20... | collective-permute-start | bytes 1179656 | tf_op jit(solution)/shard_map/ppermute | solution.py:40
  4.3 0.1 collective-permute-start
  4.4 1.5 %shard_map.65 = (f32[2,64,256]{2,1,0:T(8,128)S(1)}, f32[3,64,256]{2,1,0:T(8,128)S(1)}, f32[3,64,256]{2,1,0:T(8,128)S(1)}, f32[40,256]{1,0:T(8,128)S(1)}, f32[40,...) custom-call(f32[6,64,256]{2,1,0:T(8,128)S(1)} %get-tuple-element.26.bulk.inc, ...), custom_call_target="tpu_custom_call" | custom-call | flops 536870912 | bytes 1048576 | tf_op jit(solution)/shard_map/pallas_call | solution.py:624
  5.9 8.3 %collective-permute-done.refs_4_ = f32[64,128]{1,0:T(8,128)S(1)} collective-permute-done((f32[64,128]{1,0:T(8,128)S(1)}, f32[64,128]{1,0:T(8,128)S(1)}, u32[]{:S(2)}, u32[]{:S(2)}) %collective-permute-start) | collective-permute-done | bytes 32800 | tf_op jit(solution)/shard_map/ppermute | solution.py:40
  14.1 0.2 shard_map.66
  14.3 0.1 collective-permute-start.1
  14.4 1.9 %collective-permute-start.2 = (f32[40,256]{1,0:T(8,128)S(1)}, f32[40,256]{1,0:T(8,128)S(1)}, u32[]{:S(2)}, u32[]{:S(2)}) collective-permute-start(f32[40,256]{1,0:T(8,128)S(1)} %get-tuple-element.33), channel_id=1, source_target_pairs={{0,12},{4,8},{8,4},{12,0},{1,13},{5,9},{9,5},{13,1},{2,14},{6,10},... | collective-permute-start | bytes 122888 | tf_op jit(solution)/shard_map/ppermute | solution.py:33
  16.3 0.0 collective-permute-done.1.got_even
  16.3 1.7 %collective-permute-done.2.got_odd = f32[40,256]{1,0:T(8,128)S(1)} collective-permute-done((f32[40,256]{1,0:T(8,128)S(1)}, f32[40,256]{1,0:T(8,128)S(1)}, u32[]{:S(2)}, u32[]{:S(2)}) %collective-permute-start.2) | collective-permute-done | bytes 40992 | tf_op jit(solution)/shard_map/ppermute | solution.py:33
  17.9 0.2 shard_map.67
  18.1 1.8 %collective-permute-start.3 = (f32[24,128]{1,0:T(8,128)S(1)}, f32[24,128]{1,0:T(8,128)S(1)}, u32[]{:S(2)}, u32[]{:S(2)}) collective-permute-start(f32[24,128]{1,0:T(8,128)S(1)} %get-tuple-element.36), channel_id=1, source_target_pairs={{0,1},{1,0},{2,3},{3,2},{4,5},{5,4},{6,7},{7,6},{8,9},{9,8},{10,11... | collective-permute-start | bytes 36872 | tf_op jit(solution)/shard_map/ppermute | solution.py:32
  19.9 2.5 %collective-permute-start.4 = (f32[24,128]{1,0:T(8,128)S(1)}, f32[24,128]{1,0:T(8,128)S(1)}, u32[]{:S(2)}, u32[]{:S(2)}) collective-permute-start(f32[24,128]{1,0:T(8,128)S(1)} %get-tuple-element.37), channel_id=1, source_target_pairs={{0,3},{1,2},{2,1},{3,0},{4,7},{5,6},{6,5},{7,4},{8,11},{9,10},{10,... | collective-permute-start | bytes 36872 | tf_op jit(solution)/shard_map/ppermute | solution.py:33
  22.4 0.0 collective-permute-done.5.refs_0_
  22.4 1.4 %shard_map.68 = (f32[3,64,256]{2,1,0:T(8,128)S(1)}, f32[5,72,128]{2,1,0:T(8,128)S(1)}, f32[64,128]{1,0:T(8,128)S(1)}, f32[16,128]{1,0:T(8,128)S(1)}) custom-call(f32[6,64,256]{2,1,0:T(8,128)S(1)} %get-tuple-element.26.bulk.inc, f32[3,64,256]{2,1,0:T(8,128)S(1)} %get-tuple-element.38.wgt, f32[2,64,256]{2,1,0:T(8,128)S(1)} %get-tuple-element.39.wind, ...), custom_call_target="tpu_custom_call" | custom-call | flops 536870912 | bytes 1048576 | tf_op jit(solution)/shard_map/pallas_call | solution.py:646
  23.8 0.0 collective-permute-done.3.got_even
  23.8 1.6 %collective-permute-done.4.got_odd = f32[24,128]{1,0:T(8,128)S(1)} collective-permute-done((f32[24,128]{1,0:T(8,128)S(1)}, f32[24,128]{1,0:T(8,128)S(1)}, u32[]{:S(2)}, u32[]{:S(2)}) %collective-permute-start.4) | collective-permute-done | bytes 12320 | tf_op jit(solution)/shard_map/ppermute | solution.py:33
  25.4 1.6 %shard_map.69 = f32[3,64,256]{2,1,0:T(8,128)} custom-call(f32[24,128]{1,0:T(8,128)S(1)} %collective-permute-done.3.got_even, f32[24,128]{1,0:T(8,128)S(1)} %collective-permute-done.4.got_odd, f32[5,72,128]{2,1,0:T(8,128)S(1)} %get-tuple-element.43.edges, f32[64,128]{1,0:T(8,128)S(1)} %get-tuple-element.44.wgt_edges, ...), custom_call_target="tpu_custom_call" | custom-call | flops 33554432 | bytes 1048576 | tf_op jit(solution)/shard_map/pallas_call | solution.py:653
Async XLA Ops:
  1.3 21.1 %collective-permute-start.5 = (f32[6,64,256]{2,1,0:T(8,128)S(1)}, f32[6,64,256]{2,1,0:T(8,128)S(1)}, u32[]{:S(2)}, u32[]{:S(2)}) collective-permute-start(f32[6,64,256]{2,1,0:T(8,128)S(1)} %get-tuple-element.26.bulk.inc), channel_id=1, source_target_pairs={{0,16},{16,0},{1,17},{17,1},{2,18},{18,2},{3,19},{19,3},{4,20},{20... | collective-permute-start | bytes 1179656 | tf_op jit(solution)/shard_map/ppermute | solution.py:40
  4.3 9.8 %collective-permute-start = (f32[64,128]{1,0:T(8,128)S(1)}, f32[64,128]{1,0:T(8,128)S(1)}, u32[]{:S(2)}, u32[]{:S(2)}) collective-permute-start(f32[64,128]{1,0:T(8,128)S(1)} %get-tuple-element.31), channel_id=1, source_target_pairs={{0,16},{16,0},{1,17},{17,1},{2,18},{18,2},{3,19},{19,3},{4,20},{20... | collective-permute-start | bytes 98312 | tf_op jit(solution)/shard_map/ppermute | solution.py:40
  14.3 1.9 %collective-permute-start.1 = (f32[40,256]{1,0:T(8,128)S(1)}, f32[40,256]{1,0:T(8,128)S(1)}, u32[]{:S(2)}, u32[]{:S(2)}) collective-permute-start(f32[40,256]{1,0:T(8,128)S(1)} %get-tuple-element.32), channel_id=1, source_target_pairs={{0,4},{4,0},{8,12},{12,8},{1,5},{5,1},{9,13},{13,9},{2,6},{6,2},{1... | collective-permute-start | bytes 122888 | tf_op jit(solution)/shard_map/ppermute | solution.py:32
  14.4 3.5 %collective-permute-start.2 = (f32[40,256]{1,0:T(8,128)S(1)}, f32[40,256]{1,0:T(8,128)S(1)}, u32[]{:S(2)}, u32[]{:S(2)}) collective-permute-start(f32[40,256]{1,0:T(8,128)S(1)} %get-tuple-element.33), channel_id=1, source_target_pairs={{0,12},{4,8},{8,4},{12,0},{1,13},{5,9},{9,5},{13,1},{2,14},{6,10},... | collective-permute-start | bytes 122888 | tf_op jit(solution)/shard_map/ppermute | solution.py:33
  18.1 5.7 %collective-permute-start.3 = (f32[24,128]{1,0:T(8,128)S(1)}, f32[24,128]{1,0:T(8,128)S(1)}, u32[]{:S(2)}, u32[]{:S(2)}) collective-permute-start(f32[24,128]{1,0:T(8,128)S(1)} %get-tuple-element.36), channel_id=1, source_target_pairs={{0,1},{1,0},{2,3},{3,2},{4,5},{5,4},{6,7},{7,6},{8,9},{9,8},{10,11... | collective-permute-start | bytes 36872 | tf_op jit(solution)/shard_map/ppermute | solution.py:32
  19.9 5.5 %collective-permute-start.4 = (f32[24,128]{1,0:T(8,128)S(1)}, f32[24,128]{1,0:T(8,128)S(1)}, u32[]{:S(2)}, u32[]{:S(2)}) collective-permute-start(f32[24,128]{1,0:T(8,128)S(1)} %get-tuple-element.37), channel_id=1, source_target_pairs={{0,3},{1,2},{2,1},{3,0},{4,7},{5,6},{6,5},{7,4},{8,11},{9,10},{10,... | collective-permute-start | bytes 36872 | tf_op jit(solution)/shard_map/ppermute | solution.py:33

commit v5 on v4

--- a/solution.py
+++ b/solution.py
@@ -411,29 +411,24 @@
     ]
 
 
-SIDE = LANES // 2
-
-
-def edge_line(tiles, group):
-    out = None
-    lane = None
+def strip_lines(tiles, group):
+    west, east = None, None
     for f, x in enumerate(tiles):
-        base = group * f
-        low = turn(x[:, :LANES], base + HALO, 1)
-        high = turn(x[:, -LANES:], SIDE + base + group - HALO, 1)
-        if lane is None:
-            lane = lane_iota(low.shape)
-        both = jnp.where(lane < SIDE, low, high)
-        out = both if out is None else jnp.where(lane % SIDE >= base, both, out)
-    return out
+        low = turn(x[:, :LANES], group * f + HALO, 1)
+        high = turn(x[:, -LANES:], group * f + group - HALO, 1)
+        lane = lane_iota(low.shape)
+        west = low if f == 0 else jnp.where(lane >= group * f, low, west)
+        east = high if f == 0 else jnp.where(lane >= group * f, high, east)
+    return west, east
 
 
 def line_offsets(fields):
     return [o for o in range(1 - fields, fields)]
 
 
-def line_factors(mix, fields, group):
-    lane = lane_iota((1, LANES)) % SIDE
+def line_factors(mix, lay):
+    fields = lay.fields
+    lane = lane_iota((1, LANES)) % lay.wide
     rows = []
     for o in line_offsets(fields):
         row = jnp.zeros((1, LANES), F32)
@@ -442,7 +437,7 @@
                 factor = mix(f, f - o)[:, :LANES]
                 if o == 0:
                     factor = factor + (1.0 - 4.0 * DIFFUSION)
-                row = jnp.where((lane >= group * f) & (lane < group * (f + 1)), factor, row)
+                row = jnp.where((lane >= lay.group * f) & (lane < lay.group * (f + 1)), factor, row)
         rows.append(row)
     return rows
 
@@ -455,8 +450,9 @@
     return total
 
 
-def line_wind(pair, group):
-    lane = lane_iota(pair.shape) % SIDE
+def line_wind(pair, lay):
+    group = lay.group
+    lane = lane_iota(pair.shape) % lay.wide
     up, down = turn(pair, group, 1), turn(pair, -group, 1)
     far_up = turn(pair, 2 * group, 1)
     u = jnp.where(lane < group, pair, jnp.where(lane < 2 * group, up, far_up))
@@ -464,43 +460,82 @@
     return u, v
 
 
-def line_tangent(x, u, v, factors, fields, group):
+def folded(lay, blocks):
+    groups, per = lay.groups(blocks, lay.wide)
+    end = (blocks - 1) % per
+    far = lay.wide * (groups - 1)
+    sub, part = sub_iota((8, LANES)), lane_iota((8, LANES)) // lay.wide
+
+    def put(x, i, block):
+        pieces = [x[8 * j : 8 * j + 8] for j in range(per)]
+        pieces[i] = block
+        return jnp.concatenate(pieces, axis=0)
+
+    def up(x):
+        y = pltpu.roll(x, x.shape[0] - 1, 0)
+        last = y[8 * (per - 1) :]
+        y = put(y, per - 1, jnp.where((sub == 7) & (part < groups - 1), turn(last, -lay.wide, 1), last))
+        wrap = turn(turn(x[:8], 7, 0), far, 1)
+        here = y[8 * end : 8 * end + 8]
+        return put(y, end, jnp.where((sub == 7) & (part == groups - 1), wrap, here))
+
+    def down(x):
+        y = pltpu.roll(x, 1, 0)
+        first = y[:8]
+        wrap = turn(turn(x[8 * end : 8 * end + 8], 1, 0), -far, 1)
+        fixed = jnp.where(part == 0, wrap, turn(first, lay.wide, 1))
+        return put(y, 0, jnp.where(sub == 0, fixed, first))
+
+    return up, down
+
+
+def line_tangent(x, u, v, factors, lay, up, down):
     kn, ks, ke, kw = DIFFUSION - v, DIFFUSION + v, DIFFUSION - u, DIFFUSION + u
     return (
-        line_blend(factors, x, fields, group)
-        + (kn * north(x) + ks * south(x))
+        line_blend(factors, x, lay.fields, lay.group)
+        + (kn * up(x) + ks * down(x))
         + (ke * east_of(x) + kw * west_of(x))
     )
 
 
-def line_adjoint(x, u, v, factors, fields, group):
+def line_adjoint(x, u, v, factors, lay, up, down):
     kn, ks, ke, kw = DIFFUSION + v, DIFFUSION - v, DIFFUSION + u, DIFFUSION - u
     return (
-        line_blend(factors, x, fields, group)
-        + (north(kn * x) + south(ks * x))
+        line_blend(factors, x, lay.fields, lay.group)
+        + (up(kn * x) + down(ks * x))
         + (east_of(ke * x) + west_of(kw * x))
     )
 
 
 def inner_kernel(copies, inc, wgt, wind, hmap, mixrows, halo_rows, *refs):
     bulk = refs[:copies]
-    part, edges, wgt_edges, factors = refs[copies:]
+    part, even_base, odd_base, even_wgt, odd_wgt, factors = refs[copies:]
     fields, rows, cols = wgt.shape
     lay = Layout(fields, copies)
     tiles = [inc[f] for f in range(fields)] + [wind[0], wind[1]] + [hmap[f] for f in range(fields)]
     for ref in bulk:
         tiles += [ref[j] for j in range(lay.packet)]
     planes = [jnp.concatenate([tile, halo_rows[j]], axis=0) for j, tile in enumerate(tiles)]
+    lon_even = axis_even("lon")
+
+    def store(even_ref, odd_ref, tiles):
+        west, east = strip_lines(tiles, lay.group)
+        west, east = squeeze_lanes(west, lay.wide, lay), squeeze_lanes(east, lay.wide, lay)
+        for i, (w, e) in enumerate(zip(west, east)):
+            even_ref[pl.ds(8 * i, 8), :] = jnp.where(lon_even, e, w)
+            odd_ref[pl.ds(8 * i, 8), :] = jnp.where(lon_even, w, e)
+
     for k, members in enumerate(line_planes(lay)):
-        edges[k] = edge_line([planes[j] for j in members], lay.group)
-    wgt_edges[...] = edge_line([wgt[f] for f in range(fields)], lay.group)
+        store(even_base.at[k], odd_base.at[k], [planes[j] for j in members])
+    blank = jnp.zeros((2 * HALO, cols), F32)
+    store(even_wgt, odd_wgt, [jnp.concatenate([wgt[f], blank], axis=0) for f in range(fields)])
     above = planes[lay.own : lay.own + lay.packet]
     below = planes[-lay.packet :]
     spread = bulk[-1][2 * fields - 1, :16]
     mix, prior_mix = mixing(mixrows[:, :cols], fields), mixing(spread, fields)
     lists = []
     for maker in (mix, lambda f, g: mix(g, f), prior_mix):
-        lists += line_factors(maker, fields, lay.group)
+        lists += line_factors(maker, lay)
     for i, row in enumerate(lists):
         factors[i : i + 1] = row
     result = product(planes[: lay.own], above, below, wgt, mix, prior_mix, fields, rows)
@@ -508,60 +543,80 @@
         part[f] = result[f]
 
 
-def edge_kernel(copies, got_even, got_odd, edges, wgt_edges, factors, part, out):
+def side_kernel(copies, is_odd, got, base, wgt_line, factors, part, *refs):
     fields, rows, cols = part.shape
     lay = Layout(fields, copies)
-    blocks = rows // 8 + 1
-    group = lay.group
-    _, per = lay.groups(blocks, lay.wide)
-    lon_even = axis_even("lon")
-    even = [got_even[pl.ds(8 * i, 8), :] for i in range(per)]
-    odd = [got_odd[pl.ds(8 * i, 8), :] for i in range(per)]
-    east = spread_lanes([jnp.where(lon_even, a, b) for a, b in zip(even, odd)], blocks, lay.wide, lay)
-    west = spread_lanes([jnp.where(lon_even, b, a) for a, b in zip(even, odd)], blocks, lay.wide, lay)
-    lane = lane_iota(east.shape)
-    within = lane % SIDE % group
-    on_west = (lane < SIDE) & (within < HALO)
-    on_east = (lane >= SIDE) & (within >= group - HALO)
+    group, wide = lay.group, lay.wide
+    out = refs[1] if is_odd else refs[0]
+    on_east = axis_even("lon") != is_odd
+    msg = got[...]
+    lane, sub = lane_iota(msg.shape), sub_iota(msg.shape)
+    within = lane % wide % group
+    side = jnp.where(on_east, (within >= group - HALO).astype(jnp.int32), (within < HALO).astype(jnp.int32)) > 0
     lines = []
     for k, (spot, members) in enumerate(zip(lay.spots, line_planes(lay))):
         depth = lay.depths[members[0]]
-        left = turn(west, HALO - depth - spot, 1)
-        right = turn(east, SIDE + group - HALO - spot, 1)
-        lines.append(jnp.where(on_west, left, jnp.where(on_east, right, edges[k])))
-    clear = row_mask(rows, LANES)
-    here = lax.axis_index("win")
-    has_later = here < lax.axis_size("win") - 1
-    has_earlier = here > 0
+        moved = jnp.where(
+            on_east, turn(msg, group - HALO - spot, 1), turn(msg, HALO - depth - spot, 1)
+        )
+        lines.append(jnp.where(side, moved, base[k]))
+    row = sub + msg.shape[0] * (lane // wide)
+    here = lax.axis_index("lat")
+    from_high = (here < lax.axis_size("lat") - 1).astype(jnp.int32)
+    from_low = (here > 0).astype(jnp.int32)
+    inside = jnp.where(row < rows, 1, jnp.where(row < rows + HALO, from_high, from_low)) > 0
+
+    def clear(x):
+        return jnp.where(inside, x, 0.0)
+
+    up, down = folded(lay, rows // 8 + 1)
+    win = lax.axis_index("win")
+    has_later = win < lax.axis_size("win") - 1
+    has_earlier = win > 0
     count = 2 * fields - 1
     every = factors[...]
     mix, mix_back, mix_prior = [
         [every[g * count + i : g * count + i + 1] for i in range(count)] for g in range(3)
     ]
     inc, hmap = lines[0], lines[2]
-    u, v = line_wind(lines[1], group)
-    fwd = clear(line_tangent(inc, u, v, mix, fields, group))
-    fwd = line_tangent(fwd, u, v, mix, fields, group)
+    u, v = line_wind(lines[1], lay)
+    fwd = clear(line_tangent(inc, u, v, mix, lay, up, down))
+    fwd = line_tangent(fwd, u, v, mix, lay, up, down)
     later = lines[4] * (lines[3] - fwd)
     back = clear(hmap * fwd - jnp.where(has_later, later, 0.0))
-    back = clear(line_adjoint(back, u, v, mix_back, fields, group))
-    back = line_adjoint(back, u, v, mix_back, fields, group)
-    u, v = line_wind(lines[-1], group)
-    prior = clear(line_tangent(lines[-2], u, v, mix_prior, fields, group))
-    prior = line_tangent(prior, u, v, mix_prior, fields, group)[:rows]
-    result = wgt_edges[...] * (inc[:rows] - jnp.where(has_earlier, prior, 0.0)) + back[:rows]
-    lane = lane_iota((rows, LANES))
+    back = clear(line_adjoint(back, u, v, mix_back, lay, up, down))
+    back = line_adjoint(back, u, v, mix_back, lay, up, down)
+    u, v = line_wind(lines[-1], lay)
+    prior = clear(line_tangent(lines[-2], u, v, mix_prior, lay, up, down))
+    prior = line_tangent(prior, u, v, mix_prior, lay, up, down)
+    result = wgt_line[...] * (inc - jnp.where(has_earlier, prior, 0.0)) + back
+    per = msg.shape[0] // 8
+    lane = lane_iota((8, LANES))
+    to_west = jnp.where(on_east, 0, HALO)
+    to_east = jnp.where(on_east, LANES - HALO, LANES)
+    moves = []
     for f in range(fields):
-        low = turn(result, -(group * f + HALO), 1)
-        high = turn(result, LANES - HALO - (SIDE + group * f + group - 2 * HALO), 1)
-        whole = part[f]
-        if cols == LANES:
-            out[f] = jnp.where(lane < HALO, low, jnp.where(lane >= LANES - HALO, high, whole))
-        else:
-            out[f, :, pl.ds(0, LANES)] = jnp.where(lane < HALO, low, whole[:, :LANES])
-            for h in range(1, cols // LANES - 1):
-                out[f, :, pl.ds(h * LANES, LANES)] = whole[:, h * LANES : (h + 1) * LANES]
-            out[f, :, pl.ds(cols - LANES, LANES)] = jnp.where(lane >= LANES - HALO, high, whole[:, -LANES:])
+        for m in range(rows // 8):
+            i, at = m % per, wide * (m // per) + group * f
+            block = result[8 * i : 8 * i + 8]
+            low = turn(block, -(at + HALO), 1)
+            high = turn(block, LANES - (at + group - HALO), 1)
+            spot = pl.ds(8 * m, 8)
+            if cols == LANES:
+                whole = jnp.where(lane < to_west, low, part[f, spot, :])
+                out[f, spot, :] = jnp.where(lane >= to_east, high, whole)
+            else:
+                out[f, spot, pl.ds(0, LANES)] = jnp.where(lane < to_west, low, part[f, spot, :LANES])
+                for h in range(1, cols // LANES - 1):
+                    out[f, spot, pl.ds(h * LANES, LANES)] = part[f, spot, h * LANES : (h + 1) * LANES]
+                out[f, spot, pl.ds(cols - LANES, LANES)] = jnp.where(
+                    lane >= to_east, high, part[f, spot, cols - LANES :]
+                )
+        if is_odd:
+            moves.append(pltpu.make_async_copy(out.at[f], refs[0].at[f], refs[2].at[f]))
+            moves[-1].start()
+    for move in moves:
+        move.wait()
 
 
 def vmem():
@@ -576,14 +631,14 @@
     return pltpu.with_memory_space_constraint(array, pltpu.HBM)
 
 
-def call(kernel, in_specs, shapes, flops, scratch=()):
+def call(kernel, in_specs, shapes, flops, scratch=(), out_spec=None):
     return pl.pallas_call(
         kernel,
         scratch_shapes=scratch,
         compiler_params=pltpu.CompilerParams(vmem_limit_bytes=VMEM_LIMIT),
         out_shape=[s if isinstance(s, jax.ShapeDtypeStruct) else jax.ShapeDtypeStruct(s, F32) for s in shapes],
         in_specs=in_specs,
-        out_specs=[vmem()] * len(shapes),
+        out_specs=[out_spec or vmem()] * len(shapes),
         cost_estimate=pl.CostEstimate(flops=flops, bytes_accessed=1 << 20, transcendentals=0),
     )
 
@@ -642,17 +697,24 @@
     )(got_even, got_odd, col_low, col_high)
     got_even, got_odd = neighbour_swap(msg_even, msg_odd, "lon")
 
-    lines = len(line_planes(lay))
-    part, edges, wgt_edges, factors = call(
+    base_shape = (len(line_planes(lay)),) + col_msg
+    part, even_base, odd_base, even_wgt, odd_wgt, factors = call(
         functools.partial(inner_kernel, copies),
         [vmem()] * (6 + copies),
-        [tile, (lines, tall, LANES), (rows, LANES), (8 * -(-3 * (2 * fields - 1) // 8), LANES)],
+        [tile, base_shape, base_shape, col_msg, col_msg, (8 * -(-3 * (2 * fields - 1) // 8), LANES)],
         1 << 29,
     )(sent[0], wgt_near, wind_near, hmap, mixrows, halo_rows, *bulk)
-
+    (part,) = call(
+        functools.partial(side_kernel, copies, False), [vmem()] * 5, [tile], 1 << 28
+    )(got_even, even_base, even_wgt, factors, part)
     (out,) = call(
-        functools.partial(edge_kernel, copies), [vmem()] * 6, [tile], 1 << 25
-    )(got_even, got_odd, edges, wgt_edges, factors, part)
+        functools.partial(side_kernel, copies, True),
+        [vmem()] * 5,
+        [tile],
+        1 << 25,
+        [pltpu.VMEM(tile, F32), pltpu.SemaphoreType.DMA((fields,))],
+        hbm(),
+    )(got_odd, odd_base, odd_wgt, factors, part)
     return out[None]
 
 

time: 27.2 us -> 27.7 us (1.018)
  Pallas kernels: 6.15 us -> 6.85 us
  starting transfers between devices: 9.31 us -> 8.86 us
    ppermute x2, starting transfers between devices: 1.85 us -> 0.07 us  [neighbour_swap(): from_even = lax.ppermute(even_msg, axis, even_pairs(n))]
    ppermute x2, waiting for transfers between devices: 0.01 us -> 1.78 us  [neighbour_swap(): from_even = lax.ppermute(even_msg, axis, even_pairs(n))]
    ppermute x2, waiting for transfers between devices: 3.23 us -> 1.68 us  [neighbour_swap(): from_odd = lax.ppermute(odd_msg, axis, odd_pairs(n))]
    ppermute x2, starting transfers between devices: 4.33 us -> 5.66 us  [neighbour_swap(): from_odd = lax.ppermute(odd_msg, axis, odd_pairs(n))]
    pallas_call x1, Pallas kernels: 1.45 us -> 1.9 us  [per_device(): call(functools.partial(inner_kernel, copies), [vmem()] * (6 + copies), [t...]
    pallas_call x1 -> x2, Pallas kernels: 1.62 us -> 1.86 us  [the longest x1 1.26 us: per_device(): call(functools.partial(side_kernel, copies, True), [vmem()] * 5, [tile],...]
  transfers between devices with their start and end apart: 6 -> 6, of which waited for: 3 -> 3; matrix products, arithmetic and copies ran while one was open for 0% -> 0% of each run, Pallas kernels for 12% -> 16%
where the time goes in v5:
time: 27.7 us; the launch traced here: 27.5 us
  waiting for transfers between devices  11.7 us (42%)
  starting transfers between devices  8.86 us (32%)
  Pallas kernels  6.85 us (25%)
    ppermute x2, waiting for transfers between devices, window_swap(): got = lax.ppermute(down, 'win', even_pairs(n))  8.26 us
    ppermute x2, starting transfers between devices, neighbour_swap(): from_odd = lax.ppermute(odd_msg, axis, odd_pairs(n))  5.66 us
    ppermute x2, starting transfers between devices, window_swap(): got = lax.ppermute(down, 'win', even_pairs(n))  3.13 us
    pallas_call x1, Pallas kernels, per_device(): call(functools.partial(inner_kernel, copies), [vmem()] * (6 + copies), [t...  1.9 us
    ppermute x2, waiting for transfers between devices, neighbour_swap(): from_even = lax.ppermute(even_msg, axis, even_pairs(n))  1.78 us
    ppermute x2, waiting for transfers between devices, neighbour_swap(): from_odd = lax.ppermute(odd_msg, axis, odd_pairs(n))  1.68 us
    pallas_call x1, Pallas kernels, per_device(): call(functools.partial(own_kernel, copies), [vmem()] + [hbm()] * 4, [wind...  1.48 us
    pallas_call x1, Pallas kernels, per_device(): call(functools.partial(side_kernel, copies, True), [vmem()] * 5, [tile],...  1.26 us
  transfers between devices with their start and end apart: 6, of which 3 were waited for; matrix products, arithmetic and copies ran while one was open for 0% of the time, Pallas kernels for 16%

profile of v5, /device:TPU:0, one launch (start us, length us, event | category | flops | bytes accessed | tf_op | source)
XLA Modules:
  0.0 27.5 jit_solution(7470866678850940527)
XLA Ops:
  0.0 1.3 %shard_map.64 = (f32[16,256]{1,0:T(8,128)S(1)}, f32[6,64,256]{2,1,0:T(8,128)S(1)}, f32[64,128]{1,0:T(8,128)S(1)}) custom-call(f32[3,64,256]{2,1,0:T(8,128)} %bitcast.7, f32[3,64,256]{2,1,0:T(8,128)} %bitcast.8, f32[2,64,256]{2,1,0:T(8,128)} %bitcast.10, f32[3,1,3]{2,1,0:T(1,128)} %bitcast.12), custom_call_target="tpu_custom_call" | custom-call | flops 1048576 | bytes 1048576 | tf_op jit(solution)/shard_map/pallas_call | solution.py:668
  1.3 3.0 %collective-permute-start.4 = (f32[6,64,256]{2,1,0:T(8,128)S(1)}, f32[6,64,256]{2,1,0:T(8,128)S(1)}, u32[]{:S(2)}, u32[]{:S(2)}) collective-permute-start(f32[6,64,256]{2,1,0:T(8,128)S(1)} %get-tuple-element.28.bulk.inc), channel_id=1, source_target_pairs={{0,16},{16,0},{1,17},{17,1},{2,18},{18,2},{3,19},{19,3},{4,20},{20... | collective-permute-start | bytes 1179656 | tf_op jit(solution)/shard_map/ppermute | solution.py:40
  4.3 0.1 collective-permute-start
  4.4 1.5 %shard_map.65 = (f32[2,64,256]{2,1,0:T(8,128)S(1)}, f32[3,64,256]{2,1,0:T(8,128)S(1)}, f32[3,64,256]{2,1,0:T(8,128)S(1)}, f32[40,256]{1,0:T(8,128)S(1)}, f32[40,...) custom-call(f32[6,64,256]{2,1,0:T(8,128)S(1)} %get-tuple-element.28.bulk.inc, ...), custom_call_target="tpu_custom_call" | custom-call | flops 536870912 | bytes 1048576 | tf_op jit(solution)/shard_map/pallas_call | solution.py:679
  5.9 8.3 %collective-permute-done.refs_4_ = f32[64,128]{1,0:T(8,128)S(1)} collective-permute-done((f32[64,128]{1,0:T(8,128)S(1)}, f32[64,128]{1,0:T(8,128)S(1)}, u32[]{:S(2)}, u32[]{:S(2)}) %collective-permute-start) | collective-permute-done | bytes 32800 | tf_op jit(solution)/shard_map/ppermute | solution.py:40
  14.1 0.2 shard_map.66
  14.3 0.1 collective-permute-start.1
  14.4 1.9 %collective-permute-start.2 = (f32[40,256]{1,0:T(8,128)S(1)}, f32[40,256]{1,0:T(8,128)S(1)}, u32[]{:S(2)}, u32[]{:S(2)}) collective-permute-start(f32[40,256]{1,0:T(8,128)S(1)} %get-tuple-element.35), channel_id=1, source_target_pairs={{0,12},{4,8},{8,4},{12,0},{1,13},{5,9},{9,5},{13,1},{2,14},{6,10},... | collective-permute-start | bytes 122888 | tf_op jit(solution)/shard_map/ppermute | solution.py:33
  16.3 0.0 collective-permute-done.1.got_even
  16.3 1.7 %collective-permute-done.2.got_odd = f32[40,256]{1,0:T(8,128)S(1)} collective-permute-done((f32[40,256]{1,0:T(8,128)S(1)}, f32[40,256]{1,0:T(8,128)S(1)}, u32[]{:S(2)}, u32[]{:S(2)}) %collective-permute-start.2) | collective-permute-done | bytes 40992 | tf_op jit(solution)/shard_map/ppermute | solution.py:33
  17.9 0.2 shard_map.67
  18.1 3.8 %collective-permute-start.3 = (f32[24,128]{1,0:T(8,128)S(1)}, f32[24,128]{1,0:T(8,128)S(1)}, u32[]{:S(2)}, u32[]{:S(2)}) collective-permute-start(f32[24,128]{1,0:T(8,128)S(1)} %get-tuple-element.38), channel_id=1, source_target_pairs={{0,3},{1,2},{2,1},{3,0},{4,7},{5,6},{6,5},{7,4},{8,11},{9,10},{10,... | collective-permute-start | bytes 36872 | tf_op jit(solution)/shard_map/ppermute | solution.py:33
  21.9 0.0 collective-permute-start.5
  21.9 0.0 collective-permute-done.4.refs_0_
  21.9 1.9 %shard_map.68 = (f32[3,64,256]{2,1,0:T(8,128)S(1)}, f32[5,24,128]{2,1,0:T(8,128)S(1)}, f32[5,24,128]{2,1,0:T(8,128)S(1)}, f32[24,128]{1,0:T(8,128)S(1)}, f32[24,128]{1,0:T(8,128)S(1)}, /*index=5*/f32[16,128]{1,0:T(8,128)S(1)}) custom-call(f32[6,64,256]{2,1,0:T(8,128)S(1)} %get-tuple-element.28.bulk.inc, f32[3,64,256]{2,1,0:T(8,128)S(1)} %get-tuple-element.39.wgt, ...), custom_call_target="tpu_custom_call" | custom-call | flops 536870912 | bytes 1048576 | tf_op jit(solution)/shard_map/pallas_call | solution.py:701
  23.8 1.8 %collective-permute-done.5.got = f32[24,128]{1,0:T(8,128)S(1)} collective-permute-done((f32[24,128]{1,0:T(8,128)S(1)}, f32[24,128]{1,0:T(8,128)S(1)}, u32[]{:S(2)}, u32[]{:S(2)}) %collective-permute-start.5) | collective-permute-done | bytes 12320 | tf_op jit(solution)/shard_map/ppermute | solution.py:32
  25.6 0.6 %shard_map.69.part = f32[3,64,256]{2,1,0:T(8,128)S(1)} custom-call(f32[24,128]{1,0:T(8,128)S(1)} %collective-permute-done.5.got, f32[5,24,128]{2,1,0:T(8,128)S(1)} %get-tuple-element.48.base, f32[24,128]{1,0:T(8,128)S(1)} %get-tuple-element.49.wgt_line, f32[16,128]{1,0:T(8,128)S(1)} %get-tuple-element.46.factors, f32[3,64,256]{2,1,0:T(8,128)S(1)} %get-tuple-element.50.part), custom_call_target="tpu_custom_call" | custom-call | flops 268435456 | bytes 1048576 | tf_op jit(solution)/shard_map/pallas_call | solution.py:707
  26.2 0.0 collective-permute-done.3.got
  26.2 1.3 %shard_map.70 = f32[3,64,256]{2,1,0:T(8,128)} custom-call(f32[24,128]{1,0:T(8,128)S(1)} %collective-permute-done.3.got, f32[5,24,128]{2,1,0:T(8,128)S(1)} %get-tuple-element.44.base, f32[24,128]{1,0:T(8,128)S(1)} %get-tuple-element.45.wgt_line, f32[16,128]{1,0:T(8,128)S(1)} %get-tuple-element.46.factors, f32[3,64,256]{2,1,0:T(8,128)S(1)} %shard_map.69.part), custom_call_target="tpu_custom_call" | custom-call | flops 33554432 | bytes 1048576 | tf_op jit(solution)/shard_map/pallas_call | solution.py:710
Async XLA Ops:
  1.3 20.7 %collective-permute-start.4 = (f32[6,64,256]{2,1,0:T(8,128)S(1)}, f32[6,64,256]{2,1,0:T(8,128)S(1)}, u32[]{:S(2)}, u32[]{:S(2)}) collective-permute-start(f32[6,64,256]{2,1,0:T(8,128)S(1)} %get-tuple-element.28.bulk.inc), channel_id=1, source_target_pairs={{0,16},{16,0},{1,17},{17,1},{2,18},{18,2},{3,19},{19,3},{4,20},{20... | collective-permute-start | bytes 1179656 | tf_op jit(solution)/shard_map/ppermute | solution.py:40
  4.3 9.8 %collective-permute-start = (f32[64,128]{1,0:T(8,128)S(1)}, f32[64,128]{1,0:T(8,128)S(1)}, u32[]{:S(2)}, u32[]{:S(2)}) collective-permute-start(f32[64,128]{1,0:T(8,128)S(1)} %get-tuple-element.33), channel_id=1, source_target_pairs={{0,16},{16,0},{1,17},{17,1},{2,18},{18,2},{3,19},{19,3},{4,20},{20... | collective-permute-start | bytes 98312 | tf_op jit(solution)/shard_map/ppermute | solution.py:40
  14.3 1.9 %collective-permute-start.1 = (f32[40,256]{1,0:T(8,128)S(1)}, f32[40,256]{1,0:T(8,128)S(1)}, u32[]{:S(2)}, u32[]{:S(2)}) collective-permute-start(f32[40,256]{1,0:T(8,128)S(1)} %get-tuple-element.34), channel_id=1, source_target_pairs={{0,4},{4,0},{8,12},{12,8},{1,5},{5,1},{9,13},{13,9},{2,6},{6,2},{1... | collective-permute-start | bytes 122888 | tf_op jit(solution)/shard_map/ppermute | solution.py:32
  14.4 3.5 %collective-permute-start.2 = (f32[40,256]{1,0:T(8,128)S(1)}, f32[40,256]{1,0:T(8,128)S(1)}, u32[]{:S(2)}, u32[]{:S(2)}) collective-permute-start(f32[40,256]{1,0:T(8,128)S(1)} %get-tuple-element.35), channel_id=1, source_target_pairs={{0,12},{4,8},{8,4},{12,0},{1,13},{5,9},{9,5},{13,1},{2,14},{6,10},... | collective-permute-start | bytes 122888 | tf_op jit(solution)/shard_map/ppermute | solution.py:33
  18.1 8.1 %collective-permute-start.3 = (f32[24,128]{1,0:T(8,128)S(1)}, f32[24,128]{1,0:T(8,128)S(1)}, u32[]{:S(2)}, u32[]{:S(2)}) collective-permute-start(f32[24,128]{1,0:T(8,128)S(1)} %get-tuple-element.38), channel_id=1, source_target_pairs={{0,3},{1,2},{2,1},{3,0},{4,7},{5,6},{6,5},{7,4},{8,11},{9,10},{10,... | collective-permute-start | bytes 36872 | tf_op jit(solution)/shard_map/ppermute | solution.py:33
  21.9 3.7 %collective-permute-start.5 = (f32[24,128]{1,0:T(8,128)S(1)}, f32[24,128]{1,0:T(8,128)S(1)}, u32[]{:S(2)}, u32[]{:S(2)}) collective-permute-start(f32[24,128]{1,0:T(8,128)S(1)} %get-tuple-element.47), channel_id=1, source_target_pairs={{0,1},{1,0},{2,3},{3,2},{4,5},{5,4},{6,7},{7,6},{8,9},{9,8},{10,11... | collective-permute-start | bytes 36872 | tf_op jit(solution)/shard_map/ppermute | solution.py:32

commit v6 on v5

--- a/solution.py
+++ b/solution.py
@@ -250,30 +250,22 @@
 
 
 def join_kernel(fields, copies, *refs):
-    row_first, row_last, col_low, col_high = refs[:4]
-    strips = refs[4 : 4 + copies]
-    row_even, row_odd, low_out, high_out = refs[4 + copies :]
+    row_first, row_last = refs[:2]
+    strips = refs[2 : 2 + copies]
+    row_even, row_odd = refs[2 + copies :]
     lay = Layout(fields, copies)
-    rows, cols = col_low.shape[0], row_first.shape[1]
+    cols = row_first.shape[1]
     halves = cols // LANES
-    strip_blocks = -(-4 * lay.packet // 8)
-    first_pieces, last_pieces, low_pieces, high_pieces = [], [], [], []
+    first_pieces, last_pieces = [], []
     for k, ref in enumerate(strips):
         blocks = [
             jnp.concatenate([ref[pl.ds(8 * (m * halves + h), 8), :] for h in range(halves)], axis=1)
-            for m in range(strip_blocks)
+            for m in range(-(-4 * lay.packet // 8))
         ]
-        _, per = lay.groups(rows // 8, 4 * lay.packet)
-        base = 8 * strip_blocks * halves
-        tight = [ref[pl.ds(base + 8 * i, 8), :] for i in range(per)]
-        wide = spread_lanes(tight, rows // 8, 4 * lay.packet, lay)
         for j in range(lay.packet):
             at = lay.starts[lay.own + k * lay.packet + j]
             first_pieces.append((blocks[4 * j // 8], 4 * j % 8, at, RIM))
             last_pieces.append((blocks[4 * j // 8], 4 * j % 8 + 2, at, RIM))
-            at = lay.lanes[lay.own + k * lay.packet + j]
-            low_pieces.append((wide, 4 * j, at, RIM))
-            high_pieces.append((wide, 4 * j + 2, at, RIM))
     is_even = axis_even("lat")
     own_used = lay.starts[lay.own]
     first = pack_rows(first_pieces, lay.row_blocks)
@@ -285,8 +277,31 @@
             a, b = jnp.where(other, first[m], a), jnp.where(other, last[m], b)
         row_even[pl.ds(8 * m, 8), :] = jnp.where(is_even, b, a)
         row_odd[pl.ds(8 * m, 8), :] = jnp.where(is_even, a, b)
-    low_out[...] = pack_lanes(low_pieces, col_low[...])
-    high_out[...] = pack_lanes(high_pieces, col_high[...])
+
+
+def cols_kernel(fields, copies, *refs):
+    col_low, col_high = refs[:2]
+    strips = refs[2 : 2 + copies]
+    even_out, odd_out = refs[2 + copies :]
+    lay = Layout(fields, copies)
+    rows = col_low.shape[0]
+    low_pieces, high_pieces = [], []
+    for k, ref in enumerate(strips):
+        _, per = lay.groups(rows // 8, 4 * lay.packet)
+        base = ref.shape[0] - 8 * per
+        tight = [ref[pl.ds(base + 8 * i, 8), :] for i in range(per)]
+        wide = spread_lanes(tight, rows // 8, 4 * lay.packet, lay)
+        for j in range(lay.packet):
+            at = lay.lanes[lay.own + k * lay.packet + j]
+            low_pieces.append((wide, 4 * j, at, RIM))
+            high_pieces.append((wide, 4 * j + 2, at, RIM))
+    lon_even = axis_even("lon")
+    low = pack_lanes(low_pieces, col_low[...])
+    high = pack_lanes(high_pieces, col_high[...])
+    blank = jnp.zeros((8, LANES), F32)
+    for ref, x in ((even_out, jnp.where(lon_even, high, low)), (odd_out, jnp.where(lon_even, low, high))):
+        for i, block in enumerate(squeeze_lanes(jnp.concatenate([x, blank], axis=0), lay.wide, lay)):
+            ref[pl.ds(8 * i, 8), :] = block
 
 
 def lat_inside(width):
@@ -297,7 +312,7 @@
     return jnp.where(upper, from_high, from_low) > 0
 
 
-def rows_kernel(fields, copies, got_even, got_odd, col_low, col_high, halo_rows, msg_even, msg_odd):
+def rows_kernel(fields, copies, tail, got_even, got_odd, even_tile, odd_tile, halo_rows, msg_even, msg_odd):
     lay = Layout(fields, copies)
     cols = got_even.shape[-1]
     is_even = axis_even("lat")
@@ -320,12 +335,19 @@
     where = list(zip(blocks, lay.lanes, lay.depths))
     low_tail = pack_lanes([(x[:, :LANES], 0, at, d) for x, at, d in where])
     high_tail = pack_lanes([(x[:, -LANES:], LANES - d, at, d) for x, at, d in where])
-    low_all = squeeze_lanes(jnp.concatenate([col_low[...], low_tail], axis=0), lay.wide, lay)
-    high_all = squeeze_lanes(jnp.concatenate([col_high[...], high_tail], axis=0), lay.wide, lay)
     lon_even = axis_even("lon")
-    for m, (a, b) in enumerate(zip(low_all, high_all)):
-        msg_even[pl.ds(8 * m, 8), :] = jnp.where(lon_even, b, a)
-        msg_odd[pl.ds(8 * m, 8), :] = jnp.where(lon_even, a, b)
+    per = even_tile.shape[0] // 8
+    shift = lay.wide * (tail // per)
+    lane = lane_iota((8, LANES))
+    for ref, tile, x in (
+        (msg_even, even_tile, jnp.where(lon_even, high_tail, low_tail)),
+        (msg_odd, odd_tile, jnp.where(lon_even, low_tail, high_tail)),
+    ):
+        for i in range(per):
+            block = tile[pl.ds(8 * i, 8), :]
+            if i == tail % per:
+                block = jnp.where((lane >= shift) & (lane < shift + lay.wide), turn(x, shift, 1), block)
+            ref[pl.ds(8 * i, 8), :] = block
 
 
 def row_mask(rows, width):
@@ -684,17 +706,20 @@
         [pltpu.VMEM(cells.shape, jnp.int32), pltpu.VMEM(scale.shape, F32), pltpu.SemaphoreType.DMA((4,))],
     )(sent[0], far(wind), far(wgt), far(cells), far(scale))
 
-    row_even, row_odd, col_low, col_high = call(
-        functools.partial(join_kernel, fields, copies),
-        [vmem()] * (4 + copies),
-        [row_msg, row_msg, (rows, LANES), (rows, LANES)],
+    row_even, row_odd = call(
+        functools.partial(join_kernel, fields, copies), [vmem()] * (2 + copies), [row_msg, row_msg], 1 << 16
+    )(row_first, row_last, *strips)
+    got_even, got_odd = neighbour_swap(row_even, row_odd, "lat")
+    even_tile, odd_tile = call(
+        functools.partial(cols_kernel, fields, copies), [vmem()] * (2 + copies), [col_msg, col_msg], 1 << 28
+    )(col_low, col_high, *strips)
+
+    halo_rows, msg_even, msg_odd = call(
+        functools.partial(rows_kernel, fields, copies, rows // 8),
+        [vmem()] * 4,
+        [(lay.count, 8, cols), col_msg, col_msg],
         1 << 16,
-    )(row_first, row_last, col_low, col_high, *strips)
-    got_even, got_odd = neighbour_swap(row_even, row_odd, "lat")
-
-    halo_rows, msg_even, msg_odd = call(
-        functools.partial(rows_kernel, fields, copies), [vmem()] * 4, [(lay.count, 8, cols), col_msg, col_msg], 1 << 16
-    )(got_even, got_odd, col_low, col_high)
+    )(got_even, got_odd, even_tile, odd_tile)
     got_even, got_odd = neighbour_swap(msg_even, msg_odd, "lon")
 
     base_shape = (len(line_planes(lay)),) + col_msg

time: 27.7 us -> 27.5 us (level)
  no operation moved by 1% of the time
where the time goes in v6:
time: 27.5 us; the launch traced here: 27.3 us
  waiting for transfers between devices  11.5 us (42%)
  starting transfers between devices  8.85 us (32%)
  Pallas kernels  6.93 us (25%)
    ppermute x2, waiting for transfers between devices, window_swap(): got = lax.ppermute(down, 'win', even_pairs(n))  8.26 us
    ppermute x2, starting transfers between devices, neighbour_swap(): from_odd = lax.ppermute(odd_msg, axis, odd_pairs(n))  5.65 us
    ppermute x2, starting transfers between devices, window_swap(): got = lax.ppermute(down, 'win', even_pairs(n))  3.13 us
    pallas_call x1, Pallas kernels, per_device(): call(functools.partial(inner_kernel, copies), [vmem()] * (6 + copies), [t...  1.91 us
    ppermute x2, waiting for transfers between devices, neighbour_swap(): from_even = lax.ppermute(even_msg, axis, even_pairs(n))  1.77 us
    pallas_call x1, Pallas kernels, per_device(): call(functools.partial(own_kernel, copies), [vmem()] + [hbm()] * 4, [wind...  1.48 us
    ppermute x2, waiting for transfers between devices, neighbour_swap(): from_odd = lax.ppermute(odd_msg, axis, odd_pairs(n))  1.43 us
    pallas_call x1, Pallas kernels, per_device(): call(functools.partial(side_kernel, copies, True), [vmem()] * 5, [tile],...  1.26 us
  transfers between devices with their start and end apart: 6, of which 3 were waited for; matrix products, arithmetic and copies ran while one was open for 0% of the time, Pallas kernels for 16%

profile of v6, /device:TPU:0, one launch (start us, length us, event | category | flops | bytes accessed | tf_op | source)
XLA Modules:
  0.0 27.3 jit_solution(17161641673679652480)
XLA Ops:
  0.0 1.3 %shard_map.64 = (f32[16,256]{1,0:T(8,128)S(1)}, f32[6,64,256]{2,1,0:T(8,128)S(1)}, f32[64,128]{1,0:T(8,128)S(1)}) custom-call(f32[3,64,256]{2,1,0:T(8,128)} %bitcast.7, f32[3,64,256]{2,1,0:T(8,128)} %bitcast.8, f32[2,64,256]{2,1,0:T(8,128)} %bitcast.10, f32[3,1,3]{2,1,0:T(1,128)} %bitcast.12), custom_call_target="tpu_custom_call" | custom-call | flops 1048576 | bytes 1048576 | tf_op jit(solution)/shard_map/pallas_call | solution.py:690
  1.3 3.0 %collective-permute-start.4 = (f32[6,64,256]{2,1,0:T(8,128)S(1)}, f32[6,64,256]{2,1,0:T(8,128)S(1)}, u32[]{:S(2)}, u32[]{:S(2)}) collective-permute-start(f32[6,64,256]{2,1,0:T(8,128)S(1)} %get-tuple-element.28.bulk.inc), channel_id=1, source_target_pairs={{0,16},{16,0},{1,17},{17,1},{2,18},{18,2},{3,19},{19,3},{4,20},{20... | collective-permute-start | bytes 1179656 | tf_op jit(solution)/shard_map/ppermute | solution.py:40
  4.3 0.1 collective-permute-start
  4.4 1.5 %shard_map.65 = (f32[2,64,256]{2,1,0:T(8,128)S(1)}, f32[3,64,256]{2,1,0:T(8,128)S(1)}, f32[3,64,256]{2,1,0:T(8,128)S(1)}, f32[40,256]{1,0:T(8,128)S(1)}, f32[40,...) custom-call(f32[6,64,256]{2,1,0:T(8,128)S(1)} %get-tuple-element.28.bulk.inc, ...), custom_call_target="tpu_custom_call" | custom-call | flops 536870912 | bytes 1048576 | tf_op jit(solution)/shard_map/pallas_call | solution.py:701
  5.9 8.3 %collective-permute-done.refs_2_ = f32[64,128]{1,0:T(8,128)S(1)} collective-permute-done((f32[64,128]{1,0:T(8,128)S(1)}, f32[64,128]{1,0:T(8,128)S(1)}, u32[]{:S(2)}, u32[]{:S(2)}) %collective-permute-start) | collective-permute-done | bytes 32800 | tf_op jit(solution)/shard_map/ppermute | solution.py:40
  14.2 0.1 collective-permute-start.1
  14.2 1.9 %collective-permute-start.2 = (f32[40,256]{1,0:T(8,128)S(1)}, f32[40,256]{1,0:T(8,128)S(1)}, u32[]{:S(2)}, u32[]{:S(2)}) collective-permute-start(f32[40,256]{1,0:T(8,128)S(1)} %get-tuple-element.33), channel_id=1, source_target_pairs={{0,12},{4,8},{8,4},{12,0},{1,13},{5,9},{9,5},{13,1},{2,14},{6,10},... | collective-permute-start | bytes 122888 | tf_op jit(solution)/shard_map/ppermute | solution.py:33
  16.1 0.2 shard_map.67
  16.3 0.0 collective-permute-done.1.got_even
  16.3 1.4 %collective-permute-done.2.got_odd = f32[40,256]{1,0:T(8,128)S(1)} collective-permute-done((f32[40,256]{1,0:T(8,128)S(1)}, f32[40,256]{1,0:T(8,128)S(1)}, u32[]{:S(2)}, u32[]{:S(2)}) %collective-permute-start.2) | collective-permute-done | bytes 40992 | tf_op jit(solution)/shard_map/ppermute | solution.py:33
  17.8 0.2 shard_map.68
  17.9 3.8 %collective-permute-start.3 = (f32[24,128]{1,0:T(8,128)S(1)}, f32[24,128]{1,0:T(8,128)S(1)}, u32[]{:S(2)}, u32[]{:S(2)}) collective-permute-start(f32[24,128]{1,0:T(8,128)S(1)} %get-tuple-element.38), channel_id=1, source_target_pairs={{0,3},{1,2},{2,1},{3,0},{4,7},{5,6},{6,5},{7,4},{8,11},{9,10},{10,... | collective-permute-start | bytes 36872 | tf_op jit(solution)/shard_map/ppermute | solution.py:33
  21.7 0.0 collective-permute-start.5
  21.7 0.0 collective-permute-done.4.refs_0_
  21.7 1.9 %shard_map.69 = (f32[3,64,256]{2,1,0:T(8,128)S(1)}, f32[5,24,128]{2,1,0:T(8,128)S(1)}, f32[5,24,128]{2,1,0:T(8,128)S(1)}, f32[24,128]{1,0:T(8,128)S(1)}, f32[24,128]{1,0:T(8,128)S(1)}, /*index=5*/f32[16,128]{1,0:T(8,128)S(1)}) custom-call(f32[6,64,256]{2,1,0:T(8,128)S(1)} %get-tuple-element.28.bulk.inc, f32[3,64,256]{2,1,0:T(8,128)S(1)} %get-tuple-element.39.wgt, ...), custom_call_target="tpu_custom_call" | custom-call | flops 536870912 | bytes 1048576 | tf_op jit(solution)/shard_map/pallas_call | solution.py:726
  23.7 1.8 %collective-permute-done.5.got = f32[24,128]{1,0:T(8,128)S(1)} collective-permute-done((f32[24,128]{1,0:T(8,128)S(1)}, f32[24,128]{1,0:T(8,128)S(1)}, u32[]{:S(2)}, u32[]{:S(2)}) %collective-permute-start.5) | collective-permute-done | bytes 12320 | tf_op jit(solution)/shard_map/ppermute | solution.py:32
  25.4 0.6 %shard_map.70.part = f32[3,64,256]{2,1,0:T(8,128)S(1)} custom-call(f32[24,128]{1,0:T(8,128)S(1)} %collective-permute-done.5.got, f32[5,24,128]{2,1,0:T(8,128)S(1)} %get-tuple-element.48.base, f32[24,128]{1,0:T(8,128)S(1)} %get-tuple-element.49.wgt_line, f32[16,128]{1,0:T(8,128)S(1)} %get-tuple-element.46.factors, f32[3,64,256]{2,1,0:T(8,128)S(1)} %get-tuple-element.50.part), custom_call_target="tpu_custom_call" | custom-call | flops 268435456 | bytes 1048576 | tf_op jit(solution)/shard_map/pallas_call | solution.py:732
  26.0 0.0 collective-permute-done.3.got
  26.0 1.3 %shard_map.71 = f32[3,64,256]{2,1,0:T(8,128)} custom-call(f32[24,128]{1,0:T(8,128)S(1)} %collective-permute-done.3.got, f32[5,24,128]{2,1,0:T(8,128)S(1)} %get-tuple-element.44.base, f32[24,128]{1,0:T(8,128)S(1)} %get-tuple-element.45.wgt_line, f32[16,128]{1,0:T(8,128)S(1)} %get-tuple-element.46.factors, f32[3,64,256]{2,1,0:T(8,128)S(1)} %shard_map.70.part), custom_call_target="tpu_custom_call" | custom-call | flops 33554432 | bytes 1048576 | tf_op jit(solution)/shard_map/pallas_call | solution.py:735
  (1 shorter events, 0.0 us)
Async XLA Ops:
  1.3 20.5 %collective-permute-start.4 = (f32[6,64,256]{2,1,0:T(8,128)S(1)}, f32[6,64,256]{2,1,0:T(8,128)S(1)}, u32[]{:S(2)}, u32[]{:S(2)}) collective-permute-start(f32[6,64,256]{2,1,0:T(8,128)S(1)} %get-tuple-element.28.bulk.inc), channel_id=1, source_target_pairs={{0,16},{16,0},{1,17},{17,1},{2,18},{18,2},{3,19},{19,3},{4,20},{20... | collective-permute-start | bytes 1179656 | tf_op jit(solution)/shard_map/ppermute | solution.py:40
  4.3 9.8 %collective-permute-start = (f32[64,128]{1,0:T(8,128)S(1)}, f32[64,128]{1,0:T(8,128)S(1)}, u32[]{:S(2)}, u32[]{:S(2)}) collective-permute-start(f32[64,128]{1,0:T(8,128)S(1)} %get-tuple-element.31), channel_id=1, source_target_pairs={{0,16},{16,0},{1,17},{17,1},{2,18},{18,2},{3,19},{19,3},{4,20},{20... | collective-permute-start | bytes 98312 | tf_op jit(solution)/shard_map/ppermute | solution.py:40
  14.2 2.2 %collective-permute-start.1 = (f32[40,256]{1,0:T(8,128)S(1)}, f32[40,256]{1,0:T(8,128)S(1)}, u32[]{:S(2)}, u32[]{:S(2)}) collective-permute-start(f32[40,256]{1,0:T(8,128)S(1)} %get-tuple-element.32), channel_id=1, source_target_pairs={{0,4},{4,0},{8,12},{12,8},{1,5},{5,1},{9,13},{13,9},{2,6},{6,2},{1... | collective-permute-start | bytes 122888 | tf_op jit(solution)/shard_map/ppermute | solution.py:32
  14.2 3.5 %collective-permute-start.2 = (f32[40,256]{1,0:T(8,128)S(1)}, f32[40,256]{1,0:T(8,128)S(1)}, u32[]{:S(2)}, u32[]{:S(2)}) collective-permute-start(f32[40,256]{1,0:T(8,128)S(1)} %get-tuple-element.33), channel_id=1, source_target_pairs={{0,12},{4,8},{8,4},{12,0},{1,13},{5,9},{9,5},{13,1},{2,14},{6,10},... | collective-permute-start | bytes 122888 | tf_op jit(solution)/shard_map/ppermute | solution.py:33
  17.9 8.1 %collective-permute-start.3 = (f32[24,128]{1,0:T(8,128)S(1)}, f32[24,128]{1,0:T(8,128)S(1)}, u32[]{:S(2)}, u32[]{:S(2)}) collective-permute-start(f32[24,128]{1,0:T(8,128)S(1)} %get-tuple-element.38), channel_id=1, source_target_pairs={{0,3},{1,2},{2,1},{3,0},{4,7},{5,6},{6,5},{7,4},{8,11},{9,10},{10,... | collective-permute-start | bytes 36872 | tf_op jit(solution)/shard_map/ppermute | solution.py:33
  21.7 3.7 %collective-permute-start.5 = (f32[24,128]{1,0:T(8,128)S(1)}, f32[24,128]{1,0:T(8,128)S(1)}, u32[]{:S(2)}, u32[]{:S(2)}) collective-permute-start(f32[24,128]{1,0:T(8,128)S(1)} %get-tuple-element.47), channel_id=1, source_target_pairs={{0,1},{1,0},{2,3},{3,2},{4,5},{5,4},{6,7},{7,6},{8,9},{9,8},{10,11... | collective-permute-start | bytes 36872 | tf_op jit(solution)/shard_map/ppermute | solution.py:32

commit v7 on v6

--- a/solution.py
+++ b/solution.py
@@ -571,6 +571,22 @@
     group, wide = lay.group, lay.wide
     out = refs[1] if is_odd else refs[0]
     on_east = axis_even("lon") != is_odd
+    split = is_odd and cols > LANES
+    if split:
+        out_far, sems = refs[0], refs[2]
+
+        def ready(start):
+            lanes = pl.ds(start, cols - LANES)
+            return pltpu.make_async_copy(part.at[:, :, lanes], out_far.at[:, :, lanes], sems.at[fields])
+
+        def changed(f, start):
+            return pltpu.make_async_copy(out.at[f], out_far.at[f, :, pl.ds(start, LANES)], sems.at[f])
+
+        def by_side(east, west):
+            pl.when(on_east)(east)
+            pl.when(jnp.logical_not(on_east))(west)
+
+        by_side(lambda: ready(0).start(), lambda: ready(LANES).start())
     msg = got[...]
     lane, sub = lane_iota(msg.shape), sub_iota(msg.shape)
     within = lane % wide % group
@@ -624,7 +640,11 @@
             low = turn(block, -(at + HALO), 1)
             high = turn(block, LANES - (at + group - HALO), 1)
             spot = pl.ds(8 * m, 8)
-            if cols == LANES:
+            if split:
+                west = jnp.where(lane < to_west, low, part[f, spot, :LANES])
+                east = jnp.where(lane >= to_east, high, part[f, spot, cols - LANES :])
+                out[f, spot, :] = jnp.where(on_east, east, west)
+            elif cols == LANES:
                 whole = jnp.where(lane < to_west, low, part[f, spot, :])
                 out[f, spot, :] = jnp.where(lane >= to_east, high, whole)
             else:
@@ -634,11 +654,19 @@
                 out[f, spot, pl.ds(cols - LANES, LANES)] = jnp.where(
                     lane >= to_east, high, part[f, spot, cols - LANES :]
                 )
-        if is_odd:
+        if split:
+            by_side(
+                lambda f=f: changed(f, cols - LANES).start(), lambda f=f: changed(f, 0).start()
+            )
+        elif is_odd:
             moves.append(pltpu.make_async_copy(out.at[f], refs[0].at[f], refs[2].at[f]))
             moves[-1].start()
     for move in moves:
         move.wait()
+    if split:
+        for f in range(fields):
+            by_side(lambda f=f: changed(f, cols - LANES).wait(), lambda f=f: changed(f, 0).wait())
+        by_side(lambda: ready(0).wait(), lambda: ready(LANES).wait())
 
 
 def vmem():
@@ -737,7 +765,7 @@
         [vmem()] * 5,
         [tile],
         1 << 25,
-        [pltpu.VMEM(tile, F32), pltpu.SemaphoreType.DMA((fields,))],
+        [pltpu.VMEM((fields, rows, min(cols, LANES)), F32), pltpu.SemaphoreType.DMA((fields + 1,))],
         hbm(),
     )(got_odd, odd_base, odd_wgt, factors, part)
     return out[None]

time: 27.5 us -> 27.5 us (level)
  no operation moved by 1% of the time
where the time goes in v7:
time: 27.5 us; the launch traced here: 27.3 us
  waiting for transfers between devices  11.5 us (42%)
  starting transfers between devices  8.85 us (32%)
  Pallas kernels  6.92 us (25%)
    ppermute x2, waiting for transfers between devices, window_swap(): got = lax.ppermute(down, 'win', even_pairs(n))  8.26 us
    ppermute x2, starting transfers between devices, neighbour_swap(): from_odd = lax.ppermute(odd_msg, axis, odd_pairs(n))  5.65 us
    ppermute x2, starting transfers between devices, window_swap(): got = lax.ppermute(down, 'win', even_pairs(n))  3.13 us
    pallas_call x1, Pallas kernels, per_device(): call(functools.partial(inner_kernel, copies), [vmem()] * (6 + copies), [t...  1.91 us
    ppermute x2, waiting for transfers between devices, neighbour_swap(): from_even = lax.ppermute(even_msg, axis, even_pairs(n))  1.77 us
    pallas_call x1, Pallas kernels, per_device(): call(functools.partial(own_kernel, copies), [vmem()] + [hbm()] * 4, [wind...  1.48 us
    ppermute x2, waiting for transfers between devices, neighbour_swap(): from_odd = lax.ppermute(odd_msg, axis, odd_pairs(n))  1.43 us
    pallas_call x1, Pallas kernels, per_device(): call(functools.partial(load_kernel, swap2, copies), [hbm()] * 4, [(16, co...  1.26 us
  transfers between devices with their start and end apart: 6, of which 3 were waited for; matrix products, arithmetic and copies ran while one was open for 0% of the time, Pallas kernels for 16%

profile of v7, /device:TPU:0, one launch (start us, length us, event | category | flops | bytes accessed | tf_op | source)
XLA Modules:
  0.0 27.3 jit_solution(9543089341444068884)
XLA Ops:
  0.0 1.3 %shard_map.64 = (f32[16,256]{1,0:T(8,128)S(1)}, f32[6,64,256]{2,1,0:T(8,128)S(1)}, f32[64,128]{1,0:T(8,128)S(1)}) custom-call(f32[3,64,256]{2,1,0:T(8,128)} %bitcast.7, f32[3,64,256]{2,1,0:T(8,128)} %bitcast.8, f32[2,64,256]{2,1,0:T(8,128)} %bitcast.10, f32[3,1,3]{2,1,0:T(1,128)} %bitcast.12), custom_call_target="tpu_custom_call" | custom-call | flops 1048576 | bytes 1048576 | tf_op jit(solution)/shard_map/pallas_call | solution.py:718
  1.3 3.0 %collective-permute-start.4 = (f32[6,64,256]{2,1,0:T(8,128)S(1)}, f32[6,64,256]{2,1,0:T(8,128)S(1)}, u32[]{:S(2)}, u32[]{:S(2)}) collective-permute-start(f32[6,64,256]{2,1,0:T(8,128)S(1)} %get-tuple-element.28.bulk.inc), channel_id=1, source_target_pairs={{0,16},{16,0},{1,17},{17,1},{2,18},{18,2},{3,19},{19,3},{4,20},{20... | collective-permute-start | bytes 1179656 | tf_op jit(solution)/shard_map/ppermute | solution.py:40
  4.3 0.1 collective-permute-start
  4.4 1.5 %shard_map.65 = (f32[2,64,256]{2,1,0:T(8,128)S(1)}, f32[3,64,256]{2,1,0:T(8,128)S(1)}, f32[3,64,256]{2,1,0:T(8,128)S(1)}, f32[40,256]{1,0:T(8,128)S(1)}, f32[40,...) custom-call(f32[6,64,256]{2,1,0:T(8,128)S(1)} %get-tuple-element.28.bulk.inc, ...), custom_call_target="tpu_custom_call" | custom-call | flops 536870912 | bytes 1048576 | tf_op jit(solution)/shard_map/pallas_call | solution.py:729
  5.9 8.3 %collective-permute-done.refs_2_ = f32[64,128]{1,0:T(8,128)S(1)} collective-permute-done((f32[64,128]{1,0:T(8,128)S(1)}, f32[64,128]{1,0:T(8,128)S(1)}, u32[]{:S(2)}, u32[]{:S(2)}) %collective-permute-start) | collective-permute-done | bytes 32800 | tf_op jit(solution)/shard_map/ppermute | solution.py:40
  14.2 0.1 collective-permute-start.1
  14.2 1.9 %collective-permute-start.2 = (f32[40,256]{1,0:T(8,128)S(1)}, f32[40,256]{1,0:T(8,128)S(1)}, u32[]{:S(2)}, u32[]{:S(2)}) collective-permute-start(f32[40,256]{1,0:T(8,128)S(1)} %get-tuple-element.33), channel_id=1, source_target_pairs={{0,12},{4,8},{8,4},{12,0},{1,13},{5,9},{9,5},{13,1},{2,14},{6,10},... | collective-permute-start | bytes 122888 | tf_op jit(solution)/shard_map/ppermute | solution.py:33
  16.1 0.2 shard_map.67
  16.3 0.0 collective-permute-done.1.got_even
  16.3 1.4 %collective-permute-done.2.got_odd = f32[40,256]{1,0:T(8,128)S(1)} collective-permute-done((f32[40,256]{1,0:T(8,128)S(1)}, f32[40,256]{1,0:T(8,128)S(1)}, u32[]{:S(2)}, u32[]{:S(2)}) %collective-permute-start.2) | collective-permute-done | bytes 40992 | tf_op jit(solution)/shard_map/ppermute | solution.py:33
  17.8 0.2 shard_map.68
  17.9 3.8 %collective-permute-start.3 = (f32[24,128]{1,0:T(8,128)S(1)}, f32[24,128]{1,0:T(8,128)S(1)}, u32[]{:S(2)}, u32[]{:S(2)}) collective-permute-start(f32[24,128]{1,0:T(8,128)S(1)} %get-tuple-element.38), channel_id=1, source_target_pairs={{0,3},{1,2},{2,1},{3,0},{4,7},{5,6},{6,5},{7,4},{8,11},{9,10},{10,... | collective-permute-start | bytes 36872 | tf_op jit(solution)/shard_map/ppermute | solution.py:33
  21.7 0.0 collective-permute-start.5
  21.7 0.0 collective-permute-done.4.refs_0_
  21.7 1.9 %shard_map.69 = (f32[3,64,256]{2,1,0:T(8,128)S(1)}, f32[5,24,128]{2,1,0:T(8,128)S(1)}, f32[5,24,128]{2,1,0:T(8,128)S(1)}, f32[24,128]{1,0:T(8,128)S(1)}, f32[24,128]{1,0:T(8,128)S(1)}, /*index=5*/f32[16,128]{1,0:T(8,128)S(1)}) custom-call(f32[6,64,256]{2,1,0:T(8,128)S(1)} %get-tuple-element.28.bulk.inc, f32[3,64,256]{2,1,0:T(8,128)S(1)} %get-tuple-element.39.wgt, ...), custom_call_target="tpu_custom_call" | custom-call | flops 536870912 | bytes 1048576 | tf_op jit(solution)/shard_map/pallas_call | solution.py:754
  23.7 1.8 %collective-permute-done.5.got = f32[24,128]{1,0:T(8,128)S(1)} collective-permute-done((f32[24,128]{1,0:T(8,128)S(1)}, f32[24,128]{1,0:T(8,128)S(1)}, u32[]{:S(2)}, u32[]{:S(2)}) %collective-permute-start.5) | collective-permute-done | bytes 12320 | tf_op jit(solution)/shard_map/ppermute | solution.py:32
  25.4 0.6 %shard_map.70.part = f32[3,64,256]{2,1,0:T(8,128)S(1)} custom-call(f32[24,128]{1,0:T(8,128)S(1)} %collective-permute-done.5.got, f32[5,24,128]{2,1,0:T(8,128)S(1)} %get-tuple-element.48.base, f32[24,128]{1,0:T(8,128)S(1)} %get-tuple-element.49.wgt_line, f32[16,128]{1,0:T(8,128)S(1)} %get-tuple-element.46.factors, f32[3,64,256]{2,1,0:T(8,128)S(1)} %get-tuple-element.50.part), custom_call_target="tpu_custom_call" | custom-call | flops 268435456 | bytes 1048576 | tf_op jit(solution)/shard_map/pallas_call | solution.py:760
  26.0 0.0 collective-permute-done.3.got
  26.0 1.2 %shard_map.71 = f32[3,64,256]{2,1,0:T(8,128)} custom-call(f32[24,128]{1,0:T(8,128)S(1)} %collective-permute-done.3.got, f32[5,24,128]{2,1,0:T(8,128)S(1)} %get-tuple-element.44.base, f32[24,128]{1,0:T(8,128)S(1)} %get-tuple-element.45.wgt_line, f32[16,128]{1,0:T(8,128)S(1)} %get-tuple-element.46.factors, f32[3,64,256]{2,1,0:T(8,128)S(1)} %shard_map.70.part), custom_call_target="tpu_custom_call" | custom-call | flops 33554432 | bytes 1048576 | tf_op jit(solution)/shard_map/pallas_call | solution.py:763
  (1 shorter events, 0.0 us)
Async XLA Ops:
  1.3 20.5 %collective-permute-start.4 = (f32[6,64,256]{2,1,0:T(8,128)S(1)}, f32[6,64,256]{2,1,0:T(8,128)S(1)}, u32[]{:S(2)}, u32[]{:S(2)}) collective-permute-start(f32[6,64,256]{2,1,0:T(8,128)S(1)} %get-tuple-element.28.bulk.inc), channel_id=1, source_target_pairs={{0,16},{16,0},{1,17},{17,1},{2,18},{18,2},{3,19},{19,3},{4,20},{20... | collective-permute-start | bytes 1179656 | tf_op jit(solution)/shard_map/ppermute | solution.py:40
  4.3 9.8 %collective-permute-start = (f32[64,128]{1,0:T(8,128)S(1)}, f32[64,128]{1,0:T(8,128)S(1)}, u32[]{:S(2)}, u32[]{:S(2)}) collective-permute-start(f32[64,128]{1,0:T(8,128)S(1)} %get-tuple-element.31), channel_id=1, source_target_pairs={{0,16},{16,0},{1,17},{17,1},{2,18},{18,2},{3,19},{19,3},{4,20},{20... | collective-permute-start | bytes 98312 | tf_op jit(solution)/shard_map/ppermute | solution.py:40
  14.2 2.2 %collective-permute-start.1 = (f32[40,256]{1,0:T(8,128)S(1)}, f32[40,256]{1,0:T(8,128)S(1)}, u32[]{:S(2)}, u32[]{:S(2)}) collective-permute-start(f32[40,256]{1,0:T(8,128)S(1)} %get-tuple-element.32), channel_id=1, source_target_pairs={{0,4},{4,0},{8,12},{12,8},{1,5},{5,1},{9,13},{13,9},{2,6},{6,2},{1... | collective-permute-start | bytes 122888 | tf_op jit(solution)/shard_map/ppermute | solution.py:32
  14.2 3.5 %collective-permute-start.2 = (f32[40,256]{1,0:T(8,128)S(1)}, f32[40,256]{1,0:T(8,128)S(1)}, u32[]{:S(2)}, u32[]{:S(2)}) collective-permute-start(f32[40,256]{1,0:T(8,128)S(1)} %get-tuple-element.33), channel_id=1, source_target_pairs={{0,12},{4,8},{8,4},{12,0},{1,13},{5,9},{9,5},{13,1},{2,14},{6,10},... | collective-permute-start | bytes 122888 | tf_op jit(solution)/shard_map/ppermute | solution.py:33
  17.9 8.1 %collective-permute-start.3 = (f32[24,128]{1,0:T(8,128)S(1)}, f32[24,128]{1,0:T(8,128)S(1)}, u32[]{:S(2)}, u32[]{:S(2)}) collective-permute-start(f32[24,128]{1,0:T(8,128)S(1)} %get-tuple-element.38), channel_id=1, source_target_pairs={{0,3},{1,2},{2,1},{3,0},{4,7},{5,6},{6,5},{7,4},{8,11},{9,10},{10,... | collective-permute-start | bytes 36872 | tf_op jit(solution)/shard_map/ppermute | solution.py:33
  21.7 3.7 %collective-permute-start.5 = (f32[24,128]{1,0:T(8,128)S(1)}, f32[24,128]{1,0:T(8,128)S(1)}, u32[]{:S(2)}, u32[]{:S(2)}) collective-permute-start(f32[24,128]{1,0:T(8,128)S(1)} %get-tuple-element.47), channel_id=1, source_target_pairs={{0,1},{1,0},{2,3},{3,2},{4,5},{5,4},{6,7},{7,6},{8,9},{9,8},{10,11... | collective-permute-start | bytes 36872 | tf_op jit(solution)/shard_map/ppermute | solution.py:32

commit v8 on v6

--- a/solution.py
+++ b/solution.py
@@ -312,8 +312,7 @@
     return jnp.where(upper, from_high, from_low) > 0
 
 
-def rows_kernel(fields, copies, tail, got_even, got_odd, even_tile, odd_tile, halo_rows, msg_even, msg_odd):
-    lay = Layout(fields, copies)
+def halo_blocks(lay, got_even, got_odd):
     cols = got_even.shape[-1]
     is_even = axis_even("lat")
     inside = lat_inside(cols)
@@ -325,13 +324,18 @@
         high.append(jnp.where(is_even, a, b))
         low.append(jnp.where(is_even, b, a))
     blocks = []
-    for j, (at, d) in enumerate(zip(lay.starts, lay.depths)):
+    for at, d in zip(lay.starts, lay.depths):
         above = turn(high[at // 8], -(at % 8), 0)
         below = turn(low[at // 8], 8 - d - at % 8, 0)
         block = jnp.where(sub < d, above, jnp.where(sub >= 8 - d, below, 0.0))
         block = jnp.where(inside, block, 0.0)
-        halo_rows[j] = block
         blocks.append(block)
+    return blocks
+
+
+def rows_kernel(fields, copies, tail, got_even, got_odd, even_tile, odd_tile, msg_even, msg_odd):
+    lay = Layout(fields, copies)
+    blocks = halo_blocks(lay, got_even, got_odd)
     where = list(zip(blocks, lay.lanes, lay.depths))
     low_tail = pack_lanes([(x[:, :LANES], 0, at, d) for x, at, d in where])
     high_tail = pack_lanes([(x[:, -LANES:], LANES - d, at, d) for x, at, d in where])
@@ -529,7 +533,7 @@
     )
 
 
-def inner_kernel(copies, inc, wgt, wind, hmap, mixrows, halo_rows, *refs):
+def inner_kernel(copies, inc, wgt, wind, hmap, mixrows, lat_even, lat_odd, *refs):
     bulk = refs[:copies]
     part, even_base, odd_base, even_wgt, odd_wgt, factors = refs[copies:]
     fields, rows, cols = wgt.shape
@@ -537,6 +541,7 @@
     tiles = [inc[f] for f in range(fields)] + [wind[0], wind[1]] + [hmap[f] for f in range(fields)]
     for ref in bulk:
         tiles += [ref[j] for j in range(lay.packet)]
+    halo_rows = halo_blocks(lay, lat_even, lat_odd)
     planes = [jnp.concatenate([tile, halo_rows[j]], axis=0) for j, tile in enumerate(tiles)]
     lon_even = axis_even("lon")
 
@@ -709,26 +714,23 @@
     row_even, row_odd = call(
         functools.partial(join_kernel, fields, copies), [vmem()] * (2 + copies), [row_msg, row_msg], 1 << 16
     )(row_first, row_last, *strips)
-    got_even, got_odd = neighbour_swap(row_even, row_odd, "lat")
+    lat_even, lat_odd = neighbour_swap(row_even, row_odd, "lat")
     even_tile, odd_tile = call(
         functools.partial(cols_kernel, fields, copies), [vmem()] * (2 + copies), [col_msg, col_msg], 1 << 28
     )(col_low, col_high, *strips)
 
-    halo_rows, msg_even, msg_odd = call(
-        functools.partial(rows_kernel, fields, copies, rows // 8),
-        [vmem()] * 4,
-        [(lay.count, 8, cols), col_msg, col_msg],
-        1 << 16,
-    )(got_even, got_odd, even_tile, odd_tile)
+    msg_even, msg_odd = call(
+        functools.partial(rows_kernel, fields, copies, rows // 8), [vmem()] * 4, [col_msg, col_msg], 1 << 16
+    )(lat_even, lat_odd, even_tile, odd_tile)
     got_even, got_odd = neighbour_swap(msg_even, msg_odd, "lon")
 
     base_shape = (len(line_planes(lay)),) + col_msg
     part, even_base, odd_base, even_wgt, odd_wgt, factors = call(
         functools.partial(inner_kernel, copies),
-        [vmem()] * (6 + copies),
+        [vmem()] * (7 + copies),
         [tile, base_shape, base_shape, col_msg, col_msg, (8 * -(-3 * (2 * fields - 1) // 8), LANES)],
         1 << 29,
-    )(sent[0], wgt_near, wind_near, hmap, mixrows, halo_rows, *bulk)
+    )(sent[0], wgt_near, wind_near, hmap, mixrows, lat_even, lat_odd, *bulk)
     (part,) = call(
         functools.partial(side_kernel, copies, False), [vmem()] * 5, [tile], 1 << 28
     )(got_even, even_base, even_wgt, factors, part)

time: 27.5 us -> 27.5 us (level)
  no operation moved by 1% of the time
where the time goes in v8:
time: 27.5 us; the launch traced here: 27.3 us
  waiting for transfers between devices  11.5 us (42%)
  starting transfers between devices  8.85 us (32%)
  Pallas kernels  6.87 us (25%)
    ppermute x2, waiting for transfers between devices, window_swap(): got = lax.ppermute(down, 'win', even_pairs(n))  8.26 us
    ppermute x2, starting transfers between devices, neighbour_swap(): from_odd = lax.ppermute(odd_msg, axis, odd_pairs(n))  5.65 us
    ppermute x2, starting transfers between devices, window_swap(): got = lax.ppermute(down, 'win', even_pairs(n))  3.13 us
    pallas_call x1, Pallas kernels, per_device(): call(functools.partial(inner_kernel, copies), [vmem()] * (7 + copies), [t...  1.85 us
    ppermute x2, waiting for transfers between devices, neighbour_swap(): from_even = lax.ppermute(even_msg, axis, even_pairs(n))  1.84 us
    pallas_call x1, Pallas kernels, per_device(): call(functools.partial(own_kernel, copies), [vmem()] + [hbm()] * 4, [wind...  1.47 us
    ppermute x2, waiting for transfers between devices, neighbour_swap(): from_odd = lax.ppermute(odd_msg, axis, odd_pairs(n))  1.43 us
    pallas_call x1, Pallas kernels, per_device(): call(functools.partial(side_kernel, copies, True), [vmem()] * 5, [tile],...  1.26 us
  transfers between devices with their start and end apart: 6, of which 3 were waited for; matrix products, arithmetic and copies ran while one was open for 0% of the time, Pallas kernels for 16%

profile of v8, /device:TPU:0, one launch (start us, length us, event | category | flops | bytes accessed | tf_op | source)
XLA Modules:
  0.0 27.3 jit_solution(16908907839693893597)
XLA Ops:
  0.0 1.3 %shard_map.64 = (f32[16,256]{1,0:T(8,128)S(1)}, f32[6,64,256]{2,1,0:T(8,128)S(1)}, f32[64,128]{1,0:T(8,128)S(1)}) custom-call(f32[3,64,256]{2,1,0:T(8,128)} %bitcast.7, f32[3,64,256]{2,1,0:T(8,128)} %bitcast.8, f32[2,64,256]{2,1,0:T(8,128)} %bitcast.10, f32[3,1,3]{2,1,0:T(1,128)} %bitcast.12), custom_call_target="tpu_custom_call" | custom-call | flops 1048576 | bytes 1048576 | tf_op jit(solution)/shard_map/pallas_call | solution.py:695
  1.3 3.0 %collective-permute-start.4 = (f32[6,64,256]{2,1,0:T(8,128)S(1)}, f32[6,64,256]{2,1,0:T(8,128)S(1)}, u32[]{:S(2)}, u32[]{:S(2)}) collective-permute-start(f32[6,64,256]{2,1,0:T(8,128)S(1)} %get-tuple-element.27.bulk.inc), channel_id=1, source_target_pairs={{0,16},{16,0},{1,17},{17,1},{2,18},{18,2},{3,19},{19,3},{4,20},{20... | collective-permute-start | bytes 1179656 | tf_op jit(solution)/shard_map/ppermute | solution.py:40
  4.3 0.1 collective-permute-start
  4.4 1.5 %shard_map.65 = (f32[2,64,256]{2,1,0:T(8,128)S(1)}, f32[3,64,256]{2,1,0:T(8,128)S(1)}, f32[3,64,256]{2,1,0:T(8,128)S(1)}, f32[40,256]{1,0:T(8,128)S(1)}, f32[40,...) custom-call(f32[6,64,256]{2,1,0:T(8,128)S(1)} %get-tuple-element.27.bulk.inc, ...), custom_call_target="tpu_custom_call" | custom-call | flops 536870912 | bytes 1048576 | tf_op jit(solution)/shard_map/pallas_call | solution.py:706
  5.9 8.3 %collective-permute-done.refs_2_ = f32[64,128]{1,0:T(8,128)S(1)} collective-permute-done((f32[64,128]{1,0:T(8,128)S(1)}, f32[64,128]{1,0:T(8,128)S(1)}, u32[]{:S(2)}, u32[]{:S(2)}) %collective-permute-start) | collective-permute-done | bytes 32800 | tf_op jit(solution)/shard_map/ppermute | solution.py:40
  14.2 0.1 collective-permute-start.1
  14.2 1.9 %collective-permute-start.2 = (f32[40,256]{1,0:T(8,128)S(1)}, f32[40,256]{1,0:T(8,128)S(1)}, u32[]{:S(2)}, u32[]{:S(2)}) collective-permute-start(f32[40,256]{1,0:T(8,128)S(1)} %get-tuple-element.32), channel_id=1, source_target_pairs={{0,12},{4,8},{8,4},{12,0},{1,13},{5,9},{9,5},{13,1},{2,14},{6,10},... | collective-permute-start | bytes 122888 | tf_op jit(solution)/shard_map/ppermute | solution.py:33
  16.1 0.2 shard_map.67
  16.3 0.0 collective-permute-done.1.got_even.lat_even
  16.3 1.4 %collective-permute-done.2.got_odd.lat_odd = f32[40,256]{1,0:T(8,128)S(1)} collective-permute-done((f32[40,256]{1,0:T(8,128)S(1)}, f32[40,256]{1,0:T(8,128)S(1)}, u32[]{:S(2)}, u32[]{:S(2)}) %collective-permute-start.2) | collective-permute-done | bytes 40992 | tf_op jit(solution)/shard_map/ppermute | solution.py:33
  17.8 0.2 shard_map.68
  17.9 3.8 %collective-permute-start.3 = (f32[24,128]{1,0:T(8,128)S(1)}, f32[24,128]{1,0:T(8,128)S(1)}, u32[]{:S(2)}, u32[]{:S(2)}) collective-permute-start(f32[24,128]{1,0:T(8,128)S(1)} %get-tuple-element.37), channel_id=1, source_target_pairs={{0,3},{1,2},{2,1},{3,0},{4,7},{5,6},{6,5},{7,4},{8,11},{9,10},{10,... | collective-permute-start | bytes 36872 | tf_op jit(solution)/shard_map/ppermute | solution.py:33
  21.7 0.0 collective-permute-start.5
  21.7 0.0 collective-permute-done.4.refs_0_
  21.7 1.8 %shard_map.69 = (f32[3,64,256]{2,1,0:T(8,128)S(1)}, f32[5,24,128]{2,1,0:T(8,128)S(1)}, f32[5,24,128]{2,1,0:T(8,128)S(1)}, f32[24,128]{1,0:T(8,128)S(1)}, f32[24,128]{1,0:T(8,128)S(1)}, /*index=5*/f32[16,128]{1,0:T(8,128)S(1)}) custom-call(f32[6,64,256]{2,1,0:T(8,128)S(1)} %get-tuple-element.27.bulk.inc, f32[3,64,256]{2,1,0:T(8,128)S(1)} %get-tuple-element.38.wgt, ...), custom_call_target="tpu_custom_call" | custom-call | flops 536870912 | bytes 1048576 | tf_op jit(solution)/shard_map/pallas_call | solution.py:728
  23.6 1.8 %collective-permute-done.5.got = f32[24,128]{1,0:T(8,128)S(1)} collective-permute-done((f32[24,128]{1,0:T(8,128)S(1)}, f32[24,128]{1,0:T(8,128)S(1)}, u32[]{:S(2)}, u32[]{:S(2)}) %collective-permute-start.5) | collective-permute-done | bytes 12320 | tf_op jit(solution)/shard_map/ppermute | solution.py:32
  25.4 0.6 %shard_map.70.part = f32[3,64,256]{2,1,0:T(8,128)S(1)} custom-call(f32[24,128]{1,0:T(8,128)S(1)} %collective-permute-done.5.got, f32[5,24,128]{2,1,0:T(8,128)S(1)} %get-tuple-element.46.base, f32[24,128]{1,0:T(8,128)S(1)} %get-tuple-element.47.wgt_line, f32[16,128]{1,0:T(8,128)S(1)} %get-tuple-element.44.factors, f32[3,64,256]{2,1,0:T(8,128)S(1)} %get-tuple-element.48.part), custom_call_target="tpu_custom_call" | custom-call | flops 268435456 | bytes 1048576 | tf_op jit(solution)/shard_map/pallas_call | solution.py:734
  26.0 0.0 collective-permute-done.3.got
  26.0 1.3 %shard_map.71 = f32[3,64,256]{2,1,0:T(8,128)} custom-call(f32[24,128]{1,0:T(8,128)S(1)} %collective-permute-done.3.got, f32[5,24,128]{2,1,0:T(8,128)S(1)} %get-tuple-element.42.base, f32[24,128]{1,0:T(8,128)S(1)} %get-tuple-element.43.wgt_line, f32[16,128]{1,0:T(8,128)S(1)} %get-tuple-element.44.factors, f32[3,64,256]{2,1,0:T(8,128)S(1)} %shard_map.70.part), custom_call_target="tpu_custom_call" | custom-call | flops 33554432 | bytes 1048576 | tf_op jit(solution)/shard_map/pallas_call | solution.py:737
  (1 shorter events, 0.0 us)
Async XLA Ops:
  1.3 20.5 %collective-permute-start.4 = (f32[6,64,256]{2,1,0:T(8,128)S(1)}, f32[6,64,256]{2,1,0:T(8,128)S(1)}, u32[]{:S(2)}, u32[]{:S(2)}) collective-permute-start(f32[6,64,256]{2,1,0:T(8,128)S(1)} %get-tuple-element.27.bulk.inc), channel_id=1, source_target_pairs={{0,16},{16,0},{1,17},{17,1},{2,18},{18,2},{3,19},{19,3},{4,20},{20... | collective-permute-start | bytes 1179656 | tf_op jit(solution)/shard_map/ppermute | solution.py:40
  4.3 9.8 %collective-permute-start = (f32[64,128]{1,0:T(8,128)S(1)}, f32[64,128]{1,0:T(8,128)S(1)}, u32[]{:S(2)}, u32[]{:S(2)}) collective-permute-start(f32[64,128]{1,0:T(8,128)S(1)} %get-tuple-element.30), channel_id=1, source_target_pairs={{0,16},{16,0},{1,17},{17,1},{2,18},{18,2},{3,19},{19,3},{4,20},{20... | collective-permute-start | bytes 98312 | tf_op jit(solution)/shard_map/ppermute | solution.py:40
  14.2 2.2 %collective-permute-start.1 = (f32[40,256]{1,0:T(8,128)S(1)}, f32[40,256]{1,0:T(8,128)S(1)}, u32[]{:S(2)}, u32[]{:S(2)}) collective-permute-start(f32[40,256]{1,0:T(8,128)S(1)} %get-tuple-element.31), channel_id=1, source_target_pairs={{0,4},{4,0},{8,12},{12,8},{1,5},{5,1},{9,13},{13,9},{2,6},{6,2},{1... | collective-permute-start | bytes 122888 | tf_op jit(solution)/shard_map/ppermute | solution.py:32
  14.2 3.5 %collective-permute-start.2 = (f32[40,256]{1,0:T(8,128)S(1)}, f32[40,256]{1,0:T(8,128)S(1)}, u32[]{:S(2)}, u32[]{:S(2)}) collective-permute-start(f32[40,256]{1,0:T(8,128)S(1)} %get-tuple-element.32), channel_id=1, source_target_pairs={{0,12},{4,8},{8,4},{12,0},{1,13},{5,9},{9,5},{13,1},{2,14},{6,10},... | collective-permute-start | bytes 122888 | tf_op jit(solution)/shard_map/ppermute | solution.py:33
  17.9 8.1 %collective-permute-start.3 = (f32[24,128]{1,0:T(8,128)S(1)}, f32[24,128]{1,0:T(8,128)S(1)}, u32[]{:S(2)}, u32[]{:S(2)}) collective-permute-start(f32[24,128]{1,0:T(8,128)S(1)} %get-tuple-element.37), channel_id=1, source_target_pairs={{0,3},{1,2},{2,1},{3,0},{4,7},{5,6},{6,5},{7,4},{8,11},{9,10},{10,... | collective-permute-start | bytes 36872 | tf_op jit(solution)/shard_map/ppermute | solution.py:33
  21.7 3.7 %collective-permute-start.5 = (f32[24,128]{1,0:T(8,128)S(1)}, f32[24,128]{1,0:T(8,128)S(1)}, u32[]{:S(2)}, u32[]{:S(2)}) collective-permute-start(f32[24,128]{1,0:T(8,128)S(1)} %get-tuple-element.45), channel_id=1, source_target_pairs={{0,1},{1,0},{2,3},{3,2},{4,5},{5,4},{6,7},{7,6},{8,9},{9,8},{10,11... | collective-permute-start | bytes 36872 | tf_op jit(solution)/shard_map/ppermute | solution.py:32
